TPU v7x, 256 devices: a whole 4x4x8 slice. The times are simulated.
256 devices in a mesh: dp: 8 (over z), seq: 32 (over x, y, core).
Axes of the slice: x: 4, y: 4, z: 8, core: 2. Of those that a mesh axis runs over, the one named last changes fastest.
Arguments:
- values_in: bfloat16 [8, 4096, 2048], P('dp', 'seq'), may hold values from -6 to 6
- input_proj: bfloat16 [8, 4096, 128], P('dp', 'seq'), may hold values from -0.5 to 0.5
- output_proj: bfloat16 [8, 4096, 128], P('dp', 'seq'), may hold values from -0.09375 to 0.09375
- log_decay: float32 [8, 32, 4096], P('dp', None, 'seq'), may hold values from -1 to 0, as said below
- doc_lengths: int32 [8, 8], P('dp'), may hold values from 1 to 2048, 4096 in all within a row
- skip_gain: float32 [32], replicated, may hold values from 0.5 to 1.5
- out_cotangent: bfloat16 [8, 4096, 2048], P('dp', 'seq'), may hold values from -6 to 6
Outputs:
- mixed_out: bfloat16 [8, 4096, 2048], P('dp', 'seq')
- values_grad: bfloat16 [8, 4096, 2048], P('dp', 'seq')
- input_grad: float32 [8, 4096, 128], P('dp', 'seq')
- output_grad: float32 [8, 4096, 128], P('dp', 'seq')
- decay_grad: float32 [8, 32, 4096], P('dp', None, 'seq')
- skip_grad: float32 [32], replicated
Inputs may be any that keep to these rules, and one draw needn't show every extreme that they name: `doc_lengths`: one row lists the documents of one sequence in order and sums to 4096. `log_decay`: negative log decay of each head at each token.
All inputs are finite; a program needn't handle non-finite values.
Results may differ from a plain program's by a relative error of at most 0.0056.
Values sent between devices are 32-bit elements; how exact they have to be, the bound alone decides.
No kernel may reach another device: no remote copies, remote signals or barrier semaphores. Data moves between devices by JAX's collectives and lax.ppermute only.
A program may use at most 128 MiB of HBM per device.

v0:
```python
import functools

import jax
import jax.numpy as jnp
from jax import lax
from jax.sharding import Mesh
from jax.sharding import PartitionSpec as P

SEQ = ("seq_0", "seq_1", "seq_2")
DP_SEQ = ("dp", "seq_0", "seq_1", "seq_2")


def in_one_piece(arrays, axis, split_dim, concat_dim, along):
    ends, at = ([], 0)
    for a in arrays[:-1]:
        at += a.shape[along]
        ends.append(at)
    both = jnp.concatenate(arrays, axis=along)
    return tuple(
        jnp.split(
            lax.all_to_all(both, axis, split_axis=split_dim, concat_axis=concat_dim, tiled=True),
            ends,
            axis=along,
        )
    )


def one_axis_at_a_time(x, axes):
    return functools.reduce(lax.psum, axes, x)


def product(form, left_side, right_side):
    return jnp.einsum(form, left_side, right_side, preferred_element_type=jnp.float32)


def block_stats(log_rows, resets):
    log_cum = jnp.cumsum(log_rows, axis=1)
    seg_count = jnp.cumsum(resets)
    log_end = log_cum[:, -1:]
    count_end = seg_count[-1]
    carry_gain = jnp.exp(log_end[:, 0]) * (count_end == 0).astype(jnp.float32)
    weight_end = jnp.exp(log_end - log_cum) * (seg_count == count_end).astype(jnp.float32)[None, :]
    weight_start = jnp.exp(log_cum) * (seg_count == 0).astype(jnp.float32)[None, :]
    return (log_cum, seg_count, carry_gain, weight_end, weight_start)


def head_scale(values, factors):
    row_count, inner_width = values.shape
    head_count = factors.shape[0]
    shaped = values.reshape(row_count, head_count, inner_width // head_count)
    return (shaped * factors.T[:, :, None]).reshape(row_count, inner_width)


def head_dot(left_side, right_side, head_count):
    row_count = left_side.shape[0]
    joined = left_side.astype(jnp.float32) * right_side.astype(jnp.float32)
    return jnp.sum(joined.reshape(row_count, head_count, -1), axis=2).T


def finish_block(
    values,
    input_rows,
    output_rows,
    grads_in,
    resets,
    skip_gain,
    stats,
    weighted_values,
    weighted_grads,
    state_in,
    adjoint_in,
):
    log_cum, seg_count, carry_gain, weight_end, weight_start = stats
    head_count = log_cum.shape[0]
    row_count, inner_width = values.shape
    head_dim = inner_width // head_count
    state_half = state_in.astype(jnp.bfloat16)
    adjoint_half = adjoint_in.astype(jnp.bfloat16)
    state_read = product("ln,in->li", output_rows, state_half)
    adjoint_read = product("ln,in->li", input_rows, adjoint_half)
    scores = product("tn,sn->ts", output_rows, input_rows)
    position = jnp.arange(row_count, dtype=jnp.int32)
    causal = (position[None, :] <= position[:, None]) & (seg_count[None, :] == seg_count[:, None])
    group_size = min(4, head_count)
    outs_within = []
    outs_back = []
    grad_parts = []
    grad_scores = jnp.zeros((row_count, row_count), jnp.float32)
    for block_index in range(head_count // group_size):
        first_head = block_index * group_size
        low_col = first_head * head_dim
        high_col = (first_head + group_size) * head_dim
        value_group = values[:, low_col:high_col].reshape(row_count, group_size, head_dim)
        grad_group = grads_in[:, low_col:high_col].reshape(row_count, group_size, head_dim)
        log_group = log_cum[first_head : first_head + group_size]
        log_gap = log_group[:, :, None] - log_group[:, None, :]
        decay_mat = jnp.exp(jnp.where(causal[None], log_gap, -jnp.inf))
        weighted = scores[None] * decay_mat
        mix_half = weighted.astype(jnp.bfloat16)
        outs_within.append(product("gts,sgp->tgp", mix_half, value_group).reshape(row_count, -1))
        outs_back.append(product("gts,tgp->sgp", mix_half, grad_group).reshape(row_count, -1))
        grad_mix = product("tgp,sgp->gts", grad_group, value_group)
        sensitivity = grad_mix * weighted
        grad_parts.append(jnp.sum(sensitivity, axis=2) - jnp.sum(sensitivity, axis=1))
        grad_scores = grad_scores + jnp.sum(grad_mix * decay_mat, axis=0)
    within_out = jnp.concatenate(outs_within, axis=1)
    back_part = jnp.concatenate(outs_back, axis=1)
    grad_cum = jnp.concatenate(grad_parts, axis=0)
    skip_rows = jnp.repeat(skip_gain, head_dim)[None, :]
    mixed = (within_out + head_scale(state_read, weight_start) + skip_rows * values).astype(
        jnp.bfloat16
    )
    values_grad = (back_part + head_scale(adjoint_read, weight_end) + skip_rows * grads_in).astype(
        jnp.bfloat16
    )
    grad_start = head_dot(grads_in, state_read, head_count)
    grad_end = head_dot(values, adjoint_read, head_count)
    grad_gain = jnp.sum((state_in * adjoint_in).reshape(head_count, -1), axis=1)
    end_total = jnp.sum(weight_end * grad_end, axis=1) + carry_gain * grad_gain
    grad_cum = grad_cum + weight_start * grad_start - weight_end * grad_end
    grad_cum = grad_cum.at[:, -1].add(end_total)
    decay_raw = (
        jnp.flip(jnp.cumsum(jnp.flip(grad_cum, 1), axis=1), 1)
        * (1 - resets).astype(jnp.float32)[None, :]
    )
    grad_half = grad_scores.astype(jnp.bfloat16)
    input_raw = product("ts,tn->sn", grad_half, output_rows) + product(
        "li,in->ln", weighted_values, adjoint_half
    )
    output_raw = product("ts,sn->tn", grad_half, input_rows) + product(
        "li,in->ln", weighted_grads, state_half
    )
    skip_part = jnp.sum(head_dot(grads_in, values, head_count), axis=1)
    return (mixed, values_grad, input_raw, output_raw, decay_raw, skip_part)


def body(values_in, input_proj, output_proj, log_decay, doc_lengths, skip_gain, out_cotangent):
    values = values_in[0]
    input_rows = input_proj[0]
    output_rows = output_proj[0]
    grads_in = out_cotangent[0]
    log_rows = log_decay[0]
    row_count, inner_width = values.shape
    head_count = log_rows.shape[0]
    head_dim = inner_width // head_count
    state_width = input_rows.shape[1]
    shards = lax.axis_size(SEQ)
    position = lax.axis_index(SEQ) * row_count + jnp.arange(row_count, dtype=jnp.int32)
    lengths = doc_lengths[0]
    starts = jnp.cumsum(lengths) - lengths
    resets = jnp.any(position[:, None] == starts[None, :], axis=1).astype(jnp.int32)
    stats = block_stats(log_rows, resets)
    log_cum, seg_count, carry_gain, weight_end, weight_start = stats
    weighted_values = head_scale(values, weight_end).astype(jnp.bfloat16)
    weighted_grads = head_scale(grads_in, weight_start).astype(jnp.bfloat16)
    local_state = product("li,ln->in", weighted_values, input_rows)
    local_adjoint = product("li,ln->in", weighted_grads, output_rows)
    gain_rows = jnp.broadcast_to(carry_gain[None, :, None, None], (1, head_count, head_dim, 1))
    shaped = (
        local_state.reshape(1, head_count, head_dim, state_width),
        local_adjoint.reshape(1, head_count, head_dim, state_width),
        gain_rows,
    )
    states_all = lax.all_to_all(shaped[0], SEQ, split_axis=1, concat_axis=0, tiled=True)
    adjoints_all = lax.all_to_all(shaped[1], SEQ, split_axis=1, concat_axis=0, tiled=True)
    gains_all = lax.all_to_all(shaped[2], SEQ, split_axis=1, concat_axis=0, tiled=True)
    anchor = jnp.zeros(states_all.shape[1:], jnp.float32)

    def advance(running, element):
        factor, addend = element
        return (factor * running + addend, running)

    unused_a, state_prefix = lax.scan(advance, anchor, (gains_all, states_all))
    unused_b, adjoint_prefix = lax.scan(advance, anchor, (gains_all, adjoints_all), reverse=True)
    state_back, adjoint_back = in_one_piece((state_prefix, adjoint_prefix), SEQ, 0, 1, 2)
    state_in = state_back.reshape(inner_width, state_width)
    adjoint_in = adjoint_back.reshape(inner_width, state_width)
    results = finish_block(
        values,
        input_rows,
        output_rows,
        grads_in,
        resets,
        skip_gain,
        stats,
        weighted_values,
        weighted_grads,
        state_in,
        adjoint_in,
    )
    mixed, values_grad, input_raw, output_raw, decay_raw, skip_part = results
    token_count = shards * row_count
    seq_count = lax.axis_size("dp")
    input_grad = input_raw * (1.0 / jnp.sqrt(jnp.float32(head_count * head_dim)))
    output_grad = output_raw * jnp.sqrt(
        jnp.float32(state_width) / jnp.float32(head_count * head_dim * token_count)
    )
    decay_grad = decay_raw * (1.0 / jnp.sqrt(jnp.float32(head_dim * token_count)))
    skip_total = one_axis_at_a_time(skip_part, DP_SEQ)
    skip_grad = skip_total / jnp.sqrt(jnp.float32(seq_count * token_count * head_dim))
    return (
        mixed[None],
        values_grad[None],
        input_grad[None],
        output_grad[None],
        decay_grad[None],
        skip_grad,
    )


def solution(mesh):
    finer = Mesh(mesh.devices.reshape(mesh.shape["dp"], 4, 4, 2), ("dp", "seq_0", "seq_1", "seq_2"))
    placed = (
        P("dp", SEQ, None),
        P("dp", SEQ, None),
        P("dp", SEQ, None),
        P("dp", None, SEQ),
        P("dp", None),
        P(),
        P("dp", SEQ, None),
    )
    return jax.shard_map(
        body,
        mesh=finer,
        in_specs=placed,
        out_specs=(
            P("dp", SEQ, None),
            P("dp", SEQ, None),
            P("dp", SEQ, None),
            P("dp", SEQ, None),
            P("dp", None, SEQ),
            P(),
        ),
        check_vma=False,
    )
```

profile of v0, /device:TPU:1, one launch (start us, length us, event | category | flops | bytes accessed | tf_op | source)
XLA Modules:
  0.0 180.9 jit_solution(5471237887130458574)
XLA Ops:
  2.3 1.0 reduce_window_sum.31
  5.5 8.6 %all-to-all-start = ((f32[1,32,64,1]{2,3,0,1:T(1,128)}), f32[1,32,64,1]{2,3,0,1:T(1,128)S(1)}, u32[]{:S(2)}, u32[]{:S(2)}) async-start(f32[1,32,64,1]{2,3,0,1:T(1,128)} %broadcast_in_dim.133), calls=%async_computation | async-start | bytes 32768 | tf_op jit(solution)/shard_map/all_to_all | solution.py:166
  15.6 1.3 copy.85
  17.0 1.3 copy.92
  19.5 1.0 fusion.78
  20.8 0.9 fusion.211
  21.7 0.9 fusion.74
  22.9 0.9 fusion.210
  24.4 0.9 fusion.209
  25.9 0.9 fusion.208
  27.2 1.3 convolution_bitcast_fusion.2
  28.7 1.3 convolution_bitcast_fusion.3
  31.7 1.8 fusion.82
  33.7 0.9 copy-done.9
  34.6 7.4 %all-to-all-start.2 = ((f32[1,32,64,128]{3,2,0,1:T(8,128)}), f32[1,32,64,128]{3,2,0,1:T(8,128)S(1)}, u32[]{:S(2)}, u32[]{:S(2)}) async-start(f32[1,32,64,128]{3,2,0,1:T(8,128)} %convolution_bitcast_fusion.2), calls=%async_computation.2 | async-start | bytes 2097152 | tf_op jit(solution)/shard_map/all_to_all | solution.py:165
  42.0 0.9 constant_dynamic-update-slice_fusion.10
  42.9 1.0 copy-done.7
  43.9 1.1 fusion.207
  45.0 1.1 fusion.206
  46.1 1.1 fusion.205
  47.2 3.5 %fusion.52 = (f32[4,128]{1,0:T(4,128)}, f32[4,128]{1,0:T(4,128)}, f32[128,128]{1,0:T(8,128)}, f32[128,128]{1,0:T(8,128)}, f32[4,128]{1,0:T(4,128)}, /*index=5*/f...) fusion(f32[4,128]{1,0:T(4,128)} %get-tuple-element.369, ...), kind=kOutput, calls=%fused_computation.97 | convolution fusion | flops 12443648 | bytes 2621440 | tf_op jit(solution)/shard_map/tgp,sgp->gts/dot_general | solution.py:33
  50.7 8.2 %all-to-all-done.2 = f32[1,32,64,128]{3,2,0,1:T(8,128)S(1)} async-done(((f32[1,32,64,128]{3,2,0,1:T(8,128)}), f32[1,32,64,128]{3,2,0,1:T(8,128)S(1)}, u32[]{:S(2)}, u32[]{:S(2)}) %all-to-all-start.2) | async-done | bytes 1048608 | tf_op jit(solution)/shard_map/all_to_all | solution.py:165
  58.9 4.5 %all-to-all-start.1 = ((f32[1,32,64,128]{3,2,0,1:T(8,128)}), f32[1,32,64,128]{3,2,0,1:T(8,128)}, u32[]{:S(2)}, u32[]{:S(2)}) async-start(f32[1,32,64,128]{3,2,0,1:T(8,128)} %convolution_bitcast_fusion.3), calls=%async_computation.1 | async-start | bytes 2097152 | tf_op jit(solution)/shard_map/all_to_all | solution.py:164
  63.5 3.1 %while.32 = (s32[]{:T(128)}, f32[1,64,128]{2,1,0:T(8,128)S(1)}, f32[32,1,64,128]{3,2,1,0:T(8,128)S(1)}, f32[32,1,64,1]{2,3,1,0:T(1,128)S(1)}, f32[32,1,64,128]{3...) while((s32[]{:T(128)}, f32[1,64,128]{2,1,0:T(8,128)S(1)}, ...), condition=%wide.region_7.8_spmd.clone, body=%wide.region_6.7_spmd.clone.sunk | while | flops 32772 | bytes 164736 | solution.py:174
  66.6 13.7 %all-to-all-done.1 = f32[1,32,64,128]{3,2,0,1:T(8,128)} async-done(((f32[1,32,64,128]{3,2,0,1:T(8,128)}), f32[1,32,64,128]{3,2,0,1:T(8,128)}, u32[]{:S(2)}, u32[]{:S(2)}) %all-to-all-start.1) | async-done | bytes 1048608 | tf_op jit(solution)/shard_map/all_to_all | solution.py:164
  80.4 27.6 %while.31 = (s32[]{:T(128)}, f32[1,64,128]{2,1,0:T(8,128)S(1)}, f32[32,1,64,128]{3,2,1,0:T(8,128)S(1)}, f32[32,1,64,1]{2,3,1,0:T(1,128)S(1)}, f32[32,1,64,128]{3,2,1,0:T(8,128)}, /*index=5*/s32[]{:T(128)}, s32[]{:T(128)}) while((s32[]{:T(128)}, f32[1,64,128]{2,1,0:T(8,128)S(1)}, f32[32,1,64,128]{3,2,1,0:T(8,128)S(1)}, ...), condition=%wide.region_5.6_spmd.clone, body=%wide.region_4.5_spmd.clone.sunk | while | flops 32771 | bytes 164716 | solution.py:173
  80.5 0.8 bitcast_add_fusion.4
  81.4 0.8 bitcast_add_fusion.4
  83.1 0.8 bitcast_add_fusion.4
  84.8 0.8 bitcast_add_fusion.4
  85.7 0.8 bitcast_add_fusion.4
  86.5 0.8 bitcast_add_fusion.4
  108.1 1.5 pad_maximum_fusion
  109.6 4.0 %all-to-all-start.3 = ((f32[32,1,128,128]{3,2,1,0:T(8,128)}), f32[32,1,128,128]{3,2,1,0:T(8,128)S(1)}, u32[]{:S(2)}, u32[]{:S(2)}) async-start(f32[32,1,128,128]{3,2,1,0:T(8,128)} %pad_maximum_fusion), calls=%async_computation.3 | async-start | bytes 4194304 | tf_op jit(solution)/shard_map/all_to_all | solution.py:21
  120.3 17.4 %psum.28 = f32[32]{0:T(128)S(1)} all-reduce(f32[32]{0:T(128)S(1)} %reduce_sum.308), channel_id=1, replica_groups=mesh['dp'=8,'seq_0'=4,'seq_1'=4,'seq_2'=2] {'dp'}, use_global_device_ids=true, to_apply=%region_39.40 | all-reduce | flops 32 | bytes 256 | tf_op jit(solution)/shard_map/psum | solution.py:29
  137.7 8.6 %psum.29 = f32[32]{0:T(128)S(1)} all-reduce(f32[32]{0:T(128)S(1)} %psum.28), channel_id=1, replica_groups=mesh['dp'=8,'seq_0'=4,'seq_1'=4,'seq_2'=2] {'seq_0'}, use_global_device_ids=true, to_apply=%region_40.41 | all-reduce | flops 32 | bytes 256 | tf_op jit(solution)/shard_map/psum | solution.py:29
  146.3 8.4 %psum.30 = f32[32]{0:T(128)S(1)} all-reduce(f32[32]{0:T(128)S(1)} %psum.29), channel_id=1, replica_groups=mesh['dp'=8,'seq_0'=4,'seq_1'=4,'seq_2'=2] {'seq_1'}, use_global_device_ids=true, to_apply=%region_41.42 | all-reduce | flops 32 | bytes 256 | tf_op jit(solution)/shard_map/psum | solution.py:29
  154.7 9.1 %psum.31 = f32[32]{0:T(128)S(1)} all-reduce(f32[32]{0:T(128)S(1)} %psum.30), channel_id=1, replica_groups=mesh['dp'=8,'seq_0'=4,'seq_1'=4,'seq_2'=2] {'seq_2'}, use_global_device_ids=true, to_apply=%region_42.43 | all-reduce | flops 32 | bytes 256 | tf_op jit(solution)/shard_map/psum | solution.py:29
  163.9 1.1 fusion.84
  165.0 1.6 constant_dynamic-update-slice_fusion
  166.6 1.2 fusion.184
  168.3 1.1 add_convert_fusion
  170.4 0.9 multiply_convert_fusion
  171.3 1.0 multiply_convert_fusion.1
  175.5 1.0 copy.105
  176.5 1.0 copy.104
  178.4 1.0 fusion.5
  179.3 1.0 fusion.3
  (344 shorter events, 47.7 us)
Async XLA Ops:
  0.6 18.8 %copy-start = (bf16[1,128,128]{2,1,0:T(8,128)(2,1)S(1)}, bf16[1,128,128]{2,1,0:T(8,128)(2,1)}, u32[]{:S(2)}) copy-start(bf16[1,128,128]{2,1,0:T(8,128)(2,1)} %param.14) | copy-start | bytes 98308
  2.2 1.1 copy-start.35
  5.5 29.1 %all-to-all-start = ((f32[1,32,64,1]{2,3,0,1:T(1,128)}), f32[1,32,64,1]{2,3,0,1:T(1,128)S(1)}, u32[]{:S(2)}, u32[]{:S(2)}) async-start(f32[1,32,64,1]{2,3,0,1:T(1,128)} %broadcast_in_dim.133), calls=%async_computation | async-start | bytes 32768 | tf_op jit(solution)/shard_map/all_to_all | solution.py:166
  14.7 5.8 %copy-start.26 = (f32[4,128]{1,0:T(4,128)}, f32[4,128]{1,0:T(4,128)S(1)}, u32[]{:S(2)}) copy-start(f32[4,128]{1,0:T(4,128)S(1)} %get-tuple-element.370) | copy-start | bytes 6148
  14.7 7.9 %copy-start.27 = (f32[4,128]{1,0:T(4,128)}, f32[4,128]{1,0:T(4,128)S(1)}, u32[]{:S(2)}) copy-start(f32[4,128]{1,0:T(4,128)S(1)} %get-tuple-element.371) | copy-start | bytes 6148
  14.7 9.4 %copy-start.28 = (f32[4,128]{1,0:T(4,128)}, f32[4,128]{1,0:T(4,128)S(1)}, u32[]{:S(2)}) copy-start(f32[4,128]{1,0:T(4,128)S(1)} %get-tuple-element.372) | copy-start | bytes 6148
  14.7 10.9 %copy-start.29 = (f32[4,128]{1,0:T(4,128)}, f32[4,128]{1,0:T(4,128)S(1)}, u32[]{:S(2)}) copy-start(f32[4,128]{1,0:T(4,128)S(1)} %get-tuple-element.373) | copy-start | bytes 6148
  14.7 15.5 %copy-start.30 = (f32[4,128]{1,0:T(4,128)}, f32[4,128]{1,0:T(4,128)S(1)}, u32[]{:S(2)}) copy-start(f32[4,128]{1,0:T(4,128)S(1)} %get-tuple-element.374) | copy-start | bytes 6148
  14.7 16.0 %copy-start.31 = (f32[4,128]{1,0:T(4,128)}, f32[4,128]{1,0:T(4,128)S(1)}, u32[]{:S(2)}) copy-start(f32[4,128]{1,0:T(4,128)S(1)} %get-tuple-element.375) | copy-start | bytes 6148
  14.8 16.6 %copy-start.32 = (f32[4,128]{1,0:T(4,128)}, f32[4,128]{1,0:T(4,128)S(1)}, u32[]{:S(2)}) copy-start(f32[4,128]{1,0:T(4,128)S(1)} %get-tuple-element.376) | copy-start | bytes 6148
  14.8 12.1 %copy-start.21 = (f32[32]{0:T(128)}, f32[32]{0:T(128)S(1)}, u32[]{:S(2)}) copy-start(f32[32]{0:T(128)S(1)} %slice_bitcast_fusion) | copy-start | bytes 388
  17.0 2.4 %copy-start.11 = (bf16[1,128,128]{2,1,0:T(8,128)(2,1)S(1)}, bf16[1,128,128]{2,1,0:T(8,128)(2,1)}, u32[]{:S(2)}) copy-start(bf16[1,128,128]{2,1,0:T(8,128)(2,1)} %param.15) | copy-start | bytes 98308
  18.7 11.2 %copy-start.13 = (bf16[128,256]{0,1:T(8,128)(2,1)}, bf16[128,256]{0,1:T(8,128)(2,1)S(1)}, u32[]{:S(2)}) copy-start(bf16[128,256]{0,1:T(8,128)(2,1)S(1)} %get-tuple-element.354) | copy-start | bytes 196612
  18.7 13.0 %copy-start.19 = (bf16[128,256]{0,1:T(8,128)(2,1)}, bf16[128,256]{0,1:T(8,128)(2,1)S(1)}, u32[]{:S(2)}) copy-start(bf16[128,256]{0,1:T(8,128)(2,1)S(1)} %get-tuple-element.349) | copy-start | bytes 196612
  19.4 10.8 %copy-start.16 = (bf16[128,256]{0,1:T(8,128)(2,1)}, bf16[128,256]{0,1:T(8,128)(2,1)S(1)}, u32[]{:S(2)}) copy-start(bf16[128,256]{0,1:T(8,128)(2,1)S(1)} %get-tuple-element.362) | copy-start | bytes 196612
  19.4 11.4 %copy-start.15 = (bf16[128,256]{0,1:T(8,128)(2,1)}, bf16[128,256]{0,1:T(8,128)(2,1)S(1)}, u32[]{:S(2)}) copy-start(bf16[128,256]{0,1:T(8,128)(2,1)S(1)} %get-tuple-element.363) | copy-start | bytes 196612
  19.4 12.0 %copy-start.14 = (bf16[128,256]{0,1:T(8,128)(2,1)}, bf16[128,256]{0,1:T(8,128)(2,1)S(1)}, u32[]{:S(2)}) copy-start(bf16[128,256]{0,1:T(8,128)(2,1)S(1)} %get-tuple-element.364) | copy-start | bytes 196612
  19.5 11.8 %copy-start.20 = (f32[128,128]{1,0:T(8,128)}, f32[128,128]{1,0:T(8,128)S(1)}, u32[]{:S(2)}) copy-start(f32[128,128]{1,0:T(8,128)S(1)} %fusion.177) | copy-start | bytes 196612
  28.6 3.1 %copy-start.23 = (f32[4,128]{1,0:T(4,128)S(1)}, f32[4,128]{1,0:T(4,128)}, u32[]{:S(2)}) copy-start(f32[4,128]{1,0:T(4,128)} %get-tuple-element.369) | copy-start | bytes 6148
  33.6 1.0 copy-start.9
  34.6 24.3 %all-to-all-start.2 = ((f32[1,32,64,128]{3,2,0,1:T(8,128)}), f32[1,32,64,128]{3,2,0,1:T(8,128)S(1)}, u32[]{:S(2)}, u32[]{:S(2)}) async-start(f32[1,32,64,128]{3,2,0,1:T(8,128)} %convolution_bitcast_fusion.2), calls=%async_computation.2 | async-start | bytes 2097152 | tf_op jit(solution)/shard_map/all_to_all | solution.py:165
  42.9 1.0 copy-start.7
  58.9 21.4 %all-to-all-start.1 = ((f32[1,32,64,128]{3,2,0,1:T(8,128)}), f32[1,32,64,128]{3,2,0,1:T(8,128)}, u32[]{:S(2)}, u32[]{:S(2)}) async-start(f32[1,32,64,128]{3,2,0,1:T(8,128)} %convolution_bitcast_fusion.3), calls=%async_computation.1 | async-start | bytes 2097152 | tf_op jit(solution)/shard_map/all_to_all | solution.py:164
  109.6 4.1 %copy-start.17 = (f32[4,128,64]{1,2,0:T(8,128)S(1)}, f32[4,128,64]{1,2,0:T(8,128)}, u32[]{:S(2)}) copy-start(f32[4,128,64]{1,2,0:T(8,128)} %fusion.78) | copy-start | bytes 393220
  109.6 4.7 %copy-start.34 = (f32[32]{0:T(128)S(1)}, f32[32]{0:T(128)}, u32[]{:S(2)}) copy-start(f32[32]{0:T(128)} %param.18) | copy-start | bytes 388
  109.6 9.8 %copy-start.25 = (f32[4,128]{1,0:T(4,128)S(1)}, f32[4,128]{1,0:T(4,128)}, u32[]{:S(2)}) copy-start(f32[4,128]{1,0:T(4,128)} %get-tuple-element.325) | copy-start | bytes 6148
  109.6 54.3 %copy-start.18 = (bf16[128,256]{0,1:T(8,128)(2,1)S(1)}, bf16[128,256]{0,1:T(8,128)(2,1)}, u32[]{:S(2)}) copy-start(bf16[128,256]{0,1:T(8,128)(2,1)} %get-tuple-element.357) | copy-start | bytes 196612
  109.6 54.3 %copy-start.24 = (f32[4,128]{1,0:T(4,128)S(1)}, f32[4,128]{1,0:T(4,128)}, u32[]{:S(2)}) copy-start(f32[4,128]{1,0:T(4,128)} %get-tuple-element.369) | copy-start | bytes 6148
  109.6 62.7 %all-to-all-start.3 = ((f32[32,1,128,128]{3,2,1,0:T(8,128)}), f32[32,1,128,128]{3,2,1,0:T(8,128)S(1)}, u32[]{:S(2)}, u32[]{:S(2)}) async-start(f32[32,1,128,128]{3,2,1,0:T(8,128)} %pad_maximum_fusion), calls=%async_computation.3 | async-start | bytes 4194304 | tf_op jit(solution)/shard_map/all_to_all | solution.py:21
  172.6 1.5 copy-start.8
  172.6 1.9 %copy-start.10 = (f32[128,2048]{0,1:T(8,128)S(1)}, f32[128,2048]{0,1:T(8,128)}, u32[]{:S(2)}) copy-start(f32[128,2048]{0,1:T(8,128)} %get-tuple-element.384) | copy-start | bytes 3145732
  172.8 0.8 copy-start.1
  172.8 2.4 %copy-start.3 = (bf16[1,32,64,128]{3,2,1,0:T(8,128)(2,1)}, bf16[1,32,64,128]{3,2,1,0:T(8,128)(2,1)S(1)}, u32[]{:S(2)}) copy-start(bf16[1,32,64,128]{3,2,1,0:T(8,128)(2,1)S(1)} %get-tuple-element.347) | copy-start | bytes 1572868
  175.2 2.5 %copy-start.22 = (f32[32]{0:T(128)S(1)}, f32[32]{0:T(128)}, u32[]{:S(2)}) copy-start(f32[32]{0:T(128)} %copy-done.21) | copy-start | bytes 388
  175.3 3.1 %copy-start.4 = (bf16[1,32,64,128]{3,2,1,0:T(8,128)(2,1)S(1)}, bf16[1,32,64,128]{3,2,1,0:T(8,128)(2,1)}, u32[]{:S(2)}) copy-start(bf16[1,32,64,128]{3,2,1,0:T(8,128)(2,1)} %copy-done.3) | copy-start | bytes 1572868
  175.3 3.1 %copy-start.6 = (bf16[128,32,64]{0,2,1:T(8,128)(2,1)S(1)}, bf16[128,32,64]{0,2,1:T(8,128)(2,1)}, u32[]{:S(2)}) copy-start(bf16[128,32,64]{0,2,1:T(8,128)(2,1)} %multiply_convert_fusion.1) | copy-start | bytes 1572868
  175.3 3.1 %copy-start.12 = (f32[128,128]{1,0:T(8,128)S(1)}, f32[128,128]{1,0:T(8,128)}, u32[]{:S(2)}) copy-start(f32[128,128]{1,0:T(8,128)} %fusion.180) | copy-start | bytes 196612
  175.5 3.9 %copy-start.2 = (bf16[1,32,64,128]{3,2,1,0:T(8,128)(2,1)S(1)}, bf16[1,32,64,128]{3,2,1,0:T(8,128)(2,1)}, u32[]{:S(2)}) copy-start(bf16[1,32,64,128]{3,2,1,0:T(8,128)(2,1)} %copy-done.1) | copy-start | bytes 1572868
  175.5 3.8 %copy-start.5 = (bf16[128,32,64]{0,2,1:T(8,128)(2,1)S(1)}, bf16[128,32,64]{0,2,1:T(8,128)(2,1)}, u32[]{:S(2)}) copy-start(bf16[128,32,64]{0,2,1:T(8,128)(2,1)} %multiply_convert_fusion) | copy-start | bytes 1572868
  176.5 3.8 %copy-start.33 = (f32[128]{0:T(128)S(1)}, f32[128]{0:T(128)}, u32[]{:S(2)}) copy-start(f32[128]{0:T(128)} %fusion.184) | copy-start | bytes 1540
where the time goes:
time: 184 us; the launch traced here: 181 us
  other arithmetic  47.6 us (26%)
  blocking collectives  43.6 us (24%)
  matrix products  25.2 us (14%)
  starting transfers between devices  24.5 us (13%)
  waiting for transfers between devices  22 us (12%)
  local copies, waits for them, and re-layouts  15.6 us (8%)
  between operations  1.95 us (1%)
    psum x4, blocking collectives, one_axis_at_a_time(): return functools.reduce(lax.psum, axes, x)  43.6 us
    add x64, other arithmetic, advance(): return (factor * running + addend, running)  29.5 us
    dot_general x33, matrix products, product(): jnp.einsum(form, left_side, right_side, preferred_element_type=jnp.float32)  25.2 us
    all_to_all x1, waiting for transfers between devices, body(): lax.all_to_all(shaped[0], SEQ, split_axis=1, concat_axis=0, tiled=True)  13.7 us
    unnamed x90, local copies, waits for them, and re-layouts  9.78 us
    all_to_all x1, starting transfers between devices, body(): lax.all_to_all(shaped[2], SEQ, split_axis=1, concat_axis=0, tiled=True)  8.58 us
    all_to_all x1, waiting for transfers between devices, body(): lax.all_to_all(shaped[1], SEQ, split_axis=1, concat_axis=0, tiled=True)  8.21 us
    all_to_all x1, starting transfers between devices, body(): lax.all_to_all(shaped[1], SEQ, split_axis=1, concat_axis=0, tiled=True)  7.4 us
  transfers between devices with their start and end apart: 4, of which 2 were waited for; matrix products, arithmetic and copies ran while one was open for 25% of the time, Pallas kernels for 0%

commit v1 on v0

v1 whole, which is shorter than its diff:
```python
import functools

import jax
import jax.numpy as jnp
from jax import lax
from jax.experimental import pallas as pl
from jax.experimental.pallas import tpu as pltpu
from jax.sharding import Mesh
from jax.sharding import PartitionSpec as P

SEQ = ("seq_0", "seq_1", "seq_2")
CHIPS = ("seq_0", "seq_1")
CORE = "seq_2"
F32 = jnp.float32
BF16 = jnp.bfloat16
T = 128
N = 128
PAIRS = 16
HEADS = 32
DOCS = 8
EXT = 8
FAR = -1e30
VMEM = pl.BlockSpec(memory_space=pltpu.VMEM)
SMEM = pl.BlockSpec(memory_space=pltpu.SMEM)

NN = (((1,), (0,)), ((), ()))
NT = (((1,), (1,)), ((), ()))
TN = (((0,), (0,)), ((), ()))


def dot(a, b, dims=NN, precision=None):
    return lax.dot_general(a, b, dims, precision=precision, preferred_element_type=F32)


def exact(a, b, dims=NN):
    return dot(a, b, dims, lax.Precision.HIGHEST)


def iota(shape, dim):
    return lax.broadcasted_iota(jnp.int32, shape, dim)


def block_base():
    return lax.axis_index(SEQ) * T


def doc_starts(len_ref):
    starts, at = [], jnp.int32(0)
    for d in range(DOCS):
        starts.append(at)
        at = at + len_ref[0, d]
    return starts


def segments(starts, base, offset):
    count = jnp.zeros(offset.shape, jnp.int32)
    for s in starts:
        local = jnp.where(s >= base, s - base, jnp.int32(1 << 20))
        count = count + (offset >= local).astype(jnp.int32)
    return count


def end_count(starts, base):
    count = jnp.int32(0)
    for s in starts:
        count = count + jnp.logical_and(s >= base, s < base + T).astype(jnp.int32)
    return count


def lower_triangle():
    return (iota((T, T), 1) <= iota((T, T), 0)).astype(F32)


def weights(ld, starts, base):
    log_cum = exact(lower_triangle(), ld, NT)
    seg = segments(starts, base, iota((T, HEADS), 0))
    last = end_count(starts, base)
    log_end = log_cum[T - 1 :, :]
    w_end = jnp.where(seg == last, jnp.exp(log_end - log_cum), 0.0)
    w_start = jnp.where(seg == 0, jnp.exp(log_cum), 0.0)
    gain = jnp.exp(log_end) * (last == 0).astype(F32)
    return log_cum, w_end, w_start, gain


def spread(w, j, low):
    return jnp.where(low, w[:, 2 * j : 2 * j + 1], w[:, 2 * j + 1 : 2 * j + 2])


def cols(j):
    return slice(j * 128, (j + 1) * 128)


def prep_kernel(len_ref, v_ref, g_ref, b_ref, c_ref, ld_ref, send_ref, mine_ref, ext_ref):
    first = lax.axis_index(CORE) == 0
    base = block_base()
    starts = doc_starts(len_ref)
    _, w_end, w_start, gain = weights(ld_ref[0], starts, base)
    b_t = b_ref[0].T
    c_t = c_ref[0].T
    low = iota((T, 128), 1) < 64
    sub = iota((EXT, 128), 0)
    skip_rows = []
    for j in range(PAIRS):
        v = v_ref[0, :, cols(j)].astype(F32)
        g = g_ref[0, :, cols(j)].astype(F32)
        wv = (v * spread(w_end, j, low)).astype(BF16)
        wg = (g * spread(w_start, j, low)).astype(BF16)
        state = dot(b_t, wv)
        adjoint = dot(c_t, wg)
        mine_ref[j] = jnp.where(first, state, adjoint)
        send_ref[j, :N] = jnp.where(first, adjoint, state)
        skip_rows.append(jnp.sum(v * g, axis=0, keepdims=True))
    skips = jnp.concatenate(skip_rows, axis=0)
    lane = iota((PAIRS, 128), 1)
    row = iota((PAIRS, 128), 0)
    even = jnp.sum(jnp.where(lane < 64, skips, 0.0), axis=1, keepdims=True)
    odd = jnp.sum(jnp.where(lane < 64, 0.0, skips), axis=1, keepdims=True)
    placed = jnp.where(lane == 2 * row, even, jnp.where(lane == 2 * row + 1, odd, 0.0))
    skip = jnp.sum(placed, axis=0, keepdims=True)
    for j in range(PAIRS):
        gain_row = spread(gain, j, low[:1])
        ext = jnp.where(sub == 0, gain_row, jnp.where(sub == 1, skip, 0.0))
        send_ref[j, N:] = ext
        ext_ref[j] = ext


def combine_kernel(recv_ref, mine_ref, ext_ref, out_ref):
    sub = iota((EXT, 128), 0)
    for j in range(PAIRS):
        theirs = recv_ref[j, N:]
        ours = ext_ref[j]
        out_ref[j, :N] = theirs[:1] * mine_ref[j] + recv_ref[j, :N]
        out_ref[j, N:] = jnp.where(sub == 0, theirs * ours, theirs + ours)


def scan_kernel(in_ref, out_ref, skip_ref):
    first = lax.axis_index(CORE) == 0
    running = jnp.zeros((N, 128), F32)
    skip = jnp.zeros((EXT, 128), F32)
    for i in range(PAIRS):
        at = jnp.where(first, i, PAIRS - 1 - i)
        out_ref[at] = running
        if i < PAIRS - 1:
            running = in_ref[at, N : N + 1] * running + in_ref[at, :N]
        skip = skip + in_ref[i, N:]
    skip_ref[...] = skip


def inside_kernel(len_ref, v_ref, g_ref, b_ref, c_ref, ld_ref, out_ref, back_ref, iraw_ref, oraw_ref):
    base = block_base()
    starts = doc_starts(len_ref)
    tri = lower_triangle()
    ld = ld_ref[0]
    cum_t = exact(tri, ld, NT)
    cum_h = exact(ld, tri, NT)
    t_at = iota((T, T), 0)
    s_at = iota((T, T), 1)
    same = segments(starts, base, t_at) == segments(starts, base, s_at)
    bias = jnp.where(jnp.logical_and(s_at <= t_at, same), 0.0, FAR)
    b = b_ref[0]
    c = c_ref[0]
    scores = dot(c, b, NT)
    low = iota((T, 128), 1) < 64
    zero = jnp.zeros((T, 128), BF16)
    grad_scores = jnp.zeros((T, T), F32)
    for j in range(PAIRS):
        v = v_ref[0, :, cols(j)]
        g = g_ref[0, :, cols(j)]
        v_two = jnp.concatenate([jnp.where(low, v, zero), jnp.where(low, zero, v)], axis=0)
        g_two = jnp.concatenate([jnp.where(low, g, zero), jnp.where(low, zero, g)], axis=0)
        grad_mix = dot(g, v_two, NT)
        mixes = []
        for k in range(2):
            h = 2 * j + k
            decay = jnp.exp(cum_t[:, h : h + 1] - cum_h[h : h + 1, :] + bias)
            mixes.append((scores * decay).astype(BF16))
            grad_scores = grad_scores + grad_mix[:, k * T : (k + 1) * T] * decay
        out_ref[:, cols(j)] = dot(jnp.concatenate(mixes, axis=1), v_two)
        back_ref[:, cols(j)] = dot(jnp.concatenate(mixes, axis=0), g_two, TN)
    half = grad_scores.astype(BF16)
    iraw_ref[...] = dot(half, c, TN)
    oraw_ref[...] = dot(half, b)


def pass_on_kernel(x_ref, mine_ref, ext_ref, out_ref):
    for j in range(PAIRS):
        out_ref[j] = ext_ref[j, :1] * x_ref[j] + mine_ref[j]


def finish_kernel(
    scales,
    len_ref,
    skip_ref,
    v_ref,
    g_ref,
    b_ref,
    c_ref,
    ld_ref,
    x_ref,
    y_ref,
    within_ref,
    back_ref,
    iraw_ref,
    oraw_ref,
    mixed_ref,
    vgrad_ref,
    igrad_ref,
    ograd_ref,
    dgrad_ref,
):
    in_scale, out_scale, decay_scale = scales
    first = lax.axis_index(CORE) == 0
    base = block_base()
    starts = doc_starts(len_ref)
    _, w_end, w_start, gain = weights(ld_ref[0], starts, base)
    b = b_ref[0]
    c = c_ref[0]
    low = iota((T, 128), 1) < 64
    iraw = iraw_ref[...]
    oraw = oraw_ref[...]
    cum_grad = jnp.zeros((T, 128), F32)
    ends = jnp.zeros((1, 128), F32)
    lane = iota((128, 128), 0)
    head = iota((128, 128), 1)
    for j in range(PAIRS):
        x = x_ref[j]
        y = y_ref[j]
        state = jnp.where(first, x, y)
        adjoint = jnp.where(first, y, x)
        state_half = state.astype(BF16)
        adjoint_half = adjoint.astype(BF16)
        v16 = v_ref[0, :, cols(j)]
        g16 = g_ref[0, :, cols(j)]
        v = v16.astype(F32)
        g = g16.astype(F32)
        we = spread(w_end, j, low)
        ws = spread(w_start, j, low)
        skip = jnp.where(low[:1], skip_ref[2 * j], skip_ref[2 * j + 1])
        out = within_ref[:, cols(j)] + ws * dot(c, state_half)
        tail = we * dot(b, adjoint_half)
        back = back_ref[:, cols(j)] + tail
        mixed_ref[0, :, cols(j)] = (out + skip * v).astype(BF16)
        vgrad_ref[0, :, cols(j)] = (back + skip * g).astype(BF16)
        iraw = iraw + dot((v * we).astype(BF16), adjoint_half, NT)
        oraw = oraw + dot((g * ws).astype(BF16), state_half, NT)
        change = g * out - v * back
        gain_row = spread(gain, j, low[:1])
        end = jnp.sum(v * tail, axis=0, keepdims=True) + gain_row * jnp.sum(
            state * adjoint, axis=0, keepdims=True
        )
        change = jnp.where(iota((T, 128), 0) == T - 1, change + end, change)
        pick = (head == 2 * j + jnp.where(lane < 64, 0, 1)).astype(BF16)
        hi = change.astype(BF16)
        lo = (change - hi.astype(F32)).astype(BF16)
        cum_grad = cum_grad + dot(hi, pick) + dot(lo, pick)
    igrad_ref[0] = iraw * in_scale
    ograd_ref[0] = oraw * out_scale
    upper = (iota((T, T), 1) <= iota((T, T), 0)).astype(F32)
    total = exact(cum_grad, upper, TN)[:HEADS]
    offset = iota((HEADS, T), 1)
    reset = jnp.zeros((HEADS, T), jnp.bool_)
    for s in starts:
        reset = jnp.logical_or(reset, offset + base == s)
    dgrad_ref[0] = jnp.where(reset, 0.0, total * decay_scale)


def call(kernel, outs, *args, scalars=0, flops=0, moved=0):
    return pl.pallas_call(
        kernel,
        out_shape=outs,
        in_specs=[SMEM] * scalars + [VMEM] * (len(args) - scalars),
        out_specs=jax.tree.map(lambda _: VMEM, outs),
        cost_estimate=pl.CostEstimate(flops=flops, bytes_accessed=moved, transcendentals=0),
    )(*args)


def f32(*shape):
    return jax.ShapeDtypeStruct(shape, F32)


def swap_cores(x):
    return lax.ppermute(x, CORE, [(0, 1), (1, 0)])


def body(values_in, input_proj, output_proj, log_decay, doc_lengths, skip_gain, out_cotangent):
    inputs = (doc_lengths, values_in, out_cotangent, input_proj, output_proj, log_decay)
    shards = lax.axis_size(SEQ)
    seq_count = lax.axis_size("dp")
    token_count = shards * T
    inner = values_in.shape[2]
    head_dim = inner // HEADS
    send, mine, ext = call(
        prep_kernel,
        (f32(PAIRS, N + EXT, 128), f32(PAIRS, N, 128), f32(PAIRS, EXT, 128)),
        *inputs,
        scalars=1,
        flops=2 * 2 * T * N * inner,
        moved=4 << 20,
    )
    recv = swap_cores(send)
    chip = call(combine_kernel, f32(PAIRS, N + EXT, 128), recv, mine, ext, moved=3 << 20)
    gathered = lax.all_to_all(chip, CHIPS, split_axis=0, concat_axis=0, tiled=True)
    within, back, iraw, oraw = call(
        inside_kernel,
        (f32(T, inner), f32(T, inner), f32(T, N), f32(T, N)),
        *inputs,
        scalars=1,
        flops=40 * 2 * T * N * inner,
        moved=20 << 20,
    )
    prefix, skip = call(
        scan_kernel, (f32(PAIRS, N, 128), f32(EXT, 128)), gathered, moved=2 << 20
    )
    x = lax.all_to_all(prefix, CHIPS, split_axis=0, concat_axis=0, tiled=True)
    for step in (1, 2, 4):
        skip = skip + lax.ppermute(skip, "dp", [(i, i ^ step) for i in range(8)])
    y = swap_cores(call(pass_on_kernel, f32(PAIRS, N, 128), x, mine, ext, moved=3 << 20))
    scales = (
        float(1.0 / inner**0.5),
        float((N / (inner * token_count)) ** 0.5),
        float(1.0 / (head_dim * token_count) ** 0.5),
    )
    mixed, values_grad, input_grad, output_grad, decay_grad = call(
        functools.partial(finish_kernel, scales),
        (
            jax.ShapeDtypeStruct((1, T, inner), BF16),
            jax.ShapeDtypeStruct((1, T, inner), BF16),
            f32(1, T, N),
            f32(1, T, N),
            f32(1, HEADS, T),
        ),
        doc_lengths,
        skip_gain,
        *inputs[1:],
        x,
        y,
        within,
        back,
        iraw,
        oraw,
        scalars=2,
        flops=4 * 2 * T * N * inner,
        moved=8 << 20,
    )
    skip_grad = skip[1, :HEADS] * (1.0 / (seq_count * token_count * head_dim) ** 0.5)
    return mixed, values_grad, input_grad, output_grad, decay_grad, skip_grad


def solution(mesh):
    finer = Mesh(mesh.devices.reshape(mesh.shape["dp"], 4, 4, 2), ("dp",) + SEQ)
    placed = (
        P("dp", SEQ, None),
        P("dp", SEQ, None),
        P("dp", SEQ, None),
        P("dp", None, SEQ),
        P("dp", None),
        P(),
        P("dp", SEQ, None),
    )
    return jax.shard_map(
        body,
        mesh=finer,
        in_specs=placed,
        out_specs=(
            P("dp", SEQ, None),
            P("dp", SEQ, None),
            P("dp", SEQ, None),
            P("dp", SEQ, None),
            P("dp", None, SEQ),
            P(),
        ),
        check_vma=False,
    )
```

time: 184 us -> 90.4 us (0.49); the launches traced: 181 us -> 89.8 us
  other arithmetic: 47.6 us -> 0.53 us
  matrix products: 25.2 us -> 0 us
  Pallas kernels: 0 us -> 23.5 us
  waiting for transfers between devices: 22 us -> 4.59 us
  local copies, waits for them, and re-layouts: 15.6 us -> 1.98 us
  starting transfers between devices: 24.5 us -> 17.2 us
  blocking collectives: 43.6 us -> 41.4 us
    psum x4 -> x0, blocking collectives: 43.6 us -> none  [one_axis_at_a_time(): return functools.reduce(lax.psum, axes, x)]
    all_to_all x0 -> x2, blocking collectives: none -> 41.4 us  [the longest x1 22.3 us: body(): lax.all_to_all(chip, CHIPS, split_axis=0, concat_axis=0, tiled=True)]
    add x66 -> x3, other arithmetic: 29.5 us -> 0.01 us  [body(): skip = skip + lax.ppermute(skip, 'dp', [(i, i ^ step) for i in range(8)])]
    dot_general x33 -> x0, matrix products: 25.2 us -> none  [product(): jnp.einsum(form, left_side, right_side, preferred_element_type=jnp.float32)]
    all_to_all x4 -> x0, starting transfers between devices: 24.5 us -> none  [the longest x1 8.58 us: body(): lax.all_to_all(shaped[2], SEQ, split_axis=1, concat_axis=0, tiled=True)]
    pallas_call x0 -> x6, Pallas kernels: none -> 23.5 us  [call(): pl.pallas_call(kernel, out_shape=outs, in_specs=[SMEM] * scalars + [VMEM]...]
    all_to_all x4 -> x0, waiting for transfers between devices: 22 us -> none  [the longest x1 13.7 us: body(): lax.all_to_all(shaped[0], SEQ, split_axis=1, concat_axis=0, tiled=True)]
    ppermute x0 -> x5, starting transfers between devices: none -> 17.2 us  [the longest x3 10.7 us: body(): skip = skip + lax.ppermute(skip, 'dp', [(i, i ^ step) for i in range(8)])]
  transfers between devices with their start and end apart: 4 -> 5, of which waited for: 2 -> 3; matrix products, arithmetic and copies ran while one was open for 25% -> 1% of each run, Pallas kernels for 0% -> 5%
where the time goes in v1:
time: 90.4 us; the launch traced here: 89.8 us
  blocking collectives  41.4 us (46%)
  Pallas kernels  23.5 us (26%)
  starting transfers between devices  17.2 us (19%)
  waiting for transfers between devices  4.59 us (5%)
  local copies, waits for them, and re-layouts  1.98 us (2%)
    pallas_call x6, Pallas kernels, call(): pl.pallas_call(kernel, out_shape=outs, in_specs=[SMEM] * scalars + [VMEM]...  23.5 us
    all_to_all x1, blocking collectives, body(): lax.all_to_all(chip, CHIPS, split_axis=0, concat_axis=0, tiled=True)  22.3 us
    all_to_all x1, blocking collectives, body(): x = lax.all_to_all(prefix, CHIPS, split_axis=0, concat_axis=0, tiled=True)  19.1 us
    ppermute x3, starting transfers between devices, body(): skip = skip + lax.ppermute(skip, 'dp', [(i, i ^ step) for i in range(8)])  10.7 us
    ppermute x2, starting transfers between devices, swap_cores(): return lax.ppermute(x, CORE, [(0, 1), (1, 0)])  6.51 us
    ppermute x2, waiting for transfers between devices, swap_cores(): return lax.ppermute(x, CORE, [(0, 1), (1, 0)])  2.59 us
    ppermute x3, waiting for transfers between devices, body(): skip = skip + lax.ppermute(skip, 'dp', [(i, i ^ step) for i in range(8)])  1.99 us
    unnamed x6, local copies, waits for them, and re-layouts  1.98 us
  transfers between devices with their start and end apart: 5, of which 3 were waited for; matrix products, arithmetic and copies ran while one was open for 1% of the time, Pallas kernels for 5%

profile of v1, /device:TPU:1, one launch (start us, length us, event | category | flops | bytes accessed | tf_op | source)
XLA Modules:
  0.0 89.8 jit_solution(9113995206964872673)
XLA Ops:
  0.6 4.4 %shard_map.118 = (f32[16,136,128]{2,1,0:T(8,128)}, f32[16,128,128]{2,1,0:T(8,128)}, f32[16,8,128]{2,1,0:T(8,128)}) custom-call(s32[1,8]{1,0:T(1,128)} %len_ref.5, bf16[1,128,2048]{2,1,0:T(8,128)(2,1)} %v_ref.5, bf16[1,128,2048]{2,1,0:T(8,128)(2,1)} %g_ref.5, bf16[1,128,128]{2,1,0:T(8,128)(2,1)} %b_ref.5, bf16[1,128,128]{2,1,0:T(8,128)(2,1)} %c_ref.5, ...), custom_call_target="tpu_custom_call" | custom-call | flops 134217728 | bytes 4194304 | tf_op jit(solution)/shard_map/pallas_call | solution.py:268
  5.0 3.2 %collective-permute-start = (f32[16,136,128]{2,1,0:T(8,128)}, f32[16,136,128]{2,1,0:T(8,128)S(1)}, u32[]{:S(2)}, u32[]{:S(2)}) collective-permute-start(f32[16,136,128]{2,1,0:T(8,128)} %get-tuple-element.20), channel_id=1, source_target_pairs={{0,1},{1,0},{2,3},{3,2},{4,5},{5,4},{6,7},{7,6},{8,9},{9,8},{10,11... | collective-permute-start | bytes 3342344 | tf_op jit(solution)/shard_map/ppermute | solution.py:282
  8.2 2.6 %collective-permute-done.recv_ref = f32[16,136,128]{2,1,0:T(8,128)S(1)} collective-permute-done((f32[16,136,128]{2,1,0:T(8,128)}, f32[16,136,128]{2,1,0:T(8,128)S(1)}, u32[]{:S(2)}, u32[]{:S(2)}) %collective-permute-start) | collective-permute-done | bytes 1114144 | tf_op jit(solution)/shard_map/ppermute | solution.py:282
  10.8 0.0 copy-start
  10.8 1.0 %copy-done = f32[16,136,128]{2,1,0:T(8,128)} copy-done((f32[16,136,128]{2,1,0:T(8,128)}, f32[16,136,128]{2,1,0:T(8,128)S(1)}, u32[]{:S(2)}) %copy-start) | copy-done | bytes 1114136
  11.8 2.7 %shard_map.119 = f32[16,136,128]{2,1,0:T(8,128)} custom-call(f32[16,136,128]{2,1,0:T(8,128)} %copy-done, f32[16,128,128]{2,1,0:T(8,128)} %get-tuple-element.21.mine_ref, f32[16,8,128]{2,1,0:T(8,128)} %get-tuple-element.22.ext_ref), custom_call_target="tpu_custom_call" | custom-call | bytes 3145728 | tf_op jit(solution)/shard_map/pallas_call | solution.py:268
  14.5 22.3 %all_to_all.10.in_ref = f32[16,136,128]{2,1,0:T(8,128)} all-to-all(f32[16,136,128]{2,1,0:T(8,128)} %shard_map.119), channel_id=1, replica_groups=mesh['dp'=8,'seq_0'=4,'seq_1'=4,'seq_2'=2] {'seq_0','seq_1'}, dimensions={0} | all-to-all | bytes 2228224 | tf_op jit(solution)/shard_map/all_to_all | solution.py:302
  36.8 2.3 %shard_map.120 = (f32[16,128,128]{2,1,0:T(8,128)}, f32[8,128]{1,0:T(8,128)}) custom-call(f32[16,136,128]{2,1,0:T(8,128)} %all_to_all.10.in_ref), custom_call_target="tpu_custom_call" | custom-call | bytes 2097152 | tf_op jit(solution)/shard_map/pallas_call | solution.py:268
  39.1 19.1 %all_to_all.11.x_ref = f32[16,128,128]{2,1,0:T(8,128)} all-to-all(f32[16,128,128]{2,1,0:T(8,128)} %get-tuple-element.23), channel_id=1, replica_groups=mesh['dp'=8,'seq_0'=4,'seq_1'=4,'seq_2'=2] {'seq_0','seq_1'}, dimensions={0} | all-to-all | bytes 2097152 | tf_op jit(solution)/shard_map/all_to_all | solution.py:314
  58.2 0.0 copy-start.2
  58.2 2.7 %shard_map.121 = f32[16,128,128]{2,1,0:T(8,128)} custom-call(f32[16,128,128]{2,1,0:T(8,128)} %all_to_all.11.x_ref, f32[16,128,128]{2,1,0:T(8,128)} %get-tuple-element.21.mine_ref, f32[16,8,128]{2,1,0:T(8,128)} %get-tuple-element.22.ext_ref), custom_call_target="tpu_custom_call" | custom-call | bytes 3145728 | tf_op jit(solution)/shard_map/pallas_call | solution.py:268
  60.8 3.3 %collective-permute-start.1 = (f32[16,128,128]{2,1,0:T(8,128)}, f32[16,128,128]{2,1,0:T(8,128)S(1)}, u32[]{:S(2)}, u32[]{:S(2)}) collective-permute-start(f32[16,128,128]{2,1,0:T(8,128)} %shard_map.121), channel_id=1, source_target_pairs={{0,1},{1,0},{2,3},{3,2},{4,5},{5,4},{6,7},{7,6},{8,9},{9,8},{10,11... | collective-permute-start | bytes 3145736 | tf_op jit(solution)/shard_map/ppermute | solution.py:282
  64.2 0.0 copy-done.2
  64.2 1.6 %collective-permute-start.2 = (f32[8,128]{1,0:T(8,128)S(1)}, f32[8,128]{1,0:T(8,128)S(1)}, u32[]{:S(2)}, u32[]{:S(2)}) collective-permute-start(f32[8,128]{1,0:T(8,128)S(1)} %copy-done.2), channel_id=1, source_target_pairs={{0,32},{32,0},{64,96},{96,64},{128,160},{160,128},{192,224},{224,1... | collective-permute-start | bytes 12296 | tf_op jit(solution)/shard_map/ppermute | solution.py:316
  65.8 1.0 %collective-permute-done.2 = f32[8,128]{1,0:T(8,128)S(1)} collective-permute-done((f32[8,128]{1,0:T(8,128)S(1)}, f32[8,128]{1,0:T(8,128)S(1)}, u32[]{:S(2)}, u32[]{:S(2)}) %collective-permute-start.2) | collective-permute-done | bytes 4128 | tf_op jit(solution)/shard_map/ppermute | solution.py:316
  66.8 3.0 %collective-permute-start.3 = (f32[8,128]{1,0:T(8,128)S(1)}, f32[8,128]{1,0:T(8,128)S(1)}, u32[]{:S(2)}, u32[]{:S(2)}) collective-permute-start(f32[8,128]{1,0:T(8,128)S(1)} %add.9), channel_id=1, source_target_pairs={{0,64},{32,96},{64,0},{96,32},{128,192},{160,224},{192,128},{224,1... | collective-permute-start | bytes 12296 | tf_op jit(solution)/shard_map/ppermute | solution.py:316
  69.8 1.0 %collective-permute-done.3 = f32[8,128]{1,0:T(8,128)S(1)} collective-permute-done((f32[8,128]{1,0:T(8,128)S(1)}, f32[8,128]{1,0:T(8,128)S(1)}, u32[]{:S(2)}, u32[]{:S(2)}) %collective-permute-start.3) | collective-permute-done | bytes 4128 | tf_op jit(solution)/shard_map/ppermute | solution.py:316
  70.8 6.1 %collective-permute-start.4 = (f32[8,128]{1,0:T(8,128)S(1)}, f32[8,128]{1,0:T(8,128)S(1)}, u32[]{:S(2)}, u32[]{:S(2)}) collective-permute-start(f32[8,128]{1,0:T(8,128)S(1)} %add.10), channel_id=1, source_target_pairs={{0,128},{32,160},{64,192},{96,224},{128,0},{160,32},{192,64},{224,... | collective-permute-start | bytes 12296 | tf_op jit(solution)/shard_map/ppermute | solution.py:316
  76.9 4.6 %shard_map.122 = (f32[128,2048]{1,0:T(8,128)}, f32[128,2048]{1,0:T(8,128)}, f32[128,128]{1,0:T(8,128)}, f32[128,128]{1,0:T(8,128)}) custom-call(s32[1,8]{1,0:T(1,128)} %len_ref.5, bf16[1,128,2048]{2,1,0:T(8,128)(2,1)} %v_ref.5, bf16[1,128,2048]{2,1,0:T(8,128)(2,1)} %g_ref.5, bf16[1,128,128]{2,1,0:T(8,128)(2,1)} %b_ref.5, bf16[1,128,128]{2,1,0:T(8,128)(2,1)} %c_ref.5, ...), custom_call_target="tpu_custom_call" | custom-call | flops 2684354560 | bytes 20971520 | tf_op jit(solution)/shard_map/pallas_call | solution.py:268
  81.5 0.0 collective-permute-done.4
  81.5 0.5 multiply_bitcast_fusion
  82.0 0.0 collective-permute-done.1.y_ref
  82.0 0.0 copy-start.1
  82.0 1.0 %copy-done.1 = f32[16,128,128]{2,1,0:T(8,128)} copy-done((f32[16,128,128]{2,1,0:T(8,128)}, f32[16,128,128]{2,1,0:T(8,128)S(1)}, u32[]{:S(2)}) %copy-start.1) | copy-done | bytes 1048600
  83.0 6.8 %shard_map.123 = (bf16[1,128,2048]{2,1,0:T(8,128)(2,1)}, bf16[1,128,2048]{2,1,0:T(8,128)(2,1)}, f32[1,128,128]{2,1,0:T(8,128)}, f32[1,128,128]{2,1,0:T(8,128)}, f32[1,32,128]{2,1,0:T(8,128)}) custom-call(s32[1,8]{1,0:T(1,128)} %len_ref.5, f32[32]{0:T(128)} %skip_ref.1, bf16[1,128,2048]{2,1,0:T(8,128)(2,1)} %v_ref.5, bf16[1,128,2048]{2,1,0:T(8,128)(2,1)} %g_ref.5, ...), custom_call_target="tpu_custom_call" | custom-call | flops 268435456 | bytes 8388608 | tf_op jit(solution)/shard_map/pallas_call | solution.py:268
  (3 shorter events, 0.0 us)
Async XLA Ops:
  5.0 5.8 %collective-permute-start = (f32[16,136,128]{2,1,0:T(8,128)}, f32[16,136,128]{2,1,0:T(8,128)S(1)}, u32[]{:S(2)}, u32[]{:S(2)}) collective-permute-start(f32[16,136,128]{2,1,0:T(8,128)} %get-tuple-element.20), channel_id=1, source_target_pairs={{0,1},{1,0},{2,3},{3,2},{4,5},{5,4},{6,7},{7,6},{8,9},{9,8},{10,11... | collective-permute-start | bytes 3342344 | tf_op jit(solution)/shard_map/ppermute | solution.py:282
  10.8 1.0 %copy-start = (f32[16,136,128]{2,1,0:T(8,128)}, f32[16,136,128]{2,1,0:T(8,128)S(1)}, u32[]{:S(2)}) copy-start(f32[16,136,128]{2,1,0:T(8,128)S(1)} %collective-permute-done.recv_ref) | copy-start | bytes 3342340
  58.2 6.0 %copy-start.2 = (f32[8,128]{1,0:T(8,128)S(1)}, f32[8,128]{1,0:T(8,128)}, u32[]{:S(2)}) copy-start(f32[8,128]{1,0:T(8,128)} %get-tuple-element.33) | copy-start | bytes 12292
  60.8 21.2 %collective-permute-start.1 = (f32[16,128,128]{2,1,0:T(8,128)}, f32[16,128,128]{2,1,0:T(8,128)S(1)}, u32[]{:S(2)}, u32[]{:S(2)}) collective-permute-start(f32[16,128,128]{2,1,0:T(8,128)} %shard_map.121), channel_id=1, source_target_pairs={{0,1},{1,0},{2,3},{3,2},{4,5},{5,4},{6,7},{7,6},{8,9},{9,8},{10,11... | collective-permute-start | bytes 3145736 | tf_op jit(solution)/shard_map/ppermute | solution.py:282
  64.2 2.6 %collective-permute-start.2 = (f32[8,128]{1,0:T(8,128)S(1)}, f32[8,128]{1,0:T(8,128)S(1)}, u32[]{:S(2)}, u32[]{:S(2)}) collective-permute-start(f32[8,128]{1,0:T(8,128)S(1)} %copy-done.2), channel_id=1, source_target_pairs={{0,32},{32,0},{64,96},{96,64},{128,160},{160,128},{192,224},{224,1... | collective-permute-start | bytes 12296 | tf_op jit(solution)/shard_map/ppermute | solution.py:316
  66.8 4.0 %collective-permute-start.3 = (f32[8,128]{1,0:T(8,128)S(1)}, f32[8,128]{1,0:T(8,128)S(1)}, u32[]{:S(2)}, u32[]{:S(2)}) collective-permute-start(f32[8,128]{1,0:T(8,128)S(1)} %add.9), channel_id=1, source_target_pairs={{0,64},{32,96},{64,0},{96,32},{128,192},{160,224},{192,128},{224,1... | collective-permute-start | bytes 12296 | tf_op jit(solution)/shard_map/ppermute | solution.py:316
  70.8 10.7 %collective-permute-start.4 = (f32[8,128]{1,0:T(8,128)S(1)}, f32[8,128]{1,0:T(8,128)S(1)}, u32[]{:S(2)}, u32[]{:S(2)}) collective-permute-start(f32[8,128]{1,0:T(8,128)S(1)} %add.10), channel_id=1, source_target_pairs={{0,128},{32,160},{64,192},{96,224},{128,0},{160,32},{192,64},{224,... | collective-permute-start | bytes 12296 | tf_op jit(solution)/shard_map/ppermute | solution.py:316
  82.0 1.0 %copy-start.1 = (f32[16,128,128]{2,1,0:T(8,128)}, f32[16,128,128]{2,1,0:T(8,128)S(1)}, u32[]{:S(2)}) copy-start(f32[16,128,128]{2,1,0:T(8,128)S(1)} %collective-permute-done.1.y_ref) | copy-start | bytes 3145732

commit v2 on v1

--- a/solution.py
+++ b/solution.py
@@ -22,6 +22,8 @@
 FAR = -1e30
 VMEM = pl.BlockSpec(memory_space=pltpu.VMEM)
 SMEM = pl.BlockSpec(memory_space=pltpu.SMEM)
+ANY = pl.BlockSpec(memory_space=pl.ANY)
+HBM = pl.BlockSpec(memory_space=pltpu.HBM)
 
 NN = (((1,), (0,)), ((), ()))
 NT = (((1,), (1,)), ((), ()))
@@ -124,29 +126,43 @@
         ext_ref[j] = ext
 
 
-def combine_kernel(recv_ref, mine_ref, ext_ref, out_ref):
+def put(buffer, out_ref, sems, j):
+    return pltpu.make_async_copy(buffer.at[j], out_ref.at[j], sems.at[j])
+
+
+def combine_kernel(recv_ref, mine_ref, ext_ref, out_ref, buffer, sems):
     sub = iota((EXT, 128), 0)
+    copies = []
     for j in range(PAIRS):
         theirs = recv_ref[j, N:]
         ours = ext_ref[j]
-        out_ref[j, :N] = theirs[:1] * mine_ref[j] + recv_ref[j, :N]
-        out_ref[j, N:] = jnp.where(sub == 0, theirs * ours, theirs + ours)
-
-
-def scan_kernel(in_ref, out_ref, skip_ref):
+        buffer[j, :N] = theirs[:1] * mine_ref[j] + recv_ref[j, :N]
+        buffer[j, N:] = jnp.where(sub == 0, theirs * ours, theirs + ours)
+        copies.append(put(buffer, out_ref, sems, j))
+        copies[-1].start()
+    for copy in copies:
+        copy.wait()
+
+
+def scan_kernel(_, in_ref, skip_ref, out_ref, buffer, sems):
     first = lax.axis_index(CORE) == 0
     running = jnp.zeros((N, 128), F32)
     skip = jnp.zeros((EXT, 128), F32)
+    copies = []
     for i in range(PAIRS):
         at = jnp.where(first, i, PAIRS - 1 - i)
-        out_ref[at] = running
+        buffer[i] = running
+        copies.append(pltpu.make_async_copy(buffer.at[i], out_ref.at[at], sems.at[i]))
+        copies[-1].start()
         if i < PAIRS - 1:
             running = in_ref[at, N : N + 1] * running + in_ref[at, :N]
         skip = skip + in_ref[i, N:]
     skip_ref[...] = skip
-
-
-def inside_kernel(len_ref, v_ref, g_ref, b_ref, c_ref, ld_ref, out_ref, back_ref, iraw_ref, oraw_ref):
+    for copy in copies:
+        copy.wait()
+
+
+def inside_kernel(_, len_ref, v_ref, g_ref, b_ref, c_ref, ld_ref, out_ref, back_ref, iraw_ref, oraw_ref):
     base = block_base()
     starts = doc_starts(len_ref)
     tri = lower_triangle()
@@ -182,7 +198,7 @@
     oraw_ref[...] = dot(half, b)
 
 
-def pass_on_kernel(x_ref, mine_ref, ext_ref, out_ref):
+def pass_on_kernel(_, x_ref, mine_ref, ext_ref, out_ref):
     for j in range(PAIRS):
         out_ref[j] = ext_ref[j, :1] * x_ref[j] + mine_ref[j]
 
@@ -264,12 +280,21 @@
     dgrad_ref[0] = jnp.where(reset, 0.0, total * decay_scale)
 
 
-def call(kernel, outs, *args, scalars=0, flops=0, moved=0):
+def call(kernel, outs, *args, after=(), scalars=0, flops=0, moved=0, limit=16, staged=False):
+    args = tuple(after) + args
+    free = len(after)
+    out_specs = [VMEM] * len(outs)
+    scratch = []
+    if staged:
+        out_specs[-1] = HBM
+        scratch = [pltpu.VMEM(outs[-1].shape, F32), pltpu.SemaphoreType.DMA((PAIRS,))]
     return pl.pallas_call(
         kernel,
         out_shape=outs,
-        in_specs=[SMEM] * scalars + [VMEM] * (len(args) - scalars),
-        out_specs=jax.tree.map(lambda _: VMEM, outs),
+        in_specs=[ANY] * free + [SMEM] * scalars + [VMEM] * (len(args) - scalars - free),
+        out_specs=out_specs,
+        scratch_shapes=scratch,
+        compiler_params=pltpu.CompilerParams(vmem_limit_bytes=limit << 20),
         cost_estimate=pl.CostEstimate(flops=flops, bytes_accessed=moved, transcendentals=0),
     )(*args)
 
@@ -298,23 +323,34 @@
         moved=4 << 20,
     )
     recv = swap_cores(send)
-    chip = call(combine_kernel, f32(PAIRS, N + EXT, 128), recv, mine, ext, moved=3 << 20)
+    (chip,) = call(
+        combine_kernel, (f32(PAIRS, N + EXT, 128),), recv, mine, ext, moved=3 << 20, staged=True
+    )
     gathered = lax.all_to_all(chip, CHIPS, split_axis=0, concat_axis=0, tiled=True)
     within, back, iraw, oraw = call(
         inside_kernel,
         (f32(T, inner), f32(T, inner), f32(T, N), f32(T, N)),
         *inputs,
+        after=(chip,),
         scalars=1,
         flops=40 * 2 * T * N * inner,
         moved=20 << 20,
     )
-    prefix, skip = call(
-        scan_kernel, (f32(PAIRS, N, 128), f32(EXT, 128)), gathered, moved=2 << 20
+    skip, prefix = call(
+        scan_kernel,
+        (f32(EXT, 128), f32(PAIRS, N, 128)),
+        gathered,
+        after=(iraw,),
+        moved=2 << 20,
+        staged=True,
     )
     x = lax.all_to_all(prefix, CHIPS, split_axis=0, concat_axis=0, tiled=True)
     for step in (1, 2, 4):
         skip = skip + lax.ppermute(skip, "dp", [(i, i ^ step) for i in range(8)])
-    y = swap_cores(call(pass_on_kernel, f32(PAIRS, N, 128), x, mine, ext, moved=3 << 20))
+    (passed,) = call(
+        pass_on_kernel, (f32(PAIRS, N, 128),), x, mine, ext, after=(skip,), moved=3 << 20
+    )
+    y = swap_cores(passed)
     scales = (
         float(1.0 / inner**0.5),
         float((N / (inner * token_count)) ** 0.5),

time: 90.4 us -> 70.9 us (0.78)
  blocking collectives: 41.4 us -> 0 us
  waiting for transfers between devices: 4.59 us -> 19.9 us
  starting transfers between devices: 17.2 us -> 28.1 us
  Pallas kernels: 23.5 us -> 13 us
  local copies, waits for them, and re-layouts: 1.98 us -> 7.95 us
    all_to_all x2 -> x0, blocking collectives: 41.4 us -> none  [the longest x1 22.3 us: body(): lax.all_to_all(chip, CHIPS, split_axis=0, concat_axis=0, tiled=True)]
    all_to_all x0 -> x2, waiting for transfers between devices: none -> 12.5 us  [the longest x1 11.5 us: body(): lax.all_to_all(chip, CHIPS, split_axis=0, concat_axis=0, tiled=True)]
    pallas_call x6, Pallas kernels: 23.5 us -> 13 us  [call(): pl.pallas_call(kernel, out_shape=outs, in_specs=[ANY] * free + [SMEM] * s...]
    all_to_all x0 -> x2, starting transfers between devices: none -> 9.77 us  [the longest x1 5.19 us: body(): lax.all_to_all(chip, CHIPS, split_axis=0, concat_axis=0, tiled=True)]
    unnamed x6 -> x36, local copies, waits for them, and re-layouts: 1.98 us -> 7.95 us
    ppermute x2, waiting for transfers between devices: 2.59 us -> 4.15 us  [swap_cores(): return lax.ppermute(x, CORE, [(0, 1), (1, 0)])]
    ppermute x2, starting transfers between devices: 6.51 us -> 7.84 us  [swap_cores(): return lax.ppermute(x, CORE, [(0, 1), (1, 0)])]
    ppermute x3, waiting for transfers between devices: 1.99 us -> 3.28 us  [body(): skip = skip + lax.ppermute(skip, 'dp', [(i, i ^ step) for i in range(8)])]
  transfers between devices with their start and end apart: 5 -> 7, of which waited for: 3 -> 7; matrix products, arithmetic and copies ran while one was open for 1% -> 1% of each run, Pallas kernels for 5% -> 4%
where the time goes in v2:
time: 70.9 us; the launch traced here: 70.3 us
  starting transfers between devices  28.1 us (40%)
  waiting for transfers between devices  19.9 us (28%)
  Pallas kernels  13 us (18%)
  local copies, waits for them, and re-layouts  7.95 us (11%)
  between operations  0.81 us (1%)
    pallas_call x6, Pallas kernels, call(): pl.pallas_call(kernel, out_shape=outs, in_specs=[ANY] * free + [SMEM] * s...  13 us
    all_to_all x1, waiting for transfers between devices, body(): lax.all_to_all(chip, CHIPS, split_axis=0, concat_axis=0, tiled=True)  11.5 us
    ppermute x3, starting transfers between devices, body(): skip = skip + lax.ppermute(skip, 'dp', [(i, i ^ step) for i in range(8)])  10.5 us
    unnamed x36, local copies, waits for them, and re-layouts  7.95 us
    ppermute x2, starting transfers between devices, swap_cores(): return lax.ppermute(x, CORE, [(0, 1), (1, 0)])  7.84 us
    all_to_all x1, starting transfers between devices, body(): lax.all_to_all(chip, CHIPS, split_axis=0, concat_axis=0, tiled=True)  5.19 us
    all_to_all x1, starting transfers between devices, body(): x = lax.all_to_all(prefix, CHIPS, split_axis=0, concat_axis=0, tiled=True)  4.58 us
    ppermute x2, waiting for transfers between devices, swap_cores(): return lax.ppermute(x, CORE, [(0, 1), (1, 0)])  4.15 us
  transfers between devices with their start and end apart: 7, of which 7 were waited for; matrix products, arithmetic and copies ran while one was open for 1% of the time, Pallas kernels for 4%

profile of v2, /device:TPU:1, one launch (start us, length us, event | category | flops | bytes accessed | tf_op | source)
XLA Modules:
  0.0 70.3 jit_solution(5672711000123919846)
XLA Ops:
  0.6 0.0 copy-start
  0.6 1.0 %copy-done = bf16[1,128,2048]{2,1,0:T(8,128)(2,1)S(1)} copy-done((bf16[1,128,2048]{2,1,0:T(8,128)(2,1)S(1)}, bf16[1,128,2048]{2,1,0:T(8,128)(2,1)}, u32[]{:S(2)}) %copy-start) | copy-done | bytes 524312
  1.7 1.0 %copy-done.2 = bf16[1,128,2048]{2,1,0:T(8,128)(2,1)S(1)} copy-done((bf16[1,128,2048]{2,1,0:T(8,128)(2,1)S(1)}, bf16[1,128,2048]{2,1,0:T(8,128)(2,1)}, u32[]{:S(2)}) %copy-start.2) | copy-done | bytes 524312
  2.7 0.8 %copy-done.9 = bf16[1,128,128]{2,1,0:T(8,128)(2,1)S(1)} copy-done((bf16[1,128,128]{2,1,0:T(8,128)(2,1)S(1)}, bf16[1,128,128]{2,1,0:T(8,128)(2,1)}, u32[]{:S(2)}) %copy-start.9) | copy-done | bytes 32792
  3.5 0.8 %copy-done.11 = bf16[1,128,128]{2,1,0:T(8,128)(2,1)S(1)} copy-done((bf16[1,128,128]{2,1,0:T(8,128)(2,1)S(1)}, bf16[1,128,128]{2,1,0:T(8,128)(2,1)}, u32[]{:S(2)}) %copy-start.11) | copy-done | bytes 32792
  4.2 0.7 %copy-done.13 = f32[1,32,128]{2,1,0:T(8,128)S(1)} copy-done((f32[1,32,128]{2,1,0:T(8,128)S(1)}, f32[1,32,128]{2,1,0:T(8,128)}, u32[]{:S(2)}) %copy-start.13) | copy-done | bytes 16408
  5.0 0.7 copy-done.15
  5.6 2.4 %shard_map.118 = (f32[16,136,128]{2,1,0:T(8,128)S(1)}, f32[16,128,128]{2,1,0:T(8,128)S(1)}, f32[16,8,128]{2,1,0:T(8,128)S(1)}) custom-call(s32[1,8]{1,0:T(1,128)S(1)} %copy-done.15, bf16[1,128,2048]{2,1,0:T(8,128)(2,1)S(1)} %copy-done, bf16[1,128,2048]{2,1,0:T(8,128)(2,1)S(1)} %copy-done.2, bf16[1,128,128]{2,1,0:T(8,128)(2,1)S(1)} %copy-done.9, ...), custom_call_target="tpu_custom_call" | custom-call | flops 134217728 | bytes 4194304 | tf_op jit(solution)/shard_map/pallas_call | solution.py:291
  8.0 3.3 %collective-permute-start = (f32[16,136,128]{2,1,0:T(8,128)S(1)}, f32[16,136,128]{2,1,0:T(8,128)S(1)}, u32[]{:S(2)}, u32[]{:S(2)}) collective-permute-start(f32[16,136,128]{2,1,0:T(8,128)S(1)} %get-tuple-element.20), channel_id=1, source_target_pairs={{0,1},{1,0},{2,3},{3,2},{4,5},{5,4},{6,7},{7,6},{8,9},{9,8},{10,11... | collective-permute-start | bytes 3342344 | tf_op jit(solution)/shard_map/ppermute | solution.py:307
  11.3 2.4 %collective-permute-done.recv_ref = f32[16,136,128]{2,1,0:T(8,128)S(1)} collective-permute-done((f32[16,136,128]{2,1,0:T(8,128)S(1)}, f32[16,136,128]{2,1,0:T(8,128)S(1)}, u32[]{:S(2)}, u32[]{:S(2)}) %collective-permute-start) | collective-permute-done | bytes 1114144 | tf_op jit(solution)/shard_map/ppermute | solution.py:307
  13.6 1.2 %shard_map.119._ = f32[16,136,128]{2,1,0:T(8,128)} custom-call(f32[16,136,128]{2,1,0:T(8,128)S(1)} %collective-permute-done.recv_ref, f32[16,128,128]{2,1,0:T(8,128)S(1)} %get-tuple-element.21.mine_ref, f32[16,8,128]{2,1,0:T(8,128)S(1)} %get-tuple-element.22.ext_ref), custom_call_target="tpu_custom_call" | custom-call | bytes 3145728 | tf_op jit(solution)/shard_map/pallas_call | solution.py:291
  14.8 0.0 copy-start.1
  14.8 0.0 copy-start.3
  14.8 0.0 copy-start.10
  14.9 0.0 copy-start.12
  14.9 0.0 copy-start.14
  14.9 0.0 copy-start.16
  14.9 5.2 %all-to-all-start = ((f32[16,136,128]{2,1,0:T(8,128)}), f32[16,136,128]{2,1,0:T(8,128)S(1)}, u32[]{:S(2)}, u32[]{:S(2)}) async-start(f32[16,136,128]{2,1,0:T(8,128)} %shard_map.119._), calls=%async_computation | async-start | bytes 2228224 | tf_op jit(solution)/shard_map/all_to_all | solution.py:329
  20.1 0.0 copy-done.1
  20.1 0.0 copy-done.3
  20.1 0.0 copy-done.10
  20.1 0.0 copy-done.12
  20.1 0.0 copy-done.14
  20.1 0.0 copy-done.16
  20.2 2.8 %shard_map.120 = (f32[128,2048]{1,0:T(8,128)S(1)}, f32[128,2048]{1,0:T(8,128)S(1)}, f32[128,128]{1,0:T(8,128)S(1)}, f32[128,128]{1,0:T(8,128)S(1)}) custom-call(f32[16,136,128]{2,1,0:T(8,128)} %shard_map.119._, s32[1,8]{1,0:T(1,128)S(1)} %copy-done.16, bf16[1,128,2048]{2,1,0:T(8,128)(2,1)S(1)} %copy-done.1, bf16[1,128,2048]{2,1,0:T(8,128)(2,1)S(1)} %copy-done.3, ...), custom_call_target="tpu_custom_call" | custom-call | flops 2684354560 | bytes 20971520 | tf_op jit(solution)/shard_map/pallas_call | solution.py:291
  22.9 0.0 copy-start.5
  23.0 1.0 %copy-done.5 = f32[128,2048]{1,0:T(8,128)} copy-done((f32[128,2048]{1,0:T(8,128)}, f32[128,2048]{1,0:T(8,128)S(1)}, u32[]{:S(2)}) %copy-start.5) | copy-done | bytes 1048600
  23.9 1.0 %copy-done.7 = f32[128,2048]{1,0:T(8,128)} copy-done((f32[128,2048]{1,0:T(8,128)}, f32[128,2048]{1,0:T(8,128)S(1)}, u32[]{:S(2)}) %copy-start.7) | copy-done | bytes 1048600
  24.9 11.5 %all-to-all-done.in_ref = f32[16,136,128]{2,1,0:T(8,128)S(1)} async-done(((f32[16,136,128]{2,1,0:T(8,128)}), f32[16,136,128]{2,1,0:T(8,128)S(1)}, u32[]{:S(2)}, u32[]{:S(2)}) %all-to-all-start) | async-done | bytes 1114144 | tf_op jit(solution)/shard_map/all_to_all | solution.py:329
  36.5 1.6 %shard_map.121 = (f32[8,128]{1,0:T(8,128)S(1)}, f32[16,128,128]{2,1,0:T(8,128)S(1)}) custom-call(f32[128,128]{1,0:T(8,128)S(1)} %get-tuple-element.23._.iraw_ref, f32[16,136,128]{2,1,0:T(8,128)S(1)} %all-to-all-done.in_ref), custom_call_target="tpu_custom_call" | custom-call | bytes 2097152 | tf_op jit(solution)/shard_map/pallas_call | solution.py:291
  38.1 0.0 copy-start.4
  38.1 1.0 %copy-done.4 = f32[16,128,128]{2,1,0:T(8,128)} copy-done((f32[16,128,128]{2,1,0:T(8,128)}, f32[16,128,128]{2,1,0:T(8,128)S(1)}, u32[]{:S(2)}) %copy-start.4) | copy-done | bytes 1048600
  39.1 4.6 %all-to-all-start.1 = ((f32[16,128,128]{2,1,0:T(8,128)}), f32[16,128,128]{2,1,0:T(8,128)S(1)}, u32[]{:S(2)}, u32[]{:S(2)}) async-start(f32[16,128,128]{2,1,0:T(8,128)} %copy-done.4), calls=%async_computation.1 | async-start | bytes 2097152 | tf_op jit(solution)/shard_map/all_to_all | solution.py:347
  43.7 1.7 %collective-permute-start.1 = (f32[8,128]{1,0:T(8,128)S(1)}, f32[8,128]{1,0:T(8,128)S(1)}, u32[]{:S(2)}, u32[]{:S(2)}) collective-permute-start(f32[8,128]{1,0:T(8,128)S(1)} %get-tuple-element.25), channel_id=1, source_target_pairs={{0,32},{32,0},{64,96},{96,64},{128,160},{160,128},{192,224},{224,1... | collective-permute-start | bytes 12296 | tf_op jit(solution)/shard_map/ppermute | solution.py:349
  45.4 1.0 %collective-permute-done.1 = f32[8,128]{1,0:T(8,128)S(1)} collective-permute-done((f32[8,128]{1,0:T(8,128)S(1)}, f32[8,128]{1,0:T(8,128)S(1)}, u32[]{:S(2)}, u32[]{:S(2)}) %collective-permute-start.1) | collective-permute-done | bytes 4128 | tf_op jit(solution)/shard_map/ppermute | solution.py:349
  46.4 3.0 %collective-permute-start.2 = (f32[8,128]{1,0:T(8,128)S(1)}, f32[8,128]{1,0:T(8,128)S(1)}, u32[]{:S(2)}, u32[]{:S(2)}) collective-permute-start(f32[8,128]{1,0:T(8,128)S(1)} %add.9), channel_id=1, source_target_pairs={{0,64},{32,96},{64,0},{96,32},{128,192},{160,224},{192,128},{224,1... | collective-permute-start | bytes 12296 | tf_op jit(solution)/shard_map/ppermute | solution.py:349
  49.4 1.3 %collective-permute-done.2 = f32[8,128]{1,0:T(8,128)S(1)} collective-permute-done((f32[8,128]{1,0:T(8,128)S(1)}, f32[8,128]{1,0:T(8,128)S(1)}, u32[]{:S(2)}, u32[]{:S(2)}) %collective-permute-start.2) | collective-permute-done | bytes 4128 | tf_op jit(solution)/shard_map/ppermute | solution.py:349
  50.7 5.8 %collective-permute-start.3 = (f32[8,128]{1,0:T(8,128)S(1)}, f32[8,128]{1,0:T(8,128)S(1)}, u32[]{:S(2)}, u32[]{:S(2)}) collective-permute-start(f32[8,128]{1,0:T(8,128)S(1)} %add.10), channel_id=1, source_target_pairs={{0,128},{32,160},{64,192},{96,224},{128,0},{160,32},{192,64},{224,... | collective-permute-start | bytes 12296 | tf_op jit(solution)/shard_map/ppermute | solution.py:349
  56.5 1.0 %collective-permute-done.3 = f32[8,128]{1,0:T(8,128)S(1)} collective-permute-done((f32[8,128]{1,0:T(8,128)S(1)}, f32[8,128]{1,0:T(8,128)S(1)}, u32[]{:S(2)}, u32[]{:S(2)}) %collective-permute-start.3) | collective-permute-done | bytes 4128 | tf_op jit(solution)/shard_map/ppermute | solution.py:349
  57.5 1.0 %all-to-all-done.1.x_ref = f32[16,128,128]{2,1,0:T(8,128)S(1)} async-done(((f32[16,128,128]{2,1,0:T(8,128)}), f32[16,128,128]{2,1,0:T(8,128)S(1)}, u32[]{:S(2)}, u32[]{:S(2)}) %all-to-all-start.1) | async-done | bytes 1048608 | tf_op jit(solution)/shard_map/all_to_all | solution.py:347
  58.5 0.1 shard_map.122
  58.6 4.6 %collective-permute-start.4 = (f32[16,128,128]{2,1,0:T(8,128)S(1)}, f32[16,128,128]{2,1,0:T(8,128)S(1)}, u32[]{:S(2)}, u32[]{:S(2)}) collective-permute-start(f32[16,128,128]{2,1,0:T(8,128)S(1)} %shard_map.122), channel_id=1, source_target_pairs={{0,1},{1,0},{2,3},{3,2},{4,5},{5,4},{6,7},{7,6},{8,9},{9,8},{10,11... | collective-permute-start | bytes 3145736 | tf_op jit(solution)/shard_map/ppermute | solution.py:307
  63.1 0.5 multiply_bitcast_fusion
  63.7 1.8 %collective-permute-done.4.y_ref = f32[16,128,128]{2,1,0:T(8,128)S(1)} collective-permute-done((f32[16,128,128]{2,1,0:T(8,128)S(1)}, f32[16,128,128]{2,1,0:T(8,128)S(1)}, u32[]{:S(2)}, u32[]{:S(2)}) %collective-permute-start.4) | collective-permute-done | bytes 1048608 | tf_op jit(solution)/shard_map/ppermute | solution.py:307
  65.4 0.0 copy-done.17
  65.4 0.0 copy-done.6
  65.4 0.0 copy-done.8
  65.4 4.9 %shard_map.123 = (bf16[1,128,2048]{2,1,0:T(8,128)(2,1)}, bf16[1,128,2048]{2,1,0:T(8,128)(2,1)}, f32[1,128,128]{2,1,0:T(8,128)}, f32[1,128,128]{2,1,0:T(8,128)}, f32[1,32,128]{2,1,0:T(8,128)}) custom-call(s32[1,8]{1,0:T(1,128)S(1)} %copy-done.16, f32[32]{0:T(128)S(1)} %copy-done.17, bf16[1,128,2048]{2,1,0:T(8,128)(2,1)S(1)} %copy-done.1, ...), custom_call_target="tpu_custom_call" | custom-call | flops 268435456 | bytes 8388608 | tf_op jit(solution)/shard_map/pallas_call | solution.py:291
  (12 shorter events, 0.0 us)
Async XLA Ops:
  0.6 1.0 %copy-start = (bf16[1,128,2048]{2,1,0:T(8,128)(2,1)S(1)}, bf16[1,128,2048]{2,1,0:T(8,128)(2,1)}, u32[]{:S(2)}) copy-start(bf16[1,128,2048]{2,1,0:T(8,128)(2,1)} %v_ref.5) | copy-start | bytes 1572868
  1.7 1.0 %copy-start.2 = (bf16[1,128,2048]{2,1,0:T(8,128)(2,1)S(1)}, bf16[1,128,2048]{2,1,0:T(8,128)(2,1)}, u32[]{:S(2)}) copy-start(bf16[1,128,2048]{2,1,0:T(8,128)(2,1)} %g_ref.5) | copy-start | bytes 1572868
  2.7 0.8 %copy-start.9 = (bf16[1,128,128]{2,1,0:T(8,128)(2,1)S(1)}, bf16[1,128,128]{2,1,0:T(8,128)(2,1)}, u32[]{:S(2)}) copy-start(bf16[1,128,128]{2,1,0:T(8,128)(2,1)} %b_ref.5) | copy-start | bytes 98308
  3.5 0.8 %copy-start.11 = (bf16[1,128,128]{2,1,0:T(8,128)(2,1)S(1)}, bf16[1,128,128]{2,1,0:T(8,128)(2,1)}, u32[]{:S(2)}) copy-start(bf16[1,128,128]{2,1,0:T(8,128)(2,1)} %c_ref.5) | copy-start | bytes 98308
  4.2 0.7 %copy-start.13 = (f32[1,32,128]{2,1,0:T(8,128)S(1)}, f32[1,32,128]{2,1,0:T(8,128)}, u32[]{:S(2)}) copy-start(f32[1,32,128]{2,1,0:T(8,128)} %ld_ref.5) | copy-start | bytes 49156
  5.0 0.7 copy-start.15
  8.0 5.7 %collective-permute-start = (f32[16,136,128]{2,1,0:T(8,128)S(1)}, f32[16,136,128]{2,1,0:T(8,128)S(1)}, u32[]{:S(2)}, u32[]{:S(2)}) collective-permute-start(f32[16,136,128]{2,1,0:T(8,128)S(1)} %get-tuple-element.20), channel_id=1, source_target_pairs={{0,1},{1,0},{2,3},{3,2},{4,5},{5,4},{6,7},{7,6},{8,9},{9,8},{10,11... | collective-permute-start | bytes 3342344 | tf_op jit(solution)/shard_map/ppermute | solution.py:307
  14.8 5.3 %copy-start.1 = (bf16[1,128,2048]{2,1,0:T(8,128)(2,1)S(1)}, bf16[1,128,2048]{2,1,0:T(8,128)(2,1)}, u32[]{:S(2)}) copy-start(bf16[1,128,2048]{2,1,0:T(8,128)(2,1)} %v_ref.5) | copy-start | bytes 1572868
  14.8 5.3 %copy-start.3 = (bf16[1,128,2048]{2,1,0:T(8,128)(2,1)S(1)}, bf16[1,128,2048]{2,1,0:T(8,128)(2,1)}, u32[]{:S(2)}) copy-start(bf16[1,128,2048]{2,1,0:T(8,128)(2,1)} %g_ref.5) | copy-start | bytes 1572868
  14.8 5.3 %copy-start.10 = (bf16[1,128,128]{2,1,0:T(8,128)(2,1)S(1)}, bf16[1,128,128]{2,1,0:T(8,128)(2,1)}, u32[]{:S(2)}) copy-start(bf16[1,128,128]{2,1,0:T(8,128)(2,1)} %b_ref.5) | copy-start | bytes 98308
  14.9 5.3 %copy-start.12 = (bf16[1,128,128]{2,1,0:T(8,128)(2,1)S(1)}, bf16[1,128,128]{2,1,0:T(8,128)(2,1)}, u32[]{:S(2)}) copy-start(bf16[1,128,128]{2,1,0:T(8,128)(2,1)} %c_ref.5) | copy-start | bytes 98308
  14.9 5.3 %copy-start.14 = (f32[1,32,128]{2,1,0:T(8,128)S(1)}, f32[1,32,128]{2,1,0:T(8,128)}, u32[]{:S(2)}) copy-start(f32[1,32,128]{2,1,0:T(8,128)} %ld_ref.5) | copy-start | bytes 49156
  14.9 5.3 %copy-start.16 = (s32[1,8]{1,0:T(1,128)S(1)}, s32[1,8]{1,0:T(1,128)}, u32[]{:S(2)}) copy-start(s32[1,8]{1,0:T(1,128)} %len_ref.5) | copy-start | bytes 100
  14.9 21.6 %all-to-all-start = ((f32[16,136,128]{2,1,0:T(8,128)}), f32[16,136,128]{2,1,0:T(8,128)S(1)}, u32[]{:S(2)}, u32[]{:S(2)}) async-start(f32[16,136,128]{2,1,0:T(8,128)} %shard_map.119._), calls=%async_computation | async-start | bytes 2228224 | tf_op jit(solution)/shard_map/all_to_all | solution.py:329
  22.9 1.0 %copy-start.5 = (f32[128,2048]{1,0:T(8,128)}, f32[128,2048]{1,0:T(8,128)S(1)}, u32[]{:S(2)}) copy-start(f32[128,2048]{1,0:T(8,128)S(1)} %get-tuple-element.26.within_ref) | copy-start | bytes 3145732
  23.9 1.0 %copy-start.7 = (f32[128,2048]{1,0:T(8,128)}, f32[128,2048]{1,0:T(8,128)S(1)}, u32[]{:S(2)}) copy-start(f32[128,2048]{1,0:T(8,128)S(1)} %get-tuple-element.27.back_ref) | copy-start | bytes 3145732
  38.1 1.0 %copy-start.4 = (f32[16,128,128]{2,1,0:T(8,128)}, f32[16,128,128]{2,1,0:T(8,128)S(1)}, u32[]{:S(2)}) copy-start(f32[16,128,128]{2,1,0:T(8,128)S(1)} %get-tuple-element.24) | copy-start | bytes 3145732
  39.1 19.4 %all-to-all-start.1 = ((f32[16,128,128]{2,1,0:T(8,128)}), f32[16,128,128]{2,1,0:T(8,128)S(1)}, u32[]{:S(2)}, u32[]{:S(2)}) async-start(f32[16,128,128]{2,1,0:T(8,128)} %copy-done.4), calls=%async_computation.1 | async-start | bytes 2097152 | tf_op jit(solution)/shard_map/all_to_all | solution.py:347
  43.7 2.7 %collective-permute-start.1 = (f32[8,128]{1,0:T(8,128)S(1)}, f32[8,128]{1,0:T(8,128)S(1)}, u32[]{:S(2)}, u32[]{:S(2)}) collective-permute-start(f32[8,128]{1,0:T(8,128)S(1)} %get-tuple-element.25), channel_id=1, source_target_pairs={{0,32},{32,0},{64,96},{96,64},{128,160},{160,128},{192,224},{224,1... | collective-permute-start | bytes 12296 | tf_op jit(solution)/shard_map/ppermute | solution.py:349
  46.4 4.3 %collective-permute-start.2 = (f32[8,128]{1,0:T(8,128)S(1)}, f32[8,128]{1,0:T(8,128)S(1)}, u32[]{:S(2)}, u32[]{:S(2)}) collective-permute-start(f32[8,128]{1,0:T(8,128)S(1)} %add.9), channel_id=1, source_target_pairs={{0,64},{32,96},{64,0},{96,32},{128,192},{160,224},{192,128},{224,1... | collective-permute-start | bytes 12296 | tf_op jit(solution)/shard_map/ppermute | solution.py:349
  50.7 6.8 %collective-permute-start.3 = (f32[8,128]{1,0:T(8,128)S(1)}, f32[8,128]{1,0:T(8,128)S(1)}, u32[]{:S(2)}, u32[]{:S(2)}) collective-permute-start(f32[8,128]{1,0:T(8,128)S(1)} %add.10), channel_id=1, source_target_pairs={{0,128},{32,160},{64,192},{96,224},{128,0},{160,32},{192,64},{224,... | collective-permute-start | bytes 12296 | tf_op jit(solution)/shard_map/ppermute | solution.py:349
  57.5 7.9 %copy-start.17 = (f32[32]{0:T(128)S(1)}, f32[32]{0:T(128)}, u32[]{:S(2)}) copy-start(f32[32]{0:T(128)} %skip_ref.1) | copy-start | bytes 388
  58.5 7.0 %copy-start.6 = (f32[128,2048]{1,0:T(8,128)S(1)}, f32[128,2048]{1,0:T(8,128)}, u32[]{:S(2)}) copy-start(f32[128,2048]{1,0:T(8,128)} %copy-done.5) | copy-start | bytes 3145732
  58.5 7.0 %copy-start.8 = (f32[128,2048]{1,0:T(8,128)S(1)}, f32[128,2048]{1,0:T(8,128)}, u32[]{:S(2)}) copy-start(f32[128,2048]{1,0:T(8,128)} %copy-done.7) | copy-start | bytes 3145732
  58.6 6.8 %collective-permute-start.4 = (f32[16,128,128]{2,1,0:T(8,128)S(1)}, f32[16,128,128]{2,1,0:T(8,128)S(1)}, u32[]{:S(2)}, u32[]{:S(2)}) collective-permute-start(f32[16,128,128]{2,1,0:T(8,128)S(1)} %shard_map.122), channel_id=1, source_target_pairs={{0,1},{1,0},{2,3},{3,2},{4,5},{5,4},{6,7},{7,6},{8,9},{9,8},{10,11... | collective-permute-start | bytes 3145736 | tf_op jit(solution)/shard_map/ppermute | solution.py:307

commit v3 on v2

v3 whole, which is shorter than its diff:
```python
import functools

import jax
import jax.numpy as jnp
from jax import lax
from jax.experimental import pallas as pl
from jax.experimental.pallas import tpu as pltpu
from jax.sharding import Mesh
from jax.sharding import PartitionSpec as P

SEQ = ("seq_0", "seq_1", "seq_2")
CHIPS = ("seq_0", "seq_1")
CORE = "seq_2"
F32 = jnp.float32
BF16 = jnp.bfloat16
T = 128
N = 128
PAIRS = 16
HEADS = 32
DOCS = 8
EXT = 8
PARTS = 4
PART = 512
FAR = -1e30
VMEM = pl.BlockSpec(memory_space=pltpu.VMEM)
SMEM = pl.BlockSpec(memory_space=pltpu.SMEM)
ANY = pl.BlockSpec(memory_space=pl.ANY)
HBM = pl.BlockSpec(memory_space=pltpu.HBM)

NN = (((1,), (0,)), ((), ()))
NT = (((1,), (1,)), ((), ()))
TN = (((0,), (0,)), ((), ()))


def dot(a, b, dims=NN, precision=None):
    return lax.dot_general(a, b, dims, precision=precision, preferred_element_type=F32)


def exact(a, b, dims=NN):
    return dot(a, b, dims, lax.Precision.HIGHEST)


def iota(shape, dim):
    return lax.broadcasted_iota(jnp.int32, shape, dim)


def block_base():
    return lax.axis_index(SEQ) * T


def doc_starts(len_ref):
    starts, at = [], jnp.int32(0)
    for d in range(DOCS):
        starts.append(at)
        at = at + len_ref[0, d]
    return starts


def segments(starts, base, offset):
    count = jnp.zeros(offset.shape, jnp.int32)
    for s in starts:
        local = jnp.where(s >= base, s - base, jnp.int32(1 << 20))
        count = count + (offset >= local).astype(jnp.int32)
    return count


def end_count(starts, base):
    count = jnp.int32(0)
    for s in starts:
        count = count + jnp.logical_and(s >= base, s < base + T).astype(jnp.int32)
    return count


def lower_triangle():
    return (iota((T, T), 1) <= iota((T, T), 0)).astype(F32)


def weights(ld, starts, base):
    log_cum = exact(lower_triangle(), ld, NT)
    seg = segments(starts, base, iota((T, HEADS), 0))
    last = end_count(starts, base)
    log_end = log_cum[T - 1 :, :]
    w_end = jnp.where(seg == last, jnp.exp(log_end - log_cum), 0.0)
    w_start = jnp.where(seg == 0, jnp.exp(log_cum), 0.0)
    gain = jnp.exp(log_end) * (last == 0).astype(F32)
    return w_end, w_start, gain


def spread(w, j, low):
    return jnp.where(low, w[:, 2 * j : 2 * j + 1], w[:, 2 * j + 1 : 2 * j + 2])


def cols(j):
    return slice(j * 128, (j + 1) * 128)


def heads_of(rows):
    lane = iota((PAIRS, 128), 1)
    row = iota((PAIRS, 128), 0)
    even = jnp.sum(jnp.where(lane < 64, rows, 0.0), axis=1, keepdims=True)
    odd = jnp.sum(jnp.where(lane < 64, 0.0, rows), axis=1, keepdims=True)
    placed = jnp.where(lane == 2 * row, even, jnp.where(lane == 2 * row + 1, odd, 0.0))
    return jnp.sum(placed, axis=0, keepdims=True)


def is_first():
    return lax.axis_index(CORE) == 0


def prep_kernel(
    len_hbm, v_hbm, g_hbm, b_hbm, c_hbm, ld_hbm,
    roles_ref, rows_ref, w_ref, gain_ref, send_ref,
    len_ref, ld_ref, small_sems, v_sems, g_sems,
):
    first = is_first()
    v_slot = jnp.where(first, 1, 0)
    g_slot = 1 - v_slot
    small = [
        pltpu.make_async_copy(len_hbm, len_ref, small_sems.at[0]),
        pltpu.make_async_copy(ld_hbm.at[0], ld_ref, small_sems.at[1]),
        pltpu.make_async_copy(b_hbm.at[0], rows_ref.at[v_slot], small_sems.at[2]),
        pltpu.make_async_copy(c_hbm.at[0], rows_ref.at[g_slot], small_sems.at[3]),
    ]
    for copy in small:
        copy.start()
    wide = []
    for k in range(PARTS):
        part = slice(k * PART, (k + 1) * PART)
        vc = pltpu.make_async_copy(
            v_hbm.at[0, :, part], roles_ref.at[v_slot, :, part], v_sems.at[k]
        )
        gc = pltpu.make_async_copy(
            g_hbm.at[0, :, part], roles_ref.at[g_slot, :, part], g_sems.at[k]
        )
        vc.start()
        gc.start()
        wide.append((vc, gc))
    for copy in small:
        copy.wait()
    starts = doc_starts(len_ref)
    w_end, w_start, gain = weights(ld_ref[...], starts, block_base())
    w = jnp.where(first, w_start, w_end)
    w_ref[0] = w
    w_ref[1] = jnp.where(first, w_end, w_start)
    p_t = rows_ref[0].T
    low = iota((T, 128), 1) < 64
    sub = iota((EXT, 128), 0)
    for j in range(PAIRS):
        if j % (PAIRS // PARTS) == 0:
            for copy in wide[j // (PAIRS // PARTS)]:
                copy.wait()
        weighted = (roles_ref[0, :, cols(j)].astype(F32) * spread(w, j, low)).astype(BF16)
        send_ref[j, :N] = dot(p_t, weighted)
        gain_row = spread(gain, j, low[:1])
        gain_ref[j : j + 1] = gain_row
        send_ref[j, N:] = jnp.where(sub == 0, gain_row, 0.0)


def own_kernel(
    _, len_ref, skip_gain_ref, roles_ref, rows_ref, w_ref,
    mine_ref, keep_ref, gains_ref, skip_ref,
):
    low = iota((T, 128), 1) < 64
    p_t = rows_ref[1].T
    w = w_ref[1]
    skips = []
    for j in range(PAIRS):
        mine = roles_ref[1, :, cols(j)].astype(F32)
        other = roles_ref[0, :, cols(j)].astype(F32)
        mine_ref[j] = dot(p_t, (mine * spread(w, j, low)).astype(BF16))
        skips.append(jnp.sum(mine * other, axis=0, keepdims=True))
        gains_ref[j : j + 1] = jnp.where(
            low[:1], skip_gain_ref[2 * j], skip_gain_ref[2 * j + 1]
        )
    skip = heads_of(jnp.concatenate(skips, axis=0))
    skip_ref[...] = jnp.broadcast_to(skip, (EXT, 128))
    base = block_base()
    starts = doc_starts(len_ref)
    offset = iota((EXT, T), 1)
    keep = jnp.ones((EXT, T), F32)
    for s in starts:
        keep = jnp.where(offset + base == s, 0.0, keep)
    keep_ref[...] = keep


def put(buffer, out_ref, sems, j):
    return pltpu.make_async_copy(buffer.at[j], out_ref.at[j], sems.at[j])


def combine_kernel(recv_ref, mine_ref, gain_ref, out_ref, buffer, sems):
    copies = []
    for j in range(PAIRS):
        theirs = recv_ref[j, N:]
        buffer[j, :N] = theirs[:1] * mine_ref[j] + recv_ref[j, :N]
        buffer[j, N:] = theirs * gain_ref[j : j + 1]
        copies.append(put(buffer, out_ref, sems, j))
        copies[-1].start()
    for copy in copies:
        copy.wait()


def scan_kernel(in_ref, skip_ref, out_ref, buffer, sems):
    first = is_first()
    running = jnp.zeros((N, 128), F32)
    copies = []
    for i in range(PAIRS):
        at = jnp.where(first, i, PAIRS - 1 - i)
        buffer[i, :N] = running
        buffer[i, N:] = skip_ref[...]
        copies.append(pltpu.make_async_copy(buffer.at[i], out_ref.at[at], sems.at[i]))
        copies[-1].start()
        if i < PAIRS - 1:
            running = in_ref[at, N : N + 1] * running + in_ref[at, :N]
    for copy in copies:
        copy.wait()


def inside_kernel(_, len_ref, roles_ref, rows_ref, ld_ref, part_ref, raw_ref):
    first = is_first()
    v_slot = jnp.where(first, 1, 0)
    g_slot = 1 - v_slot
    base = block_base()
    starts = doc_starts(len_ref)
    ld = ld_ref[0]
    tri = lower_triangle()
    cum_t = exact(tri, ld, NT)
    cum_h = exact(ld, tri, NT)
    t_at = iota((T, T), 0)
    s_at = iota((T, T), 1)
    same = segments(starts, base, t_at) == segments(starts, base, s_at)
    bias = jnp.where(jnp.logical_and(s_at <= t_at, same), 0.0, FAR)
    b = rows_ref[v_slot]
    c = rows_ref[g_slot]
    scores = dot(c, b, NT)
    low = iota((T, 128), 1) < 64
    zero = jnp.zeros((T, 128), BF16)
    grad_scores = jnp.zeros((T, T), F32)
    for j in range(PAIRS):
        v = roles_ref[v_slot, :, cols(j)]
        g = roles_ref[g_slot, :, cols(j)]
        v_two = jnp.concatenate([jnp.where(low, v, zero), jnp.where(low, zero, v)], axis=0)
        g_two = jnp.concatenate([jnp.where(low, g, zero), jnp.where(low, zero, g)], axis=0)
        grad_mix = dot(g, v_two, NT)
        mixes = []
        for k in range(2):
            h = 2 * j + k
            decay = jnp.exp(cum_t[:, h : h + 1] - cum_h[h : h + 1, :] + bias)
            mixes.append((scores * decay).astype(BF16))
            grad_scores = grad_scores + grad_mix[:, k * T : (k + 1) * T] * decay
        part_ref[g_slot, :, cols(j)] = dot(jnp.concatenate(mixes, axis=1), v_two)
        part_ref[v_slot, :, cols(j)] = dot(jnp.concatenate(mixes, axis=0), g_two, TN)
    half = grad_scores.astype(BF16)
    raw_ref[g_slot] = dot(half, b)
    raw_ref[v_slot] = dot(half, c, TN)


def pass_on_kernel(scale, _, x_ref, mine_ref, gain_ref, out_ref, skip_ref):
    skip = x_ref[0, N:]
    for j in range(PAIRS):
        out_ref[j] = gain_ref[j : j + 1] * x_ref[j, :N] + mine_ref[j]
        if j > 0:
            skip = skip + x_ref[j, N:]
    skip_ref[...] = skip * scale


def finish_role(slot, j, low, x, roles_ref, rows, w, part_ref, skip_gains):
    half = x.astype(BF16)
    own = roles_ref[slot, :, cols(j)].astype(F32)
    skipped = roles_ref[1 - slot, :, cols(j)].astype(F32)
    wide = spread(w, j, low)
    tail = wide * dot(rows, half)
    out = part_ref[slot, :, cols(j)] + tail
    result = (out + skip_gains[j : j + 1] * skipped).astype(BF16)
    change = own * out
    hi = change.astype(BF16)
    lo = (change - hi.astype(F32)).astype(BF16)
    lane = iota((128, 128), 0)
    head = iota((128, 128), 1)
    pick = (head == 2 * j + jnp.where(lane < 64, 0, 1)).astype(BF16)
    end = jnp.sum(own * tail, axis=0, keepdims=True)
    return result, dot(hi, pick) + dot(lo, pick), end, dot((own * wide).astype(BF16), half, NT)


def near_kernel(
    _, x_ref, roles_ref, rows_ref, w_ref, part_ref, raw_ref, gains_ref,
    out_ref, total_ref, change_ref, end_ref,
):
    low = iota((T, 128), 1) < 64
    rows = rows_ref[0]
    w = w_ref[0]
    skip_gains = gains_ref[...]
    total = raw_ref[0]
    changes = jnp.zeros((T, 128), F32)
    for j in range(PAIRS):
        result, change, end, more = finish_role(
            0, j, low, x_ref[j, :N], roles_ref, rows, w, part_ref, skip_gains
        )
        out_ref[:, cols(j)] = result
        changes = changes + change
        total = total + more
        end_ref[j : j + 1] = end
    total_ref[...] = total
    change_ref[...] = changes


def far_kernel(
    scales, y_ref, x_ref, roles_ref, rows_ref, w_ref, part_ref, raw_ref, gains_ref,
    gain_ref, keep_ref, near_ref, near_total_ref, near_change_ref, near_end_ref,
    igrad_ref, ograd_ref, dgrad_ref, mixed_hbm, vgrad_hbm,
    mixed_ref, vgrad_ref, sems,
):
    in_scale, out_scale, decay_scale = scales
    first = is_first()
    low = iota((T, 128), 1) < 64
    rows = rows_ref[1]
    w = w_ref[1]
    skip_gains = gains_ref[...]
    total = raw_ref[1]
    changes = near_change_ref[...]
    ends = []
    copies = []
    for j in range(PAIRS):
        y = y_ref[j]
        result, change, end, more = finish_role(
            1, j, low, y, roles_ref, rows, w, part_ref, skip_gains
        )
        near = near_ref[:, cols(j)]
        mixed_ref[:, cols(j)] = jnp.where(first, near, result)
        vgrad_ref[:, cols(j)] = jnp.where(first, result, near)
        if (j + 1) % (PAIRS // PARTS) == 0:
            k = j // (PAIRS // PARTS)
            part = slice(k * PART, (k + 1) * PART)
            for n, (src, dst) in enumerate(((mixed_ref, mixed_hbm), (vgrad_ref, vgrad_hbm))):
                copies.append(
                    pltpu.make_async_copy(src.at[:, part], dst.at[0, :, part], sems.at[n, k])
                )
                copies[-1].start()
        changes = changes - change
        total = total + more
        meet = jnp.sum(x_ref[j, :N] * y, axis=0, keepdims=True)
        end = jnp.where(first, end, near_end_ref[j : j + 1])
        ends.append(end + gain_ref[j : j + 1] * meet)
    near_total = near_total_ref[...]
    igrad_ref[0] = jnp.where(first, total, near_total) * in_scale
    ograd_ref[0] = jnp.where(first, near_total, total) * out_scale
    changes = jnp.where(first, changes, -changes)
    at_end = iota((T, 128), 0) == T - 1
    changes = changes + jnp.where(at_end, heads_of(jnp.concatenate(ends, axis=0)), 0.0)
    summed = exact(changes, lower_triangle(), TN)[:HEADS]
    dgrad_ref[0] = summed * keep_ref[:1] * decay_scale
    for copy in copies:
        copy.wait()


def call(kernel, outs, *args, after=(), spaces=(), out_spaces=(), scratch=(), flops=0, moved=0):
    in_specs = [ANY] * len(after) + list(spaces)
    in_specs += [VMEM] * (len(args) + len(after) - len(in_specs))
    out_specs = [VMEM] * (len(outs) - len(out_spaces)) + list(out_spaces)
    return pl.pallas_call(
        kernel,
        out_shape=tuple(outs),
        in_specs=in_specs,
        out_specs=tuple(out_specs),
        scratch_shapes=list(scratch),
        compiler_params=pltpu.CompilerParams(vmem_limit_bytes=16 << 20),
        cost_estimate=pl.CostEstimate(flops=flops, bytes_accessed=moved, transcendentals=0),
    )(*after, *args)


def f32(*shape):
    return jax.ShapeDtypeStruct(shape, F32)


def bf16(*shape):
    return jax.ShapeDtypeStruct(shape, BF16)


def swap_cores(x):
    return lax.ppermute(x, CORE, [(0, 1), (1, 0)])


def exchange(x):
    return lax.all_to_all(x, CHIPS, split_axis=0, concat_axis=0, tiled=True)


def body(values_in, input_proj, output_proj, log_decay, doc_lengths, skip_gain, out_cotangent):
    token_count = lax.axis_size(SEQ) * T
    seq_count = lax.axis_size("dp")
    inner = values_in.shape[2]
    head_dim = inner // HEADS
    dma = pltpu.SemaphoreType.DMA
    inputs = (doc_lengths, values_in, out_cotangent, input_proj, output_proj, log_decay)
    roles, rows, w, gain, send = call(
        prep_kernel,
        (
            bf16(2, T, inner), bf16(2, T, N), f32(2, T, HEADS), f32(PAIRS, 128),
            f32(PAIRS, N + EXT, 128),
        ),
        *(pltpu.with_memory_space_constraint(a, pltpu.HBM) for a in inputs),
        spaces=[HBM] * 6,
        scratch=[
            pltpu.SMEM((1, DOCS), jnp.int32), pltpu.VMEM((HEADS, T), F32),
            dma((4,)), dma((PARTS,)), dma((PARTS,)),
        ],
        moved=4 << 20,
    )
    recv = swap_cores(send)
    mine, keep, gains, skip = call(
        own_kernel,
        (f32(PAIRS, N, 128), f32(EXT, T), f32(PAIRS, 128), f32(EXT, 128)),
        doc_lengths, skip_gain, roles, rows, w,
        after=(send,),
        spaces=[SMEM] * 2,
        moved=4 << 20,
    )
    (chip,) = call(
        combine_kernel,
        (f32(PAIRS, N + EXT, 128),),
        recv, mine, gain,
        out_spaces=[HBM],
        scratch=[pltpu.VMEM((PAIRS, N + EXT, 128), F32), dma((PAIRS,))],
        moved=3 << 20,
    )
    gathered = exchange(chip)
    skip, _ = lax.optimization_barrier((skip, chip))
    skip = skip + swap_cores(skip)
    for step in (1, 2, 4):
        skip = skip + lax.ppermute(skip, "dp", [(i, i ^ step) for i in range(8)])
    (prefix,) = call(
        scan_kernel,
        (f32(PAIRS, N + EXT, 128),),
        gathered, skip,
        out_spaces=[HBM],
        scratch=[pltpu.VMEM((PAIRS, N + EXT, 128), F32), dma((PAIRS,))],
        moved=2 << 20,
    )
    x = exchange(prefix)
    part, raw = call(
        inside_kernel,
        (f32(2, T, inner), f32(2, T, N)),
        doc_lengths, roles, rows, log_decay,
        after=(prefix,),
        spaces=[SMEM],
        flops=40 * 2 * T * N * inner,
        moved=20 << 20,
    )
    passed, skip_total = call(
        functools.partial(pass_on_kernel, 1.0 / (seq_count * token_count * head_dim) ** 0.5),
        (f32(PAIRS, N, 128), f32(EXT, 128)),
        x, mine, gain,
        after=(raw,),
        moved=3 << 20,
    )
    y = swap_cores(passed)
    near, near_total, near_change, near_end = call(
        near_kernel,
        (bf16(T, inner), f32(T, N), f32(T, 128), f32(PAIRS, 128)),
        x, roles, rows, w, part, raw, gains,
        after=(passed,),
        moved=8 << 20,
    )
    scales = (
        1.0 / inner**0.5,
        (N / (inner * token_count)) ** 0.5,
        1.0 / (head_dim * token_count) ** 0.5,
    )
    input_grad, output_grad, decay_grad, mixed, values_grad = call(
        functools.partial(far_kernel, scales),
        (f32(1, T, N), f32(1, T, N), f32(1, HEADS, T), bf16(1, T, inner), bf16(1, T, inner)),
        y, x, roles, rows, w, part, raw, gains, gain, keep,
        near, near_total, near_change, near_end,
        out_spaces=[HBM] * 2,
        scratch=[pltpu.VMEM((T, inner), BF16), pltpu.VMEM((T, inner), BF16), dma((2, PARTS))],
        moved=8 << 20,
    )
    return mixed, values_grad, input_grad, output_grad, decay_grad, skip_total[1, :HEADS]


def solution(mesh):
    finer = Mesh(mesh.devices.reshape(mesh.shape["dp"], 4, 4, 2), ("dp",) + SEQ)
    placed = (
        P("dp", SEQ, None),
        P("dp", SEQ, None),
        P("dp", SEQ, None),
        P("dp", None, SEQ),
        P("dp", None),
        P(),
        P("dp", SEQ, None),
    )
    return jax.shard_map(
        body,
        mesh=finer,
        in_specs=placed,
        out_specs=(
            P("dp", SEQ, None),
            P("dp", SEQ, None),
            P("dp", SEQ, None),
            P("dp", SEQ, None),
            P("dp", None, SEQ),
            P(),
        ),
        check_vma=False,
    )
```

time: 70.9 us -> 65.4 us (0.922)
  local copies, waits for them, and re-layouts: 7.95 us -> 3.23 us
  waiting for transfers between devices: 19.9 us -> 15.2 us
  Pallas kernels: 13 us -> 15.4 us
  starting transfers between devices: 28.1 us -> 30.5 us
    unnamed x36 -> x16, local copies, waits for them, and re-layouts: 7.95 us -> 2.71 us
    all_to_all x2, waiting for transfers between devices: 12.5 us -> 9.56 us  [exchange(): return lax.all_to_all(x, CHIPS, split_axis=0, concat_axis=0, tiled=True)]
    pallas_call x6 -> x8, Pallas kernels: 13 us -> 15.4 us  [call(): pl.pallas_call(kernel, out_shape=tuple(outs), in_specs=in_specs, out_spec...]
    ppermute x2 -> x3, waiting for transfers between devices: 4.15 us -> 1.73 us  [swap_cores(): return lax.ppermute(x, CORE, [(0, 1), (1, 0)])]
    all_to_all x2, starting transfers between devices: 9.77 us -> 11.5 us  [exchange(): return lax.all_to_all(x, CHIPS, split_axis=0, concat_axis=0, tiled=True)]
    ppermute x2 -> x3, starting transfers between devices: 7.84 us -> 8.29 us  [swap_cores(): return lax.ppermute(x, CORE, [(0, 1), (1, 0)])]
  transfers between devices with their start and end apart: 7 -> 8, of which waited for: 7 -> 7; matrix products, arithmetic and copies ran while one was open for 1% -> 1% of each run, Pallas kernels for 4% -> 9%
where the time goes in v3:
time: 65.4 us; the launch traced here: 65 us
  starting transfers between devices  30.5 us (47%)
  Pallas kernels  15.4 us (24%)
  waiting for transfers between devices  15.2 us (23%)
  local copies, waits for them, and re-layouts  3.23 us (5%)
  between operations  0.75 us (1%)
    pallas_call x8, Pallas kernels, call(): pl.pallas_call(kernel, out_shape=tuple(outs), in_specs=in_specs, out_spec...  15.4 us
    all_to_all x2, starting transfers between devices, exchange(): return lax.all_to_all(x, CHIPS, split_axis=0, concat_axis=0, tiled=True)  11.5 us
    ppermute x3, starting transfers between devices, body(): skip = skip + lax.ppermute(skip, 'dp', [(i, i ^ step) for i in range(8)])  10.7 us
    all_to_all x2, waiting for transfers between devices, exchange(): return lax.all_to_all(x, CHIPS, split_axis=0, concat_axis=0, tiled=True)  9.56 us
    ppermute x3, starting transfers between devices, swap_cores(): return lax.ppermute(x, CORE, [(0, 1), (1, 0)])  8.29 us
    ppermute x3, waiting for transfers between devices, body(): skip = skip + lax.ppermute(skip, 'dp', [(i, i ^ step) for i in range(8)])  3.87 us
    unnamed x16, local copies, waits for them, and re-layouts  2.71 us
    ppermute x3, waiting for transfers between devices, swap_cores(): return lax.ppermute(x, CORE, [(0, 1), (1, 0)])  1.73 us
  transfers between devices with their start and end apart: 8, of which 7 were waited for; matrix products, arithmetic and copies ran while one was open for 1% of the time, Pallas kernels for 9%

profile of v3, /device:TPU:1, one launch (start us, length us, event | category | flops | bytes accessed | tf_op | source)
XLA Modules:
  0.0 65.0 jit_solution(14490024896659842083)
XLA Ops:
  0.6 0.0 copy-start.5
  0.6 0.0 copy-start.7
  0.7 3.1 %shard_map.118 = (bf16[2,128,2048]{2,1,0:T(8,128)(2,1)S(1)}, bf16[2,128,128]{2,1,0:T(8,128)(2,1)S(1)}, f32[2,128,32]{2,1,0:T(8,128)S(1)}, f32[16,128]{1,0:T(8,128)S(1)}, f32[16,136,128]{2,1,0:T(8,128)S(1)}) custom-call(s32[1,8]{1,0:T(1,128)} %len_ref.3, bf16[1,128,2048]{2,1,0:T(8,128)(2,1)} %v_hbm.1, bf16[1,128,2048]{2,1,0:T(8,128)(2,1)} %g_hbm.1, ...), custom_call_target="tpu_custom_call" | custom-call | bytes 4194304 | tf_op jit(solution)/shard_map/pallas_call | solution.py:359
  3.8 3.3 %collective-permute-start = (f32[16,136,128]{2,1,0:T(8,128)S(1)}, f32[16,136,128]{2,1,0:T(8,128)S(1)}, u32[]{:S(2)}, u32[]{:S(2)}) collective-permute-start(f32[16,136,128]{2,1,0:T(8,128)S(1)} %get-tuple-element.29._), channel_id=1, source_target_pairs={{0,1},{1,0},{2,3},{3,2},{4,5},{5,4},{6,7},{7,6},{8,9},{9,8},{10,11... | collective-permute-start | bytes 3342344 | tf_op jit(solution)/shard_map/ppermute | solution.py:379
  7.1 0.0 copy-done.5
  7.1 0.0 copy-done.7
  7.1 1.5 %shard_map.119 = (f32[16,128,128]{2,1,0:T(8,128)S(1)}, f32[8,128]{1,0:T(8,128)S(1)}, f32[16,128]{1,0:T(8,128)S(1)}, f32[8,128]{1,0:T(8,128)S(1)}) custom-call(f32[16,136,128]{2,1,0:T(8,128)S(1)} %get-tuple-element.29._, s32[1,8]{1,0:T(1,128)S(1)} %copy-done.5, f32[32]{0:T(128)S(1)} %copy-done.7, bf16[2,128,2048]{2,1,0:T(8,128)(2,1)S(1)} %get-tuple-element.30.roles_ref, ...), custom_call_target="tpu_custom_call" | custom-call | bytes 4194304 | tf_op jit(solution)/shard_map/pallas_call | solution.py:359
  8.5 0.0 copy-start.3
  8.6 0.9 %collective-permute-done.recv_ref = f32[16,136,128]{2,1,0:T(8,128)S(1)} collective-permute-done((f32[16,136,128]{2,1,0:T(8,128)S(1)}, f32[16,136,128]{2,1,0:T(8,128)S(1)}, u32[]{:S(2)}, u32[]{:S(2)}) %collective-permute-start) | collective-permute-done | bytes 1114144 | tf_op jit(solution)/shard_map/ppermute | solution.py:379
  9.5 1.2 %shard_map.120 = f32[16,136,128]{2,1,0:T(8,128)} custom-call(f32[16,136,128]{2,1,0:T(8,128)S(1)} %collective-permute-done.recv_ref, f32[16,128,128]{2,1,0:T(8,128)S(1)} %get-tuple-element.33.mine_ref, f32[16,128]{1,0:T(8,128)S(1)} %get-tuple-element.34.gain_ref), custom_call_target="tpu_custom_call" | custom-call | bytes 3145728 | tf_op jit(solution)/shard_map/pallas_call | solution.py:359
  10.7 0.0 copy-done.3
  10.7 5.1 %all-to-all-start = ((f32[16,136,128]{2,1,0:T(8,128)}), f32[16,136,128]{2,1,0:T(8,128)S(1)}, u32[]{:S(2)}, u32[]{:S(2)}) async-start(f32[16,136,128]{2,1,0:T(8,128)} %shard_map.120), calls=%async_computation | async-start | bytes 2228224 | tf_op jit(solution)/shard_map/all_to_all | solution.py:383
  15.7 0.7 %collective-permute-start.1 = (f32[8,128]{1,0:T(8,128)S(1)}, f32[8,128]{1,0:T(8,128)S(1)}, u32[]{:S(2)}, u32[]{:S(2)}) collective-permute-start(f32[8,128]{1,0:T(8,128)S(1)} %get-tuple-element.36), channel_id=1, source_target_pairs={{0,1},{1,0},{2,3},{3,2},{4,5},{5,4},{6,7},{7,6},{8,9},{9,8},{10,11... | collective-permute-start | bytes 12296 | tf_op jit(solution)/shard_map/ppermute | solution.py:379
  16.5 0.8 %collective-permute-done.1 = f32[8,128]{1,0:T(8,128)S(1)} collective-permute-done((f32[8,128]{1,0:T(8,128)S(1)}, f32[8,128]{1,0:T(8,128)S(1)}, u32[]{:S(2)}, u32[]{:S(2)}) %collective-permute-start.1) | collective-permute-done | bytes 4128 | tf_op jit(solution)/shard_map/ppermute | solution.py:379
  17.3 1.6 %collective-permute-start.2 = (f32[8,128]{1,0:T(8,128)S(1)}, f32[8,128]{1,0:T(8,128)S(1)}, u32[]{:S(2)}, u32[]{:S(2)}) collective-permute-start(f32[8,128]{1,0:T(8,128)S(1)} %add.12), channel_id=1, source_target_pairs={{0,32},{32,0},{64,96},{96,64},{128,160},{160,128},{192,224},{224,1... | collective-permute-start | bytes 12296 | tf_op jit(solution)/shard_map/ppermute | solution.py:428
  18.9 1.3 %collective-permute-done.2 = f32[8,128]{1,0:T(8,128)S(1)} collective-permute-done((f32[8,128]{1,0:T(8,128)S(1)}, f32[8,128]{1,0:T(8,128)S(1)}, u32[]{:S(2)}, u32[]{:S(2)}) %collective-permute-start.2) | collective-permute-done | bytes 4128 | tf_op jit(solution)/shard_map/ppermute | solution.py:428
  20.2 3.0 %collective-permute-start.3 = (f32[8,128]{1,0:T(8,128)S(1)}, f32[8,128]{1,0:T(8,128)S(1)}, u32[]{:S(2)}, u32[]{:S(2)}) collective-permute-start(f32[8,128]{1,0:T(8,128)S(1)} %add.13), channel_id=1, source_target_pairs={{0,64},{32,96},{64,0},{96,32},{128,192},{160,224},{192,128},{224,1... | collective-permute-start | bytes 12296 | tf_op jit(solution)/shard_map/ppermute | solution.py:428
  23.2 1.3 %collective-permute-done.3 = f32[8,128]{1,0:T(8,128)S(1)} collective-permute-done((f32[8,128]{1,0:T(8,128)S(1)}, f32[8,128]{1,0:T(8,128)S(1)}, u32[]{:S(2)}, u32[]{:S(2)}) %collective-permute-start.3) | collective-permute-done | bytes 4128 | tf_op jit(solution)/shard_map/ppermute | solution.py:428
  24.5 6.1 %collective-permute-start.4 = (f32[8,128]{1,0:T(8,128)S(1)}, f32[8,128]{1,0:T(8,128)S(1)}, u32[]{:S(2)}, u32[]{:S(2)}) collective-permute-start(f32[8,128]{1,0:T(8,128)S(1)} %add.14), channel_id=1, source_target_pairs={{0,128},{32,160},{64,192},{96,224},{128,0},{160,32},{192,64},{224,... | collective-permute-start | bytes 12296 | tf_op jit(solution)/shard_map/ppermute | solution.py:428
  30.6 1.3 %collective-permute-done.4 = f32[8,128]{1,0:T(8,128)S(1)} collective-permute-done((f32[8,128]{1,0:T(8,128)S(1)}, f32[8,128]{1,0:T(8,128)S(1)}, u32[]{:S(2)}, u32[]{:S(2)}) %collective-permute-start.4) | collective-permute-done | bytes 4128 | tf_op jit(solution)/shard_map/ppermute | solution.py:428
  31.9 0.2 all-to-all-done.in_ref
  32.1 1.1 %shard_map.121._ = f32[16,136,128]{2,1,0:T(8,128)} custom-call(f32[16,136,128]{2,1,0:T(8,128)S(1)} %all-to-all-done.in_ref, f32[8,128]{1,0:T(8,128)S(1)} %add.15.skip_ref), custom_call_target="tpu_custom_call" | custom-call | bytes 2097152 | tf_op jit(solution)/shard_map/pallas_call | solution.py:359
  33.3 6.4 %all-to-all-start.1 = ((f32[16,136,128]{2,1,0:T(8,128)}), f32[16,136,128]{2,1,0:T(8,128)S(1)}, u32[]{:S(2)}, u32[]{:S(2)}) async-start(f32[16,136,128]{2,1,0:T(8,128)} %shard_map.121._), calls=%async_computation.1 | async-start | bytes 2228224 | tf_op jit(solution)/shard_map/all_to_all | solution.py:383
  39.7 0.0 copy-start.2
  39.7 0.7 %copy-done.2 = f32[1,32,128]{2,1,0:T(8,128)S(1)} copy-done((f32[1,32,128]{2,1,0:T(8,128)S(1)}, f32[1,32,128]{2,1,0:T(8,128)}, u32[]{:S(2)}) %copy-start.2) | copy-done | bytes 16408
  40.4 0.0 copy-start.6
  40.4 0.7 %copy-done.6 = s32[1,8]{1,0:T(1,128)S(1)} copy-done((s32[1,8]{1,0:T(1,128)S(1)}, s32[1,8]{1,0:T(1,128)}, u32[]{:S(2)}) %copy-start.6) | copy-done | bytes 56
  41.0 2.8 %shard_map.122 = (f32[2,128,2048]{2,1,0:T(8,128)S(1)}, f32[2,128,128]{2,1,0:T(8,128)S(1)}) custom-call(f32[16,136,128]{2,1,0:T(8,128)} %shard_map.121._, s32[1,8]{1,0:T(1,128)S(1)} %copy-done.6, bf16[2,128,2048]{2,1,0:T(8,128)(2,1)S(1)} %get-tuple-element.30.roles_ref, bf16[2,128,128]{2,1,0:T(8,128)(2,1)S(1)} %get-tuple-element.31.rows_ref, ...), custom_call_target="tpu_custom_call" | custom-call | flops 2684354560 | bytes 20971520 | tf_op jit(solution)/shard_map/pallas_call | solution.py:359
  43.8 0.0 copy-start
  43.8 1.3 %copy-done = f32[2,128,2048]{2,1,0:T(8,128)} copy-done((f32[2,128,2048]{2,1,0:T(8,128)}, f32[2,128,2048]{2,1,0:T(8,128)S(1)}, u32[]{:S(2)}) %copy-start) | copy-done | bytes 2097176
  45.1 9.4 %all-to-all-done.1.x_ref = f32[16,136,128]{2,1,0:T(8,128)S(1)} async-done(((f32[16,136,128]{2,1,0:T(8,128)}), f32[16,136,128]{2,1,0:T(8,128)S(1)}, u32[]{:S(2)}, u32[]{:S(2)}) %all-to-all-start.1) | async-done | bytes 1114144 | tf_op jit(solution)/shard_map/all_to_all | solution.py:383
  54.5 0.0 copy-start.1
  54.5 0.1 shard_map.123
  54.6 4.3 %collective-permute-start.5 = (f32[16,128,128]{2,1,0:T(8,128)S(1)}, f32[16,128,128]{2,1,0:T(8,128)S(1)}, u32[]{:S(2)}, u32[]{:S(2)}) collective-permute-start(f32[16,128,128]{2,1,0:T(8,128)S(1)} %get-tuple-element.38._), channel_id=1, source_target_pairs={{0,1},{1,0},{2,3},{3,2},{4,5},{5,4},{6,7},{7,6},{8,9},{9,8},{10,11... | collective-permute-start | bytes 3145736 | tf_op jit(solution)/shard_map/ppermute | solution.py:379
  58.9 0.0 copy-done.1
  58.9 0.0 copy-start.4
  58.9 2.0 %shard_map.124 = (bf16[128,2048]{1,0:T(8,128)(2,1)S(1)}, f32[128,128]{1,0:T(8,128)S(1)}, f32[128,128]{1,0:T(8,128)S(1)}, f32[16,128]{1,0:T(8,128)S(1)}) custom-call(f32[16,128,128]{2,1,0:T(8,128)S(1)} %get-tuple-element.38._, f32[16,136,128]{2,1,0:T(8,128)S(1)} %all-to-all-done.1.x_ref, bf16[2,128,2048]{2,1,0:T(8,128)(2,1)S(1)} %get-tuple-element.30.roles_ref, ...), custom_call_target="tpu_custom_call" | custom-call | bytes 8388608 | tf_op jit(solution)/shard_map/pallas_call | solution.py:359
  60.8 0.5 slice_bitcast_fusion
  61.4 0.0 collective-permute-done.5.y_ref
  61.4 0.0 copy-done.4
  61.4 3.6 %shard_map.125 = (f32[1,128,128]{2,1,0:T(8,128)}, f32[1,128,128]{2,1,0:T(8,128)}, f32[1,32,128]{2,1,0:T(8,128)}, bf16[1,128,2048]{2,1,0:T(8,128)(2,1)}, bf16[1,128,2048]{2,1,0:T(8,128)(2,1)}) custom-call(f32[16,128,128]{2,1,0:T(8,128)S(1)} %collective-permute-done.5.y_ref, f32[16,136,128]{2,1,0:T(8,128)S(1)} %all-to-all-done.1.x_ref, ...), custom_call_target="tpu_custom_call" | custom-call | bytes 8388608 | tf_op jit(solution)/shard_map/pallas_call | solution.py:359
  (4 shorter events, 0.0 us)
Async XLA Ops:
  0.6 6.5 %copy-start.5 = (s32[1,8]{1,0:T(1,128)S(1)}, s32[1,8]{1,0:T(1,128)}, u32[]{:S(2)}) copy-start(s32[1,8]{1,0:T(1,128)} %len_ref.3) | copy-start | bytes 100
  0.6 6.4 %copy-start.7 = (f32[32]{0:T(128)S(1)}, f32[32]{0:T(128)}, u32[]{:S(2)}) copy-start(f32[32]{0:T(128)} %skip_gain_ref.1) | copy-start | bytes 388
  3.8 5.7 %collective-permute-start = (f32[16,136,128]{2,1,0:T(8,128)S(1)}, f32[16,136,128]{2,1,0:T(8,128)S(1)}, u32[]{:S(2)}, u32[]{:S(2)}) collective-permute-start(f32[16,136,128]{2,1,0:T(8,128)S(1)} %get-tuple-element.29._), channel_id=1, source_target_pairs={{0,1},{1,0},{2,3},{3,2},{4,5},{5,4},{6,7},{7,6},{8,9},{9,8},{10,11... | collective-permute-start | bytes 3342344 | tf_op jit(solution)/shard_map/ppermute | solution.py:379
  8.5 2.1 %copy-start.3 = (f32[8,128]{1,0:T(8,128)}, f32[8,128]{1,0:T(8,128)S(1)}, u32[]{:S(2)}) copy-start(f32[8,128]{1,0:T(8,128)S(1)} %get-tuple-element.41.keep_ref) | copy-start | bytes 12292
  10.7 21.4 %all-to-all-start = ((f32[16,136,128]{2,1,0:T(8,128)}), f32[16,136,128]{2,1,0:T(8,128)S(1)}, u32[]{:S(2)}, u32[]{:S(2)}) async-start(f32[16,136,128]{2,1,0:T(8,128)} %shard_map.120), calls=%async_computation | async-start | bytes 2228224 | tf_op jit(solution)/shard_map/all_to_all | solution.py:383
  15.7 1.6 %collective-permute-start.1 = (f32[8,128]{1,0:T(8,128)S(1)}, f32[8,128]{1,0:T(8,128)S(1)}, u32[]{:S(2)}, u32[]{:S(2)}) collective-permute-start(f32[8,128]{1,0:T(8,128)S(1)} %get-tuple-element.36), channel_id=1, source_target_pairs={{0,1},{1,0},{2,3},{3,2},{4,5},{5,4},{6,7},{7,6},{8,9},{9,8},{10,11... | collective-permute-start | bytes 12296 | tf_op jit(solution)/shard_map/ppermute | solution.py:379
  17.3 2.9 %collective-permute-start.2 = (f32[8,128]{1,0:T(8,128)S(1)}, f32[8,128]{1,0:T(8,128)S(1)}, u32[]{:S(2)}, u32[]{:S(2)}) collective-permute-start(f32[8,128]{1,0:T(8,128)S(1)} %add.12), channel_id=1, source_target_pairs={{0,32},{32,0},{64,96},{96,64},{128,160},{160,128},{192,224},{224,1... | collective-permute-start | bytes 12296 | tf_op jit(solution)/shard_map/ppermute | solution.py:428
  20.2 4.3 %collective-permute-start.3 = (f32[8,128]{1,0:T(8,128)S(1)}, f32[8,128]{1,0:T(8,128)S(1)}, u32[]{:S(2)}, u32[]{:S(2)}) collective-permute-start(f32[8,128]{1,0:T(8,128)S(1)} %add.13), channel_id=1, source_target_pairs={{0,64},{32,96},{64,0},{96,32},{128,192},{160,224},{192,128},{224,1... | collective-permute-start | bytes 12296 | tf_op jit(solution)/shard_map/ppermute | solution.py:428
  24.5 7.4 %collective-permute-start.4 = (f32[8,128]{1,0:T(8,128)S(1)}, f32[8,128]{1,0:T(8,128)S(1)}, u32[]{:S(2)}, u32[]{:S(2)}) collective-permute-start(f32[8,128]{1,0:T(8,128)S(1)} %add.14), channel_id=1, source_target_pairs={{0,128},{32,160},{64,192},{96,224},{128,0},{160,32},{192,64},{224,... | collective-permute-start | bytes 12296 | tf_op jit(solution)/shard_map/ppermute | solution.py:428
  33.3 21.2 %all-to-all-start.1 = ((f32[16,136,128]{2,1,0:T(8,128)}), f32[16,136,128]{2,1,0:T(8,128)S(1)}, u32[]{:S(2)}, u32[]{:S(2)}) async-start(f32[16,136,128]{2,1,0:T(8,128)} %shard_map.121._), calls=%async_computation.1 | async-start | bytes 2228224 | tf_op jit(solution)/shard_map/all_to_all | solution.py:383
  39.7 0.7 %copy-start.2 = (f32[1,32,128]{2,1,0:T(8,128)S(1)}, f32[1,32,128]{2,1,0:T(8,128)}, u32[]{:S(2)}) copy-start(f32[1,32,128]{2,1,0:T(8,128)} %ld_ref.1) | copy-start | bytes 49156
  40.4 0.7 %copy-start.6 = (s32[1,8]{1,0:T(1,128)S(1)}, s32[1,8]{1,0:T(1,128)}, u32[]{:S(2)}) copy-start(s32[1,8]{1,0:T(1,128)} %len_ref.3) | copy-start | bytes 100
  43.8 1.3 %copy-start = (f32[2,128,2048]{2,1,0:T(8,128)}, f32[2,128,2048]{2,1,0:T(8,128)S(1)}, u32[]{:S(2)}) copy-start(f32[2,128,2048]{2,1,0:T(8,128)S(1)} %get-tuple-element.39.part_ref) | copy-start | bytes 6291460
  54.5 4.4 %copy-start.1 = (f32[2,128,2048]{2,1,0:T(8,128)S(1)}, f32[2,128,2048]{2,1,0:T(8,128)}, u32[]{:S(2)}) copy-start(f32[2,128,2048]{2,1,0:T(8,128)} %copy-done) | copy-start | bytes 6291460
  54.6 6.7 %collective-permute-start.5 = (f32[16,128,128]{2,1,0:T(8,128)S(1)}, f32[16,128,128]{2,1,0:T(8,128)S(1)}, u32[]{:S(2)}, u32[]{:S(2)}) collective-permute-start(f32[16,128,128]{2,1,0:T(8,128)S(1)} %get-tuple-element.38._), channel_id=1, source_target_pairs={{0,1},{1,0},{2,3},{3,2},{4,5},{5,4},{6,7},{7,6},{8,9},{9,8},{10,11... | collective-permute-start | bytes 3145736 | tf_op jit(solution)/shard_map/ppermute | solution.py:379
  58.9 2.5 %copy-start.4 = (f32[8,128]{1,0:T(8,128)S(1)}, f32[8,128]{1,0:T(8,128)}, u32[]{:S(2)}) copy-start(f32[8,128]{1,0:T(8,128)} %copy-done.3) | copy-start | bytes 12292

commit v4 on v3

v4 whole, which is shorter than its diff:
```python
import functools

import jax
import jax.numpy as jnp
from jax import lax
from jax.experimental import pallas as pl
from jax.experimental.pallas import tpu as pltpu
from jax.sharding import Mesh
from jax.sharding import PartitionSpec as P

SEQ = ("seq_0", "seq_1", "seq_2")
ROW, COL = "seq_0", "seq_1"
CORE = "seq_2"
F32 = jnp.float32
BF16 = jnp.bfloat16
T = 128
N = 128
PAIRS = 16
HEADS = 32
DOCS = 8
EXT = 8
Q = 4
HALF = PAIRS // 2
LOAD = 2 * N
PARTS = 4
PART = 512
FAR = -1e30
VMEM = pl.BlockSpec(memory_space=pltpu.VMEM)
SMEM = pl.BlockSpec(memory_space=pltpu.SMEM)
ANY = pl.BlockSpec(memory_space=pl.ANY)
HBM = pl.BlockSpec(memory_space=pltpu.HBM)

NN = (((1,), (0,)), ((), ()))
NT = (((1,), (1,)), ((), ()))
TN = (((0,), (0,)), ((), ()))


def dot(a, b, dims=NN, precision=None):
    return lax.dot_general(a, b, dims, precision=precision, preferred_element_type=F32)


def exact(a, b, dims=NN):
    return dot(a, b, dims, lax.Precision.HIGHEST)


def iota(shape, dim):
    return lax.broadcasted_iota(jnp.int32, shape, dim)


def block_base():
    return lax.axis_index(SEQ) * T


def doc_starts(len_ref):
    starts, at = [], jnp.int32(0)
    for d in range(DOCS):
        starts.append(at)
        at = at + len_ref[0, d]
    return starts


def segments(starts, base, offset):
    count = jnp.zeros(offset.shape, jnp.int32)
    for s in starts:
        local = jnp.where(s >= base, s - base, jnp.int32(1 << 20))
        count = count + (offset >= local).astype(jnp.int32)
    return count


def end_count(starts, base):
    count = jnp.int32(0)
    for s in starts:
        count = count + jnp.logical_and(s >= base, s < base + T).astype(jnp.int32)
    return count


def lower_triangle():
    return (iota((T, T), 1) <= iota((T, T), 0)).astype(F32)


def weights(ld, starts, base):
    log_cum = exact(lower_triangle(), ld, NT)
    seg = segments(starts, base, iota((T, HEADS), 0))
    last = end_count(starts, base)
    log_end = log_cum[T - 1 :, :]
    w_end = jnp.where(seg == last, jnp.exp(log_end - log_cum), 0.0)
    w_start = jnp.where(seg == 0, jnp.exp(log_cum), 0.0)
    gain = jnp.exp(log_end) * (last == 0).astype(F32)
    return w_end, w_start, gain


def spread(w, j, low):
    return jnp.where(low, w[:, 2 * j : 2 * j + 1], w[:, 2 * j + 1 : 2 * j + 2])


def cols(j):
    return slice(j * 128, (j + 1) * 128)


def heads_of(rows):
    lane = iota(rows.shape, 1)
    spot = lane & (HEADS - 1)
    row = iota(rows.shape, 0)
    even = jnp.sum(jnp.where(lane < 64, rows, 0.0), axis=1, keepdims=True)
    odd = jnp.sum(jnp.where(lane < 64, 0.0, rows), axis=1, keepdims=True)
    placed = jnp.where(spot == 2 * row, even, jnp.where(spot == 2 * row + 1, odd, 0.0))
    return jnp.sum(placed, axis=0, keepdims=True)


def is_first():
    return lax.axis_index(CORE) == 0


def shares(chunk):
    return [(q, i, HALF * chunk + 2 * q + i) for q in range(Q) for i in range(2)]


def rows_of(i):
    return slice(i * N, (i + 1) * N)


def local_sums(roles_ref, slot, j, w, low, p_t):
    own = roles_ref[slot, :, cols(j)].astype(F32)
    return dot(p_t, (own * spread(w, j, low)).astype(BF16))


def extra(gain_ref, chunk, q, skip):
    sub = iota((EXT, 128), 0)
    j = HALF * chunk + 2 * q
    block = jnp.where(sub == 0, gain_ref[j : j + 1], gain_ref[j + 1 : j + 2])
    return jnp.where(sub < 2, block, jnp.where(sub == 2, skip, 0.0))


def prep_kernel(
    len_hbm, v_hbm, g_hbm, b_hbm, c_hbm, ld_hbm,
    roles_ref, rows_ref, w_ref, gain_ref, send_ref,
    len_ref, ld_ref, small_sems, v_sems, g_sems,
):
    first = is_first()
    v_slot = jnp.where(first, 1, 0)
    g_slot = 1 - v_slot
    small = [
        pltpu.make_async_copy(len_hbm, len_ref, small_sems.at[0]),
        pltpu.make_async_copy(ld_hbm.at[0], ld_ref, small_sems.at[1]),
        pltpu.make_async_copy(b_hbm.at[0], rows_ref.at[v_slot], small_sems.at[2]),
        pltpu.make_async_copy(c_hbm.at[0], rows_ref.at[g_slot], small_sems.at[3]),
    ]
    for copy in small:
        copy.start()
    wide = []
    for k in range(PARTS):
        part = slice(k * PART, (k + 1) * PART)
        vc = pltpu.make_async_copy(
            v_hbm.at[0, :, part], roles_ref.at[v_slot, :, part], v_sems.at[k]
        )
        gc = pltpu.make_async_copy(
            g_hbm.at[0, :, part], roles_ref.at[g_slot, :, part], g_sems.at[k]
        )
        vc.start()
        gc.start()
        wide.append((vc, gc))
    for copy in small:
        copy.wait()
    starts = doc_starts(len_ref)
    w_end, w_start, gain = weights(ld_ref[...], starts, block_base())
    w = jnp.where(first, w_start, w_end)
    w_ref[0] = w
    w_ref[1] = jnp.where(first, w_end, w_start)
    p_t = rows_ref[0].T
    low = iota((T, 128), 1) < 64
    skips = []
    for j in range(PAIRS):
        if j % (PAIRS // PARTS) == 0:
            for copy in wide[j // (PAIRS // PARTS)]:
                copy.wait()
        gain_ref[j : j + 1] = spread(gain, j, low[:1])
        both = roles_ref[0, :, cols(j)].astype(F32) * roles_ref[1, :, cols(j)].astype(F32)
        skips.append(jnp.sum(both, axis=0, keepdims=True))
        if j < HALF:
            send_ref[j // 2, rows_of(j % 2)] = local_sums(roles_ref, 0, j, w, low, p_t)
    skip = heads_of(jnp.concatenate(skips, axis=0))
    for q in range(Q):
        send_ref[q, LOAD:] = extra(gain_ref, 0, q, skip)


def own_kernel(
    _, len_ref, skip_gain_ref, roles_ref, rows_ref, w_ref, mine_ref, keep_ref, gains_ref
):
    low = iota((T, 128), 1) < 64
    p_t = rows_ref[1].T
    w = w_ref[1]
    for q, i, j in shares(0):
        mine_ref[q, rows_of(i)] = local_sums(roles_ref, 1, j, w, low, p_t)
    for j in range(PAIRS):
        gains_ref[j : j + 1] = jnp.where(
            low[:1], skip_gain_ref[2 * j], skip_gain_ref[2 * j + 1]
        )
    base = block_base()
    starts = doc_starts(len_ref)
    offset = iota((EXT, T), 1)
    keep = jnp.ones((EXT, T), F32)
    for s in starts:
        keep = jnp.where(offset + base == s, 0.0, keep)
    keep_ref[...] = keep


def second_kernel(_, roles_ref, rows_ref, w_ref, gain_ref, send_ref, mine_ref):
    low = iota((T, 128), 1) < 64
    other_t = rows_ref[0].T
    mine_t = rows_ref[1].T
    w_other = w_ref[0]
    w_mine = w_ref[1]
    for q, i, j in shares(1):
        send_ref[q, rows_of(i)] = local_sums(roles_ref, 0, j, w_other, low, other_t)
        mine_ref[q, rows_of(i)] = local_sums(roles_ref, 1, j, w_mine, low, mine_t)
    for q in range(Q):
        send_ref[q, LOAD:] = extra(gain_ref, 1, q, 0.0)


def combine_kernel(recv_ref, mine_ref, send_ref, out_ref, buffer, sems):
    sub = iota((EXT, 128), 0)
    copies = []
    for q in range(Q):
        theirs = recv_ref[q, LOAD:]
        ours = send_ref[q, LOAD:]
        for i in range(2):
            r = rows_of(i)
            buffer[q, r] = theirs[i : i + 1] * mine_ref[q, r] + recv_ref[q, r]
        buffer[q, LOAD:] = jnp.where(sub == 2, theirs + ours, theirs * ours)
        copies.append(pltpu.make_async_copy(buffer.at[q], out_ref.at[q], sems.at[q]))
        copies[-1].start()
    for copy in copies:
        copy.wait()


def row_kernel(in_ref, prefix_ref, factor_ref, total_ref):
    first = is_first()
    sub = iota((EXT, 128), 0)
    place = iota((EXT, 128), 1) // HEADS == lax.axis_index(ROW)
    running = [jnp.zeros((N, 128), F32), jnp.zeros((N, 128), F32)]
    factor = jnp.ones((EXT, 128), F32)
    skip = jnp.zeros((EXT, 128), F32)
    for step in range(Q):
        at = jnp.where(first, step, Q - 1 - step)
        factor_ref[at] = factor
        ext = in_ref[at, LOAD:]
        for i in range(2):
            r = rows_of(i)
            prefix_ref[at, r] = running[i]
            running[i] = ext[i : i + 1] * running[i] + in_ref[at, r]
        factor = factor * ext
        skip = skip + in_ref[step, LOAD:]
    for i in range(2):
        total_ref[rows_of(i)] = running[i]
    total_ref[LOAD:] = jnp.where(sub == 2, jnp.where(place, skip, 0.0), factor)


def incoming(near_ref, next_ref, i):
    first = is_first()
    x = jnp.where(first, lax.axis_index(ROW), Q - 1 - lax.axis_index(ROW))
    r = rows_of(i)
    beyond = near_ref[LOAD + i : LOAD + i + 1] * next_ref[r]
    return jnp.where(x > 0, near_ref[r], 0.0) + jnp.where(x > 1, beyond, 0.0)


def enter(near_ref, next_ref, prefix_ref, factor_ref, buffer):
    for i in range(2):
        r = rows_of(i)
        start = incoming(near_ref, next_ref, i)
        for q in range(Q):
            buffer[q, r] = prefix_ref[q, r] + factor_ref[q, i : i + 1] * start


def send_out(buffer, out_ref, sems):
    copies = [pltpu.make_async_copy(buffer.at[q], out_ref.at[q], sems.at[q]) for q in range(Q)]
    for copy in copies:
        copy.start()
    for copy in copies:
        copy.wait()


def enter_first_kernel(
    near_ref, next_ref, prefix_ref, factor_ref, total_ref, skip_ref, out_ref, buffer, sems
):
    enter(near_ref, next_ref, prefix_ref, factor_ref, buffer)
    skip = jnp.where(is_first(), total_ref[LOAD:], next_ref[LOAD:]) + near_ref[LOAD:]
    skip_ref[...] = jnp.broadcast_to(skip[2:3], (EXT, 128))
    send_out(buffer, out_ref, sems)


def enter_second_kernel(
    near_ref, next_ref, prefix_ref, factor_ref, low_ref, high_ref, out_ref, buffer, sems
):
    enter(near_ref, next_ref, prefix_ref, factor_ref, buffer)
    plane = lax.axis_index("dp") + lax.axis_index(COL)
    sub = iota((EXT, 128), 0)
    ext = jnp.where(
        sub == (plane & 7),
        low_ref[...],
        jnp.where(sub == ((plane + 4) & 7), high_ref[...], 0.0),
    )
    for q in range(Q):
        buffer[q, LOAD:] = ext
    send_out(buffer, out_ref, sems)


def inside_kernel(_, len_ref, roles_ref, rows_ref, ld_ref, low_ref, high_ref, raw_ref):
    first = is_first()
    v_slot = jnp.where(first, 1, 0)
    g_slot = 1 - v_slot
    base = block_base()
    starts = doc_starts(len_ref)
    ld = ld_ref[0]
    tri = lower_triangle()
    cum_t = exact(tri, ld, NT)
    cum_h = exact(ld, tri, NT)
    t_at = iota((T, T), 0)
    s_at = iota((T, T), 1)
    same = segments(starts, base, t_at) == segments(starts, base, s_at)
    bias = jnp.where(jnp.logical_and(s_at <= t_at, same), 0.0, FAR)
    b = rows_ref[v_slot]
    c = rows_ref[g_slot]
    scores = dot(c, b, NT)
    low = iota((T, 128), 1) < 64
    zero = jnp.zeros((T, 128), BF16)
    grad_scores = jnp.zeros((T, T), F32)
    for j in range(PAIRS):
        v = roles_ref[v_slot, :, cols(j)]
        g = roles_ref[g_slot, :, cols(j)]
        v_two = jnp.concatenate([jnp.where(low, v, zero), jnp.where(low, zero, v)], axis=0)
        g_two = jnp.concatenate([jnp.where(low, g, zero), jnp.where(low, zero, g)], axis=0)
        grad_mix = dot(g, v_two, NT)
        mixes = []
        for k in range(2):
            h = 2 * j + k
            decay = jnp.exp(cum_t[:, h : h + 1] - cum_h[h : h + 1, :] + bias)
            mixes.append((scores * decay).astype(BF16))
            grad_scores = grad_scores + grad_mix[:, k * T : (k + 1) * T] * decay
        part_ref = low_ref if j < HALF else high_ref
        part_ref[g_slot, :, cols(j % HALF)] = dot(jnp.concatenate(mixes, axis=1), v_two)
        part_ref[v_slot, :, cols(j % HALF)] = dot(jnp.concatenate(mixes, axis=0), g_two, TN)
    half = grad_scores.astype(BF16)
    raw_ref[g_slot] = dot(half, b)
    raw_ref[v_slot] = dot(half, c, TN)


def pass_on_kernel(chunk, _, x_ref, mine_ref, gain_ref, out_ref):
    for q, i, j in shares(chunk):
        r = rows_of(i)
        out_ref[q, r] = gain_ref[j : j + 1] * x_ref[q, r] + mine_ref[q, r]
    if chunk == 1:
        skip = x_ref[0, LOAD:] + x_ref[1, LOAD:] + x_ref[2, LOAD:] + x_ref[3, LOAD:]
        for q in range(Q):
            out_ref[q, LOAD:] = skip


def finish_role(slot, chunk, j, low, x, roles_ref, rows, w, part_ref, skip_gains):
    half = x.astype(BF16)
    own = roles_ref[slot, :, cols(j)].astype(F32)
    skipped = roles_ref[1 - slot, :, cols(j)].astype(F32)
    wide = spread(w, j, low)
    tail = wide * dot(rows, half)
    out = part_ref[slot, :, cols(j - HALF * chunk)] + tail
    result = (out + skip_gains[j : j + 1] * skipped).astype(BF16)
    change = own * out
    hi = change.astype(BF16)
    lo = (change - hi.astype(F32)).astype(BF16)
    lane = iota((128, 128), 0)
    head = iota((128, 128), 1)
    pick = (head == 2 * j + jnp.where(lane < 64, 0, 1)).astype(BF16)
    end = jnp.sum(own * tail, axis=0, keepdims=True)
    return result, dot(hi, pick) + dot(lo, pick), end, dot((own * wide).astype(BF16), half, NT)


def finish_first_kernel(
    y_ref, x_ref, roles_ref, rows_ref, w_ref, part_ref, raw_ref, gains_ref, gain_ref,
    mixed_ref, vgrad_ref, total_ref, change_ref, end_ref,
):
    first = is_first()
    low = iota((T, 128), 1) < 64
    skip_gains = gains_ref[...]
    totals = [raw_ref[0], raw_ref[1]]
    changes = jnp.zeros((T, 128), F32)
    for q, i, j in shares(0):
        x = x_ref[q, rows_of(i)]
        y = y_ref[q, rows_of(i)]
        near, near_change, near_end, more = finish_role(
            0, 0, j, low, x, roles_ref, rows_ref[0], w_ref[0], part_ref, skip_gains
        )
        totals[0] = totals[0] + more
        far, far_change, far_end, more = finish_role(
            1, 0, j, low, y, roles_ref, rows_ref[1], w_ref[1], part_ref, skip_gains
        )
        totals[1] = totals[1] + more
        mixed_ref[:, cols(j)] = jnp.where(first, near, far)
        vgrad_ref[:, cols(j)] = jnp.where(first, far, near)
        changes = changes + near_change - far_change
        meet = jnp.sum(x * y, axis=0, keepdims=True)
        end_ref[j : j + 1] = jnp.where(first, far_end, near_end) + gain_ref[j : j + 1] * meet
    total_ref[0] = totals[0]
    total_ref[1] = totals[1]
    change_ref[...] = changes


def near_kernel(
    _, x_ref, roles_ref, rows_ref, w_ref, part_ref, gains_ref, total_in_ref, change_in_ref,
    out_ref, total_ref, change_ref, end_ref,
):
    low = iota((T, 128), 1) < 64
    skip_gains = gains_ref[...]
    total = total_in_ref[0]
    changes = change_in_ref[...]
    for q, i, j in shares(1):
        result, change, end, more = finish_role(
            0, 1, j, low, x_ref[q, rows_of(i)], roles_ref, rows_ref[0], w_ref[0], part_ref,
            skip_gains,
        )
        out_ref[:, cols(j - HALF)] = result
        changes = changes + change
        total = total + more
        end_ref[j - HALF : j - HALF + 1] = end
    total_ref[...] = total
    change_ref[...] = changes


def far_kernel(
    scales, y_ref, x_ref, passed_ref, roles_ref, rows_ref, w_ref, part_ref, gains_ref, gain_ref,
    keep_ref, mixed_in_ref, vgrad_in_ref, total_in_ref, end_in_ref,
    near_ref, near_total_ref, near_change_ref, near_end_ref,
    igrad_ref, ograd_ref, dgrad_ref, skip_ref, mixed_hbm, vgrad_hbm,
    mixed_ref, vgrad_ref, sems,
):
    in_scale, out_scale, decay_scale, skip_scale = scales
    first = is_first()
    low = iota((T, 128), 1) < 64
    skip_gains = gains_ref[...]
    copies = []

    def leave(src, dst, lo, hi, sem):
        copies.append(pltpu.make_async_copy(src, dst.at[0, :, lo:hi], sem))
        copies[-1].start()

    middle = HALF * 128
    leave(mixed_in_ref, mixed_hbm, 0, middle, sems.at[0, 0])
    leave(vgrad_in_ref, vgrad_hbm, 0, middle, sems.at[1, 0])
    total = total_in_ref[1]
    changes = near_change_ref[...]
    ends = [end_in_ref[...]]
    for q, i, j in shares(1):
        y = y_ref[q, rows_of(i)]
        result, change, end, more = finish_role(
            1, 1, j, low, y, roles_ref, rows_ref[1], w_ref[1], part_ref, skip_gains
        )
        k = j - HALF
        near = near_ref[:, cols(k)]
        mixed_ref[:, cols(k)] = jnp.where(first, near, result)
        vgrad_ref[:, cols(k)] = jnp.where(first, result, near)
        if k % 4 == 3:
            part = slice((k - 3) * 128, (k + 1) * 128)
            lo, hi = middle + part.start, middle + part.stop
            leave(mixed_ref.at[:, part], mixed_hbm, lo, hi, sems.at[0, 1 + k // 4])
            leave(vgrad_ref.at[:, part], vgrad_hbm, lo, hi, sems.at[1, 1 + k // 4])
        changes = changes - change
        total = total + more
        meet = jnp.sum(x_ref[q, rows_of(i)] * y, axis=0, keepdims=True)
        end = jnp.where(first, end, near_end_ref[k : k + 1])
        ends.append(end + gain_ref[j : j + 1] * meet)
    near_total = near_total_ref[...]
    igrad_ref[0] = jnp.where(first, total, near_total) * in_scale
    ograd_ref[0] = jnp.where(first, near_total, total) * out_scale
    changes = jnp.where(first, changes, -changes)
    at_end = iota((T, 128), 0) == T - 1
    changes = changes + jnp.where(at_end, heads_of(jnp.concatenate(ends, axis=0)), 0.0)
    summed = exact(changes, lower_triangle(), TN)[:HEADS]
    dgrad_ref[0] = summed * keep_ref[:1] * decay_scale
    skips = jnp.sum(passed_ref[0, LOAD:] + y_ref[0, LOAD:], axis=0, keepdims=True)
    skip = skips[:, :HEADS]
    for x in range(1, Q):
        skip = skip + skips[:, x * HEADS : (x + 1) * HEADS]
    skip_ref[...] = skip * skip_scale
    for copy in copies:
        copy.wait()


def call(kernel, outs, *args, after=(), spaces=(), out_spaces=(), scratch=(), flops=0, moved=0):
    in_specs = [ANY] * len(after) + list(spaces)
    in_specs += [VMEM] * (len(args) + len(after) - len(in_specs))
    out_specs = [VMEM] * (len(outs) - len(out_spaces)) + list(out_spaces)
    return pl.pallas_call(
        kernel,
        out_shape=tuple(outs),
        in_specs=in_specs,
        out_specs=tuple(out_specs),
        scratch_shapes=list(scratch),
        compiler_params=pltpu.CompilerParams(vmem_limit_bytes=16 << 20),
        cost_estimate=pl.CostEstimate(flops=flops, bytes_accessed=moved, transcendentals=0),
    )(*after, *args)


def f32(*shape):
    return jax.ShapeDtypeStruct(shape, F32)


def bf16(*shape):
    return jax.ShapeDtypeStruct(shape, BF16)


def dma(*shape):
    return pltpu.SemaphoreType.DMA(shape)


def swap_cores(x):
    return lax.ppermute(x, CORE, [(0, 1), (1, 0)])


def along_row(x):
    return lax.all_to_all(x, COL, split_axis=0, concat_axis=0, tiled=True)


def to_row(x, step):
    pairs = []
    for r in range(Q):
        pairs.append((2 * r, 2 * ((r + step) % Q)))
        pairs.append((2 * r + 1, 2 * ((r - step) % Q) + 1))
    return lax.ppermute(x, (ROW, CORE), pairs)


def from_plane(x, offset):
    pairs = []
    for d in range(8):
        for y in range(Q):
            pairs.append((((d + y + offset) % 8) * Q + y, d * Q + y))
    return lax.ppermute(x, ("dp", COL), pairs)


def body(values_in, input_proj, output_proj, log_decay, doc_lengths, skip_gain, out_cotangent):
    inputs = (doc_lengths, values_in, out_cotangent, input_proj, output_proj, log_decay)
    token_count = lax.axis_size(SEQ) * T
    seq_count = lax.axis_size("dp")
    inner = values_in.shape[2]
    head_dim = inner // HEADS
    loaded = f32(Q, LOAD + EXT, 128)
    plain = f32(Q, LOAD, 128)

    def leaving(shape):
        return dict(
            out_spaces=[HBM], scratch=[pltpu.VMEM(shape.shape, F32), dma(Q)], moved=2 << 20
        )

    roles, rows, w, gain, send_a = call(
        prep_kernel,
        (bf16(2, T, inner), bf16(2, T, N), f32(2, T, HEADS), f32(PAIRS, 128), loaded),
        *(pltpu.with_memory_space_constraint(a, pltpu.HBM) for a in inputs),
        spaces=[HBM] * 6,
        scratch=[
            pltpu.SMEM((1, DOCS), jnp.int32), pltpu.VMEM((HEADS, T), F32),
            dma(4), dma(PARTS), dma(PARTS),
        ],
        moved=4 << 20,
    )
    recv_a = swap_cores(send_a)
    mine_a, keep, gains = call(
        own_kernel,
        (plain, f32(EXT, T), f32(PAIRS, 128)),
        doc_lengths, skip_gain, roles, rows, w,
        after=(send_a,),
        spaces=[SMEM] * 2,
        moved=4 << 20,
    )
    (chip_a,) = call(combine_kernel, (loaded,), recv_a, mine_a, send_a, **leaving(loaded))
    in_a = along_row(chip_a)
    send_b, mine_b = call(
        second_kernel, (loaded, plain), roles, rows, w, gain, after=(chip_a,), moved=4 << 20
    )
    recv_b = swap_cores(send_b)
    (chip_b,) = call(combine_kernel, (loaded,), recv_b, mine_b, send_b, **leaving(loaded))
    scanned = (plain, f32(Q, EXT, 128), f32(LOAD + EXT, 128))
    prefix_a, factor_a, total_a = call(row_kernel, scanned, in_a, moved=1 << 20)
    in_b = along_row(chip_b)
    skip, out_a = call(
        enter_first_kernel,
        (f32(EXT, 128), plain),
        to_row(total_a, 1), to_row(total_a, 2), prefix_a, factor_a, total_a,
        **leaving(plain),
    )
    prefix_b, factor_b, total_b = call(row_kernel, scanned, in_b, moved=1 << 20)
    x_a = along_row(out_a)
    (out_b,) = call(
        enter_second_kernel,
        (loaded,),
        to_row(total_b, 1), to_row(total_b, 2), prefix_b, factor_b,
        from_plane(skip, 0), from_plane(skip, 4),
        **leaving(loaded),
    )
    (passed_a,) = call(
        functools.partial(pass_on_kernel, 0), (plain,), x_a, mine_a, gain, after=(out_b,),
        moved=1 << 20,
    )
    x_b = along_row(out_b)
    y_a = swap_cores(passed_a)
    part_a, part_b, raw = call(
        inside_kernel,
        (f32(2, T, inner // 2), f32(2, T, inner // 2), f32(2, T, N)),
        doc_lengths, roles, rows, log_decay,
        after=(out_b,),
        spaces=[SMEM],
        flops=40 * 2 * T * N * inner,
        moved=20 << 20,
    )
    mixed_a, vgrad_a, total, change, end = call(
        finish_first_kernel,
        (bf16(T, inner // 2), bf16(T, inner // 2), f32(2, T, N), f32(T, 128), f32(HALF, 128)),
        y_a, x_a, roles, rows, w, part_a, raw, gains, gain,
        moved=8 << 20,
    )
    (passed_b,) = call(
        functools.partial(pass_on_kernel, 1), (loaded,), x_b, mine_b, gain, after=(change,),
        moved=1 << 20,
    )
    y_b = swap_cores(passed_b)
    near = call(
        near_kernel,
        (bf16(T, inner // 2), f32(T, N), f32(T, 128), f32(HALF, 128)),
        x_b, roles, rows, w, part_b, gains, total, change,
        after=(passed_b,),
        moved=4 << 20,
    )
    scales = (
        1.0 / inner**0.5,
        (N / (inner * token_count)) ** 0.5,
        1.0 / (head_dim * token_count) ** 0.5,
        1.0 / (seq_count * token_count * head_dim) ** 0.5,
    )
    input_grad, output_grad, decay_grad, skip_grad, mixed, values_grad = call(
        functools.partial(far_kernel, scales),
        (
            f32(1, T, N), f32(1, T, N), f32(1, HEADS, T), f32(1, HEADS),
            bf16(1, T, inner), bf16(1, T, inner),
        ),
        y_b, x_b, passed_b, roles, rows, w, part_b, gains, gain, keep,
        mixed_a, vgrad_a, total, end, *near,
        out_spaces=[HBM] * 2,
        scratch=[
            pltpu.VMEM((T, inner // 2), BF16), pltpu.VMEM((T, inner // 2), BF16), dma(2, 3)
        ],
        moved=8 << 20,
    )
    return mixed, values_grad, input_grad, output_grad, decay_grad, skip_grad[0]


def solution(mesh):
    finer = Mesh(mesh.devices.reshape(mesh.shape["dp"], 4, 4, 2), ("dp",) + SEQ)
    placed = (
        P("dp", SEQ, None),
        P("dp", SEQ, None),
        P("dp", SEQ, None),
        P("dp", None, SEQ),
        P("dp", None),
        P(),
        P("dp", SEQ, None),
    )
    return jax.shard_map(
        body,
        mesh=finer,
        in_specs=placed,
        out_specs=(
            P("dp", SEQ, None),
            P("dp", SEQ, None),
            P("dp", SEQ, None),
            P("dp", SEQ, None),
            P("dp", None, SEQ),
            P(),
        ),
        check_vma=False,
    )
```

time: 65.4 us -> 81 us (1.24)
  starting transfers between devices: 30.5 us -> 38.6 us
  Pallas kernels: 15.4 us -> 21.2 us
  local copies, waits for them, and re-layouts: 3.23 us -> 5.58 us
  waiting for transfers between devices: 15.2 us -> 13.5 us
    all_to_all x2 -> x4, starting transfers between devices: 11.5 us -> 17.8 us  [along_row(): return lax.all_to_all(x, COL, split_axis=0, concat_axis=0, tiled=True)]
    pallas_call x8 -> x15, Pallas kernels: 15.4 us -> 21.2 us  [call(): pl.pallas_call(kernel, out_shape=tuple(outs), in_specs=in_specs, out_spec...]
    ppermute x3 -> x6, starting transfers between devices: 10.7 us -> 13.6 us  [the longest x2 7.56 us: from_plane(): return lax.ppermute(x, ('dp', COL), pairs)]
    unnamed x16 -> x40, local copies, waits for them, and re-layouts: 2.71 us -> 5.58 us
    all_to_all x2 -> x4, waiting for transfers between devices: 9.56 us -> 8.22 us  [along_row(): return lax.all_to_all(x, COL, split_axis=0, concat_axis=0, tiled=True)]
    ppermute x3 -> x4, waiting for transfers between devices: 1.73 us -> 0.46 us  [swap_cores(): return lax.ppermute(x, CORE, [(0, 1), (1, 0)])]
    ppermute x3 -> x4, starting transfers between devices: 8.29 us -> 7.14 us  [swap_cores(): return lax.ppermute(x, CORE, [(0, 1), (1, 0)])]
    ppermute x3 -> x6, waiting for transfers between devices: 3.87 us -> 4.84 us  [the longest x4 4.5 us: to_row(): return lax.ppermute(x, (ROW, CORE), pairs)]
  transfers between devices with their start and end apart: 8 -> 14, of which waited for: 7 -> 7; matrix products, arithmetic and copies ran while one was open for 1% -> 0% of each run, Pallas kernels for 9% -> 16%
where the time goes in v4:
time: 81 us; the launch traced here: 79.9 us
  starting transfers between devices  38.6 us (48%)
  Pallas kernels  21.2 us (26%)
  waiting for transfers between devices  13.5 us (17%)
  local copies, waits for them, and re-layouts  5.58 us (7%)
  between operations  1.04 us (1%)
    pallas_call x15, Pallas kernels, call(): pl.pallas_call(kernel, out_shape=tuple(outs), in_specs=in_specs, out_spec...  21.2 us
    all_to_all x4, starting transfers between devices, along_row(): return lax.all_to_all(x, COL, split_axis=0, concat_axis=0, tiled=True)  17.8 us
    all_to_all x4, waiting for transfers between devices, along_row(): return lax.all_to_all(x, COL, split_axis=0, concat_axis=0, tiled=True)  8.22 us
    ppermute x2, starting transfers between devices, from_plane(): return lax.ppermute(x, ('dp', COL), pairs)  7.56 us
    ppermute x4, starting transfers between devices, swap_cores(): return lax.ppermute(x, CORE, [(0, 1), (1, 0)])  7.14 us
    ppermute x4, starting transfers between devices, to_row(): return lax.ppermute(x, (ROW, CORE), pairs)  6.05 us
    unnamed x40, local copies, waits for them, and re-layouts  5.58 us
    ppermute x4, waiting for transfers between devices, to_row(): return lax.ppermute(x, (ROW, CORE), pairs)  4.5 us
  transfers between devices with their start and end apart: 14, of which 7 were waited for; matrix products, arithmetic and copies ran while one was open for 0% of the time, Pallas kernels for 16%

profile of v4, /device:TPU:1, one launch (start us, length us, event | category | flops | bytes accessed | tf_op | source)
XLA Modules:
  0.0 79.9 jit_solution(18150470046875182710)
XLA Ops:
  0.6 2.6 %shard_map.118 = (bf16[2,128,2048]{2,1,0:T(8,128)(2,1)S(1)}, bf16[2,128,128]{2,1,0:T(8,128)(2,1)S(1)}, f32[2,128,32]{2,1,0:T(8,128)S(1)}, f32[16,128]{1,0:T(8,128)S(1)}, f32[4,264,128]{2,1,0:T(8,128)S(1)}) custom-call(s32[1,8]{1,0:T(1,128)} %len_ref.3, bf16[1,128,2048]{2,1,0:T(8,128)(2,1)} %v_hbm.1, bf16[1,128,2048]{2,1,0:T(8,128)(2,1)} %g_hbm.1, ...), custom_call_target="tpu_custom_call" | custom-call | bytes 4194304 | tf_op jit(solution)/shard_map/pallas_call | solution.py:489
  3.2 0.0 copy-start.7
  3.2 3.3 %collective-permute-start = (f32[4,264,128]{2,1,0:T(8,128)S(1)}, f32[4,264,128]{2,1,0:T(8,128)S(1)}, u32[]{:S(2)}, u32[]{:S(2)}) collective-permute-start(f32[4,264,128]{2,1,0:T(8,128)S(1)} %get-tuple-element.42._.send_ref), channel_id=1, source_target_pairs={{0,1},{1,0},{2,3},{3,2},{4,5},{5,4},{6,7},{7,6},{8,9},{9,8},{10,11... | collective-permute-start | bytes 1622024 | tf_op jit(solution)/shard_map/ppermute | solution.py:513
  6.5 0.7 copy-done.18
  7.2 0.0 copy-done.19
  7.2 1.1 %shard_map.119 = (f32[4,256,128]{2,1,0:T(8,128)S(1)}, f32[8,128]{1,0:T(8,128)S(1)}, f32[16,128]{1,0:T(8,128)S(1)}) custom-call(f32[4,264,128]{2,1,0:T(8,128)S(1)} %get-tuple-element.42._.send_ref, s32[1,8]{1,0:T(1,128)S(1)} %copy-done.18, f32[32]{0:T(128)S(1)} %copy-done.19, bf16[2,128,2048]{2,1,0:T(8,128)(2,1)S(1)} %get-tuple-element.43.roles_ref, ...), custom_call_target="tpu_custom_call" | custom-call | bytes 4194304 | tf_op jit(solution)/shard_map/pallas_call | solution.py:489
  8.3 0.9 %shard_map.120._ = f32[4,264,128]{2,1,0:T(8,128)} custom-call(f32[4,264,128]{2,1,0:T(8,128)S(1)} %collective-permute-done.recv_ref, f32[4,256,128]{2,1,0:T(8,128)S(1)} %get-tuple-element.46.mine_ref, f32[4,264,128]{2,1,0:T(8,128)S(1)} %get-tuple-element.42._.send_ref), custom_call_target="tpu_custom_call" | custom-call | bytes 2097152 | tf_op jit(solution)/shard_map/pallas_call | solution.py:489
  9.2 1.7 %shard_map.121 = (f32[4,264,128]{2,1,0:T(8,128)}, f32[4,256,128]{2,1,0:T(8,128)S(1)}) custom-call(f32[4,264,128]{2,1,0:T(8,128)} %shard_map.120._, bf16[2,128,2048]{2,1,0:T(8,128)(2,1)S(1)} %get-tuple-element.43.roles_ref, bf16[2,128,128]{2,1,0:T(8,128)(2,1)S(1)} %get-tuple-element.44.rows_ref, f32[2,128,32]{2,1,0:T(8,128)S(1)} %get-tuple-element.45.w_ref, ...), custom_call_target="tpu_custom_call" | custom-call | bytes 4194304 | tf_op jit(solution)/shard_map/pallas_call | solution.py:489
  10.9 0.1 collective-permute-start.1
  11.0 3.5 %all-to-all-start.1 = ((f32[4,264,128]{2,1,0:T(8,128)}), f32[4,264,128]{2,1,0:T(8,128)S(1)}, u32[]{:S(2)}, u32[]{:S(2)}) async-start(f32[4,264,128]{2,1,0:T(8,128)} %shard_map.120._), calls=%async_computation.1 | async-start | bytes 1081344 | tf_op jit(solution)/shard_map/all_to_all | solution.py:517
  14.5 2.1 %shard_map.122 = f32[4,264,128]{2,1,0:T(8,128)} custom-call(f32[4,264,128]{2,1,0:T(8,128)} %collective-permute-done.1.recv_ref, f32[4,256,128]{2,1,0:T(8,128)S(1)} %get-tuple-element.49.mine_ref, f32[4,264,128]{2,1,0:T(8,128)} %get-tuple-element.48.send_ref), custom_call_target="tpu_custom_call" | custom-call | bytes 2097152 | tf_op jit(solution)/shard_map/pallas_call | solution.py:489
  16.6 7.2 %all-to-all-done.1.in_ref = f32[4,264,128]{2,1,0:T(8,128)S(1)} async-done(((f32[4,264,128]{2,1,0:T(8,128)}), f32[4,264,128]{2,1,0:T(8,128)S(1)}, u32[]{:S(2)}, u32[]{:S(2)}) %all-to-all-start.1) | async-done | bytes 540704 | tf_op jit(solution)/shard_map/all_to_all | solution.py:517
  23.8 3.5 %all-to-all-start = ((f32[4,264,128]{2,1,0:T(8,128)}), f32[4,264,128]{2,1,0:T(8,128)S(1)}, u32[]{:S(2)}, u32[]{:S(2)}) async-start(f32[4,264,128]{2,1,0:T(8,128)} %shard_map.122), calls=%async_computation | async-start | bytes 1081344 | tf_op jit(solution)/shard_map/all_to_all | solution.py:517
  27.3 0.1 shard_map.124
  27.4 1.6 %collective-permute-start.5 = (f32[264,128]{1,0:T(8,128)S(1)}, f32[264,128]{1,0:T(8,128)S(1)}, u32[]{:S(2)}, u32[]{:S(2)}) collective-permute-start(f32[264,128]{1,0:T(8,128)S(1)} %get-tuple-element.53.total_ref), channel_id=1, source_target_pairs={{0,16},{1,17},{8,24},{9,25},{16,0},{17,1},{24,8},{25,9},{2,18},{3,... | collective-permute-start | bytes 405512 | tf_op jit(solution)/shard_map/ppermute | solution.py:525
  29.0 0.9 %collective-permute-start.4 = (f32[264,128]{1,0:T(8,128)S(1)}, f32[264,128]{1,0:T(8,128)S(1)}, u32[]{:S(2)}, u32[]{:S(2)}) collective-permute-start(f32[264,128]{1,0:T(8,128)S(1)} %get-tuple-element.53.total_ref), channel_id=1, source_target_pairs={{0,8},{1,25},{8,16},{9,1},{16,24},{17,9},{24,0},{25,17},{2,10},{3,... | collective-permute-start | bytes 405512 | tf_op jit(solution)/shard_map/ppermute | solution.py:525
  29.8 3.0 %collective-permute-done.5.next_ref = f32[264,128]{1,0:T(8,128)S(1)} collective-permute-done((f32[264,128]{1,0:T(8,128)S(1)}, f32[264,128]{1,0:T(8,128)S(1)}, u32[]{:S(2)}, u32[]{:S(2)}) %collective-permute-start.5) | collective-permute-done | bytes 135200 | tf_op jit(solution)/shard_map/ppermute | solution.py:525
  32.8 1.5 %collective-permute-done.4.near_ref = f32[264,128]{1,0:T(8,128)S(1)} collective-permute-done((f32[264,128]{1,0:T(8,128)S(1)}, f32[264,128]{1,0:T(8,128)S(1)}, u32[]{:S(2)}, u32[]{:S(2)}) %collective-permute-start.4) | collective-permute-done | bytes 135200 | tf_op jit(solution)/shard_map/ppermute | solution.py:525
  34.3 0.8 shard_map.125
  35.1 0.4 all-to-all-done.in_ref
  35.5 0.4 copy-done.2
  35.9 3.9 %all-to-all-start.2 = ((f32[4,256,128]{2,1,0:T(8,128)}), f32[4,256,128]{2,1,0:T(8,128)S(1)}, u32[]{:S(2)}, u32[]{:S(2)}) async-start(f32[4,256,128]{2,1,0:T(8,128)} %copy-done.2), calls=%async_computation.2 | async-start | bytes 1048576 | tf_op jit(solution)/shard_map/all_to_all | solution.py:517
  39.8 0.1 shard_map.123
  39.9 1.8 %collective-permute-start.3 = (f32[264,128]{1,0:T(8,128)S(1)}, f32[264,128]{1,0:T(8,128)S(1)}, u32[]{:S(2)}, u32[]{:S(2)}) collective-permute-start(f32[264,128]{1,0:T(8,128)S(1)} %get-tuple-element.50), channel_id=1, source_target_pairs={{0,16},{1,17},{8,24},{9,25},{16,0},{17,1},{24,8},{25,9},{2,18},{3,... | collective-permute-start | bytes 405512 | tf_op jit(solution)/shard_map/ppermute | solution.py:525
  41.7 1.8 %collective-permute-start.2 = (f32[264,128]{1,0:T(8,128)S(1)}, f32[264,128]{1,0:T(8,128)S(1)}, u32[]{:S(2)}, u32[]{:S(2)}) collective-permute-start(f32[264,128]{1,0:T(8,128)S(1)} %get-tuple-element.50), channel_id=1, source_target_pairs={{0,8},{1,25},{8,16},{9,1},{16,24},{17,9},{24,0},{25,17},{2,10},{3,... | collective-permute-start | bytes 405512 | tf_op jit(solution)/shard_map/ppermute | solution.py:525
  43.5 6.9 %collective-permute-start.7 = (f32[8,128]{1,0:T(8,128)S(1)}, f32[8,128]{1,0:T(8,128)S(1)}, u32[]{:S(2)}, u32[]{:S(2)}) collective-permute-start(f32[8,128]{1,0:T(8,128)S(1)} %get-tuple-element.56), channel_id=1, source_target_pairs={{128,0},{162,2},{196,4},{230,6},{160,32},{194,34},{228,36},{6,38},... | collective-permute-start | bytes 12296 | tf_op jit(solution)/shard_map/ppermute | solution.py:533
  50.4 0.6 collective-permute-start.6
  51.0 0.3 collective-permute-done.7.high_ref
  51.4 0.9 %shard_map.126._ = f32[4,264,128]{2,1,0:T(8,128)} custom-call(f32[264,128]{1,0:T(8,128)S(1)} %collective-permute-done.2.near_ref, f32[264,128]{1,0:T(8,128)S(1)} %collective-permute-done.3.next_ref, f32[4,256,128]{2,1,0:T(8,128)S(1)} %get-tuple-element.51.prefix_ref, f32[4,8,128]{2,1,0:T(8,128)S(1)} %get-tuple-element.52.factor_ref, ...), custom_call_target="tpu_custom_call" | custom-call | bytes 2097152 | tf_op jit(solution)/shard_map/pallas_call | solution.py:489
  52.3 0.8 %shard_map.127 = f32[4,256,128]{2,1,0:T(8,128)} custom-call(f32[4,264,128]{2,1,0:T(8,128)} %shard_map.126._, f32[4,256,128]{2,1,0:T(8,128)S(1)} %all-to-all-done.2.x_ref, f32[4,256,128]{2,1,0:T(8,128)S(1)} %get-tuple-element.46.mine_ref, f32[16,128]{1,0:T(8,128)S(1)} %get-tuple-element.47.gain_ref), custom_call_target="tpu_custom_call" | custom-call | bytes 1048576 | tf_op jit(solution)/shard_map/pallas_call | solution.py:489
  53.2 2.4 %collective-permute-start.8 = (f32[4,256,128]{2,1,0:T(8,128)}, f32[4,256,128]{2,1,0:T(8,128)}, u32[]{:S(2)}, u32[]{:S(2)}) collective-permute-start(f32[4,256,128]{2,1,0:T(8,128)} %shard_map.127), channel_id=1, source_target_pairs={{0,1},{1,0},{2,3},{3,2},{4,5},{5,4},{6,7},{7,6},{8,9},{9,8},{10,11... | collective-permute-start | bytes 1572872 | tf_op jit(solution)/shard_map/ppermute | solution.py:513
  55.6 7.0 %all-to-all-start.3 = ((f32[4,264,128]{2,1,0:T(8,128)}), f32[4,264,128]{2,1,0:T(8,128)S(1)}, u32[]{:S(2)}, u32[]{:S(2)}) async-start(f32[4,264,128]{2,1,0:T(8,128)} %shard_map.126._), calls=%async_computation.3 | async-start | bytes 1081344 | tf_op jit(solution)/shard_map/all_to_all | solution.py:517
  62.5 2.8 %shard_map.128 = (f32[2,128,1024]{2,1,0:T(8,128)S(1)}, f32[2,128,1024]{2,1,0:T(8,128)S(1)}, f32[2,128,128]{2,1,0:T(8,128)S(1)}) custom-call(f32[4,264,128]{2,1,0:T(8,128)} %shard_map.126._, s32[1,8]{1,0:T(1,128)S(1)} %copy-done.18, bf16[2,128,2048]{2,1,0:T(8,128)(2,1)S(1)} %get-tuple-element.43.roles_ref, ...), custom_call_target="tpu_custom_call" | custom-call | flops 2684354560 | bytes 20971520 | tf_op jit(solution)/shard_map/pallas_call | solution.py:489
  65.3 3.9 %shard_map.129 = (bf16[128,1024]{1,0:T(8,128)(2,1)S(1)}, bf16[128,1024]{1,0:T(8,128)(2,1)S(1)}, f32[2,128,128]{2,1,0:T(8,128)S(1)}, f32[128,128]{1,0:T(8,128)S(1)}, f32[8,128]{1,0:T(8,128)S(1)}) custom-call(f32[4,256,128]{2,1,0:T(8,128)} %collective-permute-done.8.y_ref, f32[4,256,128]{2,1,0:T(8,128)S(1)} %all-to-all-done.2.x_ref, ...), custom_call_target="tpu_custom_call" | custom-call | bytes 8388608 | tf_op jit(solution)/shard_map/pallas_call | solution.py:489
  69.2 0.0 copy-start.3
  69.2 0.7 copy-done.3
  69.9 0.7 copy-done.5
  70.6 0.6 copy-done.16
  71.2 0.6 all-to-all-done.3.x_ref
  71.9 1.0 %copy-done.1 = f32[4,256,128]{2,1,0:T(8,128)S(1)} copy-done((f32[4,256,128]{2,1,0:T(8,128)S(1)}, f32[4,256,128]{2,1,0:T(8,128)}, u32[]{:S(2)}) %copy-start.1) | copy-done | bytes 524312
  72.9 0.7 copy-done.9
  73.6 0.1 shard_map.130._.passed_ref
  73.7 1.4 %collective-permute-start.9 = (f32[4,264,128]{2,1,0:T(8,128)S(1)}, f32[4,264,128]{2,1,0:T(8,128)S(1)}, u32[]{:S(2)}, u32[]{:S(2)}) collective-permute-start(f32[4,264,128]{2,1,0:T(8,128)S(1)} %shard_map.130._.passed_ref), channel_id=1, source_target_pairs={{0,1},{1,0},{2,3},{3,2},{4,5},{5,4},{6,7},{7,6},{8,9},{9,8},{10,11... | collective-permute-start | bytes 1622024 | tf_op jit(solution)/shard_map/ppermute | solution.py:513
  75.1 1.1 %shard_map.131 = (bf16[128,1024]{1,0:T(8,128)(2,1)S(1)}, f32[128,128]{1,0:T(8,128)S(1)}, f32[128,128]{1,0:T(8,128)S(1)}, f32[8,128]{1,0:T(8,128)S(1)}) custom-call(f32[4,264,128]{2,1,0:T(8,128)S(1)} %shard_map.130._.passed_ref, f32[4,264,128]{2,1,0:T(8,128)S(1)} %all-to-all-done.3.x_ref, bf16[2,128,2048]{2,1,0:T(8,128)(2,1)S(1)} %get-tuple-element.43.roles_ref, ...), custom_call_target="tpu_custom_call" | custom-call | bytes 4194304 | tf_op jit(solution)/shard_map/pallas_call | solution.py:489
  76.2 0.5 collective-permute-done.9.y_ref
  76.6 0.7 copy-done.17
  77.3 0.0 copy-done.15
  77.3 2.4 %shard_map.132 = (f32[1,128,128]{2,1,0:T(8,128)}, f32[1,128,128]{2,1,0:T(8,128)}, f32[1,32,128]{2,1,0:T(8,128)}, f32[1,32]{1,0:T(1,128)}, bf16[1,128,2048]{2,1,0:T(8,128)(2,1)}, /*index=5*/bf16[1,128,2048]{2,1,0:T(8,128)(2,1)}) custom-call(f32[4,264,128]{2,1,0:T(8,128)S(1)} %collective-permute-done.9.y_ref, f32[4,264,128]{2,1,0:T(8,128)S(1)} %all-to-all-done.3.x_ref, ...), custom_call_target="tpu_custom_call" | custom-call | bytes 8388608 | tf_op jit(solution)/shard_map/pallas_call | solution.py:489
  (35 shorter events, 0.1 us)
Async XLA Ops:
  3.2 49.1 %copy-start.7 = (f32[16,128]{1,0:T(8,128)}, f32[16,128]{1,0:T(8,128)S(1)}, u32[]{:S(2)}) copy-start(f32[16,128]{1,0:T(8,128)S(1)} %get-tuple-element.47.gain_ref) | copy-start | bytes 24580
  3.2 5.1 %collective-permute-start = (f32[4,264,128]{2,1,0:T(8,128)S(1)}, f32[4,264,128]{2,1,0:T(8,128)S(1)}, u32[]{:S(2)}, u32[]{:S(2)}) collective-permute-start(f32[4,264,128]{2,1,0:T(8,128)S(1)} %get-tuple-element.42._.send_ref), channel_id=1, source_target_pairs={{0,1},{1,0},{2,3},{3,2},{4,5},{5,4},{6,7},{7,6},{8,9},{9,8},{10,11... | collective-permute-start | bytes 1622024 | tf_op jit(solution)/shard_map/ppermute | solution.py:513
  6.5 0.7 copy-start.18
  6.5 0.7 copy-start.19
  8.3 0.9 %copy-start.10 = (f32[16,128]{1,0:T(8,128)}, f32[16,128]{1,0:T(8,128)S(1)}, u32[]{:S(2)}) copy-start(f32[16,128]{1,0:T(8,128)S(1)} %get-tuple-element.60.gains_ref) | copy-start | bytes 24580
  8.3 0.9 %copy-start.14 = (f32[8,128]{1,0:T(8,128)}, f32[8,128]{1,0:T(8,128)S(1)}, u32[]{:S(2)}) copy-start(f32[8,128]{1,0:T(8,128)S(1)} %get-tuple-element.63.keep_ref) | copy-start | bytes 12292
  10.9 3.6 %copy-start = (f32[4,256,128]{2,1,0:T(8,128)}, f32[4,256,128]{2,1,0:T(8,128)S(1)}, u32[]{:S(2)}) copy-start(f32[4,256,128]{2,1,0:T(8,128)S(1)} %get-tuple-element.49.mine_ref) | copy-start | bytes 1572868
  10.9 3.6 %collective-permute-start.1 = (f32[4,264,128]{2,1,0:T(8,128)}, f32[4,264,128]{2,1,0:T(8,128)}, u32[]{:S(2)}, u32[]{:S(2)}) collective-permute-start(f32[4,264,128]{2,1,0:T(8,128)} %get-tuple-element.48.send_ref), channel_id=1, source_target_pairs={{0,1},{1,0},{2,3},{3,2},{4,5},{5,4},{6,7},{7,6},{8,9},{9,8},{10,11... | collective-permute-start | bytes 1622024 | tf_op jit(solution)/shard_map/ppermute | solution.py:513
  11.0 12.8 %all-to-all-start.1 = ((f32[4,264,128]{2,1,0:T(8,128)}), f32[4,264,128]{2,1,0:T(8,128)S(1)}, u32[]{:S(2)}, u32[]{:S(2)}) async-start(f32[4,264,128]{2,1,0:T(8,128)} %shard_map.120._), calls=%async_computation.1 | async-start | bytes 1081344 | tf_op jit(solution)/shard_map/all_to_all | solution.py:517
  23.8 11.6 %all-to-all-start = ((f32[4,264,128]{2,1,0:T(8,128)}), f32[4,264,128]{2,1,0:T(8,128)S(1)}, u32[]{:S(2)}, u32[]{:S(2)}) async-start(f32[4,264,128]{2,1,0:T(8,128)} %shard_map.122), calls=%async_computation | async-start | bytes 1081344 | tf_op jit(solution)/shard_map/all_to_all | solution.py:517
  27.4 5.5 %collective-permute-start.5 = (f32[264,128]{1,0:T(8,128)S(1)}, f32[264,128]{1,0:T(8,128)S(1)}, u32[]{:S(2)}, u32[]{:S(2)}) collective-permute-start(f32[264,128]{1,0:T(8,128)S(1)} %get-tuple-element.53.total_ref), channel_id=1, source_target_pairs={{0,16},{1,17},{8,24},{9,25},{16,0},{17,1},{24,8},{25,9},{2,18},{3,... | collective-permute-start | bytes 405512 | tf_op jit(solution)/shard_map/ppermute | solution.py:525
  29.0 5.4 %collective-permute-start.4 = (f32[264,128]{1,0:T(8,128)S(1)}, f32[264,128]{1,0:T(8,128)S(1)}, u32[]{:S(2)}, u32[]{:S(2)}) collective-permute-start(f32[264,128]{1,0:T(8,128)S(1)} %get-tuple-element.53.total_ref), channel_id=1, source_target_pairs={{0,8},{1,25},{8,16},{9,1},{16,24},{17,9},{24,0},{25,17},{2,10},{3,... | collective-permute-start | bytes 405512 | tf_op jit(solution)/shard_map/ppermute | solution.py:525
  35.1 0.8 copy-start.2
  35.9 16.4 %all-to-all-start.2 = ((f32[4,256,128]{2,1,0:T(8,128)}), f32[4,256,128]{2,1,0:T(8,128)S(1)}, u32[]{:S(2)}, u32[]{:S(2)}) async-start(f32[4,256,128]{2,1,0:T(8,128)} %copy-done.2), calls=%async_computation.2 | async-start | bytes 1048576 | tf_op jit(solution)/shard_map/all_to_all | solution.py:517
  39.9 11.5 %collective-permute-start.3 = (f32[264,128]{1,0:T(8,128)S(1)}, f32[264,128]{1,0:T(8,128)S(1)}, u32[]{:S(2)}, u32[]{:S(2)}) collective-permute-start(f32[264,128]{1,0:T(8,128)S(1)} %get-tuple-element.50), channel_id=1, source_target_pairs={{0,16},{1,17},{8,24},{9,25},{16,0},{17,1},{24,8},{25,9},{2,18},{3,... | collective-permute-start | bytes 405512 | tf_op jit(solution)/shard_map/ppermute | solution.py:525
  41.7 9.7 %collective-permute-start.2 = (f32[264,128]{1,0:T(8,128)S(1)}, f32[264,128]{1,0:T(8,128)S(1)}, u32[]{:S(2)}, u32[]{:S(2)}) collective-permute-start(f32[264,128]{1,0:T(8,128)S(1)} %get-tuple-element.50), channel_id=1, source_target_pairs={{0,8},{1,25},{8,16},{9,1},{16,24},{17,9},{24,0},{25,17},{2,10},{3,... | collective-permute-start | bytes 405512 | tf_op jit(solution)/shard_map/ppermute | solution.py:525
  43.5 7.9 %collective-permute-start.7 = (f32[8,128]{1,0:T(8,128)S(1)}, f32[8,128]{1,0:T(8,128)S(1)}, u32[]{:S(2)}, u32[]{:S(2)}) collective-permute-start(f32[8,128]{1,0:T(8,128)S(1)} %get-tuple-element.56), channel_id=1, source_target_pairs={{128,0},{162,2},{196,4},{230,6},{160,32},{194,34},{228,36},{6,38},... | collective-permute-start | bytes 12296 | tf_op jit(solution)/shard_map/ppermute | solution.py:533
  50.4 1.0 %collective-permute-start.6 = (f32[8,128]{1,0:T(8,128)S(1)}, f32[8,128]{1,0:T(8,128)S(1)}, u32[]{:S(2)}, u32[]{:S(2)}) collective-permute-start(f32[8,128]{1,0:T(8,128)S(1)} %get-tuple-element.56), channel_id=1, source_target_pairs={{0,0},{34,2},{68,4},{102,6},{32,32},{66,34},{100,36},{134,38},{64,... | collective-permute-start | bytes 12296 | tf_op jit(solution)/shard_map/ppermute | solution.py:533
  53.2 9.4 %copy-start.13 = (f32[1,32,128]{2,1,0:T(8,128)S(1)}, f32[1,32,128]{2,1,0:T(8,128)}, u32[]{:S(2)}) copy-start(f32[1,32,128]{2,1,0:T(8,128)} %ld_ref.1) | copy-start | bytes 49156
  53.2 12.1 %collective-permute-start.8 = (f32[4,256,128]{2,1,0:T(8,128)}, f32[4,256,128]{2,1,0:T(8,128)}, u32[]{:S(2)}, u32[]{:S(2)}) collective-permute-start(f32[4,256,128]{2,1,0:T(8,128)} %shard_map.127), channel_id=1, source_target_pairs={{0,1},{1,0},{2,3},{3,2},{4,5},{5,4},{6,7},{7,6},{8,9},{9,8},{10,11... | collective-permute-start | bytes 1572872 | tf_op jit(solution)/shard_map/ppermute | solution.py:513
  55.6 16.3 %all-to-all-start.3 = ((f32[4,264,128]{2,1,0:T(8,128)}), f32[4,264,128]{2,1,0:T(8,128)S(1)}, u32[]{:S(2)}, u32[]{:S(2)}) async-start(f32[4,264,128]{2,1,0:T(8,128)} %shard_map.126._), calls=%async_computation.3 | async-start | bytes 1081344 | tf_op jit(solution)/shard_map/all_to_all | solution.py:517
  62.5 2.8 %copy-start.8 = (f32[16,128]{1,0:T(8,128)S(1)}, f32[16,128]{1,0:T(8,128)}, u32[]{:S(2)}) copy-start(f32[16,128]{1,0:T(8,128)} %copy-done.7) | copy-start | bytes 24580
  62.5 2.8 %copy-start.11 = (f32[16,128]{1,0:T(8,128)S(1)}, f32[16,128]{1,0:T(8,128)}, u32[]{:S(2)}) copy-start(f32[16,128]{1,0:T(8,128)} %copy-done.10) | copy-start | bytes 24580
  69.2 0.7 copy-start.3
  69.9 0.7 copy-start.5
  70.6 0.6 copy-start.16
  71.9 1.0 %copy-start.1 = (f32[4,256,128]{2,1,0:T(8,128)S(1)}, f32[4,256,128]{2,1,0:T(8,128)}, u32[]{:S(2)}) copy-start(f32[4,256,128]{2,1,0:T(8,128)} %copy-done) | copy-start | bytes 1572868
  72.9 0.7 copy-start.9
  73.6 1.5 %copy-start.12 = (f32[16,128]{1,0:T(8,128)S(1)}, f32[16,128]{1,0:T(8,128)}, u32[]{:S(2)}) copy-start(f32[16,128]{1,0:T(8,128)} %copy-done.10) | copy-start | bytes 24580
  73.7 2.9 %collective-permute-start.9 = (f32[4,264,128]{2,1,0:T(8,128)S(1)}, f32[4,264,128]{2,1,0:T(8,128)S(1)}, u32[]{:S(2)}, u32[]{:S(2)}) collective-permute-start(f32[4,264,128]{2,1,0:T(8,128)S(1)} %shard_map.130._.passed_ref), channel_id=1, source_target_pairs={{0,1},{1,0},{2,3},{3,2},{4,5},{5,4},{6,7},{7,6},{8,9},{9,8},{10,11... | collective-permute-start | bytes 1622024 | tf_op jit(solution)/shard_map/ppermute | solution.py:513
  75.1 1.6 %copy-start.4 = (bf16[128,1024]{1,0:T(8,128)(2,1)S(1)}, bf16[128,1024]{1,0:T(8,128)(2,1)}, u32[]{:S(2)}) copy-start(bf16[128,1024]{1,0:T(8,128)(2,1)} %copy-done.3) | copy-start | bytes 786436
  75.1 1.6 %copy-start.6 = (bf16[128,1024]{1,0:T(8,128)(2,1)S(1)}, bf16[128,1024]{1,0:T(8,128)(2,1)}, u32[]{:S(2)}) copy-start(bf16[128,1024]{1,0:T(8,128)(2,1)} %copy-done.5) | copy-start | bytes 786436
  76.6 0.7 copy-start.17
  76.6 0.7 copy-start.15
